TPU v7x, 256 devices: a whole 4x4x8 slice. The times are simulated.
256 devices in a mesh: tm: 8 (over z), chan: 32 (over x, y, core).
Axes of the slice: x: 4, y: 4, z: 8, core: 2. Of those that a mesh axis runs over, the one named last changes fastest.
Arguments:
- signal: float32 [256, 16384], P('chan', 'tm'), may hold values from -6 to 6
- band: float32 [2, 16, 256], replicated, may hold values from -4 to 4
- response: float32 [2, 8, 16, 2048], P(None, 'tm', None, 'chan'), may hold values from -6 to 6
- offsets: int32 [8, 2048], P('tm', 'chan'), may hold values from 0 to 255, as said below
Outputs:
- smoothed: float32 [256, 16384], P('chan', 'tm')
Inputs may be any that keep to these rules, and one draw needn't show every extreme that they name: Row c of bin k's gain holds the columns c + offsets + j, wrapping around the 256 channels; every offset lies within 8 of 0 modulo 256, and entry [p, q] is the same for all p and for all q in one run of 64 consecutive q.
All inputs are finite; a program needn't handle non-finite values.
Results may differ from a plain program's by a relative error of at most 0.0003.
Values sent between devices are 32-bit elements; how exact they have to be, the bound alone decides.
No kernel may reach another device: no remote copies, remote signals or barrier semaphores. Data moves between devices by JAX's collectives and lax.ppermute only.
A program may use at most 64 MiB of HBM per device.

v0:
```python
import math

import jax
import jax.numpy as jnp
from jax import lax
from jax.sharding import PartitionSpec as P

PRECISE = lax.Precision.HIGHEST


def from_partner(block, axis, stride):
    count = lax.axis_size(axis)
    route = []
    for low in range(count):
        high = low | 1 << stride
        if high != low and high < count:
            route += [(low, high), (high, low)]
    return lax.ppermute(block, axis, route)


def twiddle(numer, length):
    angle = -2.0 * math.pi / length * numer.astype(jnp.float32)
    return (jnp.cos(angle), jnp.sin(angle))


def dft_table(length):
    steps = lax.iota(jnp.int32, length)
    return twiddle(steps[:, None] * steps[None, :] % length, length)


def reverse_bits(value, bit_count):
    result = value * 0
    for bit_index in range(bit_count):
        result = result + value // (1 << bit_index) % 2 * (1 << bit_count - 1 - bit_index)
    return result


def complex_einsum(form, left_real, left_imag, right_real, right_imag):
    out_real = jnp.einsum(form, left_real, right_real, precision=PRECISE) - jnp.einsum(
        form, left_imag, right_imag, precision=PRECISE
    )
    out_imag = jnp.einsum(form, left_real, right_imag, precision=PRECISE) + jnp.einsum(
        form, left_imag, right_real, precision=PRECISE
    )
    return (out_real, out_imag)


def forward_local(real_part, imag_part, phase_bin, total_len, inner_len):
    channel_count, length = real_part.shape
    outer_len = length // inner_len
    sample_pos = lax.iota(jnp.int32, length)
    cosine, sine_part = twiddle(sample_pos * phase_bin % total_len, total_len)
    real_part, imag_part = (
        real_part * cosine - imag_part * sine_part,
        real_part * sine_part + imag_part * cosine,
    )
    real_part = real_part.reshape(channel_count, inner_len, outer_len)
    imag_part = imag_part.reshape(channel_count, inner_len, outer_len)
    table_real, table_imag = dft_table(inner_len)
    real_part, imag_part = complex_einsum(
        "cab,ak->cbk", real_part, imag_part, table_real, table_imag
    )
    outer_ids = lax.iota(jnp.int32, outer_len)[:, None]
    inner_ids = lax.iota(jnp.int32, inner_len)[None, :]
    cosine, sine_part = twiddle(outer_ids * inner_ids, length)
    real_part, imag_part = (
        real_part * cosine - imag_part * sine_part,
        real_part * sine_part + imag_part * cosine,
    )
    table_real, table_imag = dft_table(outer_len)
    return complex_einsum("cbk,bm->mck", real_part, imag_part, table_real, table_imag)


def inverse_local(spec_real, spec_imag, phase_bin, total_len):
    outer_len, channel_count, inner_len = spec_real.shape
    length = outer_len * inner_len
    table_real, table_imag = dft_table(outer_len)
    real_part, imag_part = complex_einsum(
        "mck,mb->cbk", spec_real, spec_imag, table_real, -table_imag
    )
    outer_ids = lax.iota(jnp.int32, outer_len)[:, None]
    inner_ids = lax.iota(jnp.int32, inner_len)[None, :]
    cosine, sine_part = twiddle(outer_ids * inner_ids, length)
    sine_part = -sine_part
    real_part, imag_part = (
        real_part * cosine - imag_part * sine_part,
        real_part * sine_part + imag_part * cosine,
    )
    table_real, table_imag = dft_table(inner_len)
    real_part, imag_part = complex_einsum(
        "cbk,ka->cab", real_part, imag_part, table_real, -table_imag
    )
    real_part = real_part.reshape(channel_count, length)
    imag_part = imag_part.reshape(channel_count, length)
    sample_pos = lax.iota(jnp.int32, length)
    cosine, sine_part = twiddle(sample_pos * phase_bin % total_len, total_len)
    sine_part = -sine_part
    return (real_part * cosine - imag_part * sine_part, real_part * sine_part + imag_part * cosine)


def mix_bins(spread, band, response, offsets):
    fine_len, channel_all, inner_len = (spread.shape[1], spread.shape[2], spread.shape[3])
    band_width = band.shape[1]
    half_width = band_width // 2
    shift_cols = offsets.reshape(1, fine_len, 1, inner_len)
    centered = (shift_cols + half_width) % channel_all - half_width
    moved = jnp.zeros_like(spread)
    for shift_amount in range(-half_width, half_width + 1):
        rolled = jnp.roll(spread, -shift_amount, axis=2)
        moved = jnp.where(centered == shift_amount, rolled, moved)
    moved_real = moved[0]
    moved_imag = moved[1]
    wide_real = jnp.concatenate([moved_real, moved_real[:, : band_width - 1]], axis=1)
    wide_imag = jnp.concatenate([moved_imag, moved_imag[:, : band_width - 1]], axis=1)
    responses = response.reshape(2, band_width, fine_len, 1, inner_len)
    acc_real = jnp.zeros_like(moved_real)
    acc_imag = jnp.zeros_like(moved_imag)
    for lag_index in range(band_width):
        value_real = wide_real[:, lag_index : lag_index + channel_all]
        value_imag = wide_imag[:, lag_index : lag_index + channel_all]
        gain_real = band[0, lag_index][None, :, None]
        gain_imag = band[1, lag_index][None, :, None]
        coef_real = gain_real * responses[0, lag_index] - gain_imag * responses[1, lag_index]
        coef_imag = gain_real * responses[1, lag_index] + gain_imag * responses[0, lag_index]
        acc_real = acc_real + coef_real * value_real - coef_imag * value_imag
        acc_imag = acc_imag + coef_real * value_imag + coef_imag * value_real
    return (acc_real, acc_imag)


def per_device(signal, band, response, offsets):
    blocks = lax.axis_size("tm")
    levels = blocks.bit_length() - 1
    device_pos = lax.axis_index("tm")
    phase_bin = reverse_bits(device_pos, levels)
    channel_count, length = signal.shape
    total_len = length * blocks
    inner_len = math.gcd(128, length // lax.axis_size("chan"))
    real_part = signal
    imag_part = jnp.zeros_like(signal)
    for bit_index in range(levels - 1, -1, -1):
        half_span = 1 << bit_index
        partner = from_partner(jnp.stack([real_part, imag_part]), "tm", bit_index)
        upper_half = device_pos // half_span % 2 == 1
        cosine, sine_part = twiddle(device_pos % half_span, 2 * half_span)
        diff_real = partner[0] - real_part
        diff_imag = partner[1] - imag_part
        new_real = jnp.where(
            upper_half, diff_real * cosine - diff_imag * sine_part, real_part + partner[0]
        )
        new_imag = jnp.where(
            upper_half, diff_real * sine_part + diff_imag * cosine, imag_part + partner[1]
        )
        real_part, imag_part = (new_real, new_imag)
    spec_real, spec_imag = forward_local(real_part, imag_part, phase_bin, total_len, inner_len)
    spread = lax.all_to_all(
        jnp.stack([spec_real, spec_imag]), "chan", split_axis=1, concat_axis=2, tiled=True
    )
    mixed_real, mixed_imag = mix_bins(spread, band, response, offsets)
    returned = lax.all_to_all(
        jnp.stack([mixed_real, mixed_imag]), "chan", split_axis=2, concat_axis=1, tiled=True
    )
    real_part, imag_part = inverse_local(returned[0], returned[1], phase_bin, total_len)
    for bit_index in range(levels):
        half_span = 1 << bit_index
        partner = from_partner(jnp.stack([real_part, imag_part]), "tm", bit_index)
        upper_half = device_pos // half_span % 2 == 1
        cosine, sine_part = twiddle(device_pos % half_span, 2 * half_span)
        sine_part = -sine_part
        base_real = jnp.where(upper_half, partner[0], real_part)
        base_imag = jnp.where(upper_half, partner[1], imag_part)
        scaled_real = jnp.where(upper_half, real_part, partner[0])
        scaled_imag = jnp.where(upper_half, imag_part, partner[1])
        prod_real = scaled_real * cosine - scaled_imag * sine_part
        prod_imag = scaled_real * sine_part + scaled_imag * cosine
        real_part = jnp.where(upper_half, base_real - prod_real, base_real + prod_real)
        imag_part = jnp.where(upper_half, base_imag - prod_imag, base_imag + prod_imag)
    smoothed = real_part / total_len
    return smoothed


def solution(mesh):
    in_specs = (P("chan", "tm"), P(), P(None, "tm", None, "chan"), P("tm", "chan"))
    out_specs = P("chan", "tm")
    return jax.shard_map(
        per_device, mesh=mesh, in_specs=in_specs, out_specs=out_specs, check_vma=False
    )
```

profile of v0, /device:TPU:2, one launch (start us, length us, event | category | flops | bytes accessed | tf_op | source)
XLA Modules:
  0.0 98.8 jit_solution(2592375580562808138)
XLA Ops:
  0.0 0.8 stack.58
  0.9 7.3 %collective-permute-start = (f32[2,8,2048]{2,1,0:T(8,128)S(1)}, f32[2,8,2048]{2,1,0:T(8,128)S(1)}, u32[]{:S(2)}, u32[]{:S(2)}) collective-permute-start(f32[2,8,2048]{2,1,0:T(8,128)S(1)} %stack.58), channel_id=1, source_target_pairs={{0,128},{128,0},{32,160},{160,32},{64,192},{192,64},{96,224},{224,... | collective-permute-start | bytes 393224 | tf_op jit(solution)/shard_map/ppermute | solution.py:18
  9.0 0.7 copy-done.2
  9.7 2.0 %collective-permute-done = f32[2,8,2048]{2,1,0:T(8,128)S(1)} collective-permute-done((f32[2,8,2048]{2,1,0:T(8,128)S(1)}, f32[2,8,2048]{2,1,0:T(8,128)S(1)}, u32[]{:S(2)}, u32[]{:S(2)}) %collective-permute-start) | collective-permute-done | bytes 131104 | tf_op jit(solution)/shard_map/ppermute | solution.py:18
  11.8 4.7 %collective-permute-start.1 = (f32[2,8,2048]{2,1,0:T(8,128)S(1)}, f32[2,8,2048]{2,1,0:T(8,128)S(1)}, u32[]{:S(2)}, u32[]{:S(2)}) collective-permute-start(f32[2,8,2048]{2,1,0:T(8,128)S(1)} %pad_maximum_fusion.1), channel_id=1, source_target_pairs={{0,64},{64,0},{32,96},{96,32},{128,192},{192,128},{160,224},{224,1... | collective-permute-start | bytes 393224 | tf_op jit(solution)/shard_map/ppermute | solution.py:18
  16.5 3.1 %collective-permute-done.1 = f32[2,8,2048]{2,1,0:T(8,128)S(1)} collective-permute-done((f32[2,8,2048]{2,1,0:T(8,128)S(1)}, f32[2,8,2048]{2,1,0:T(8,128)S(1)}, u32[]{:S(2)}, u32[]{:S(2)}) %collective-permute-start.1) | collective-permute-done | bytes 131104 | tf_op jit(solution)/shard_map/ppermute | solution.py:18
  19.6 2.0 %collective-permute-start.2 = (f32[2,8,2048]{2,1,0:T(8,128)S(1)}, f32[2,8,2048]{2,1,0:T(8,128)S(1)}, u32[]{:S(2)}, u32[]{:S(2)}) collective-permute-start(f32[2,8,2048]{2,1,0:T(8,128)S(1)} %pad_maximum_fusion.2), channel_id=1, source_target_pairs={{0,32},{32,0},{64,96},{96,64},{128,160},{160,128},{192,224},{224,1... | collective-permute-start | bytes 393224 | tf_op jit(solution)/shard_map/ppermute | solution.py:18
  21.8 2.9 %collective-permute-done.2 = f32[2,8,2048]{2,1,0:T(8,128)S(1)} collective-permute-done((f32[2,8,2048]{2,1,0:T(8,128)S(1)}, f32[2,8,2048]{2,1,0:T(8,128)S(1)}, u32[]{:S(2)}, u32[]{:S(2)}) %collective-permute-start.2) | collective-permute-done | bytes 131104 | tf_op jit(solution)/shard_map/ppermute | solution.py:18
  24.9 0.6 fusion.64
  25.5 0.6 fusion.58
  26.2 0.6 convolution_subtract_fusion.3
  26.8 0.6 convolution_add_fusion.3
  29.0 0.8 reshape.5110
  29.8 7.6 %all-to-all-start = ((f32[32,1,1024]{2,1,0:T(1,128)}), f32[32,1,1024]{2,1,0:T(1,128)S(1)}, u32[]{:S(2)}, u32[]{:S(2)}) async-start(f32[32,1,1024]{2,1,0:T(1,128)} %reshape.5110), calls=%async_computation | async-start | bytes 262144 | tf_op jit(solution)/shard_map/all_to_all | solution.py:155
  37.5 6.6 %all-to-all-done = f32[32,1,1024]{2,1,0:T(1,128)S(1)} async-done(((f32[32,1,1024]{2,1,0:T(1,128)}), f32[32,1,1024]{2,1,0:T(1,128)S(1)}, u32[]{:S(2)}, u32[]{:S(2)}) %all-to-all-start) | async-done | bytes 131104 | tf_op jit(solution)/shard_map/all_to_all | solution.py:155
  44.1 0.5 broadcast.3586
  44.6 0.9 reduce
  47.3 0.7 maximum_select_fusion
  48.1 1.2 %subtract_bitcast_fusion = f32[1,1,256,64]{2,3,1,0:T(8,128)S(1)} fusion(f32[1,256,64]{1,2,0:T(8,128)S(1)} %get-tuple-element.22, f32[1,256,64]{1,2,0:T(8,128)S(1)} %get-tuple-element.23, f32[1,15,64]{1,2,0:T(8,128)S(1)} %slice.698, f32[1,15,64]{1,2,0:T(8,128)S(1)} %slice.701, f32[64]{0:T(128)S(1)} %get-tuple-element.89, f32[256]{0:T(256)S(1)} %bitcast.365, ...), kind=kLoop, calls=%fused_computation.168 | loop fusion | flops 3096576 | bytes 245248 | tf_op jit(solution)/shard_map/stack | solution.py:160
  49.2 1.1 %add_bitcast_fusion = f32[1,1,256,64]{2,3,1,0:T(8,128)S(1)} fusion(f32[1,256,64]{1,2,0:T(8,128)S(1)} %get-tuple-element.23, f32[1,256,64]{1,2,0:T(8,128)S(1)} %get-tuple-element.22, f32[1,15,64]{1,2,0:T(8,128)S(1)} %slice.698, f32[1,15,64]{1,2,0:T(8,128)S(1)} %slice.701, f32[64]{0:T(128)S(1)} %get-tuple-element.89, f32[256]{0:T(256)S(1)} %bitcast.366, ...), kind=kLoop, calls=%fused_computation.167 | loop fusion | flops 3096576 | bytes 245248 | tf_op jit(solution)/shard_map/stack | solution.py:160
  50.5 1.5 %reduce.1 = f32[256,2,64]{2,1,0:T(2,128)S(1)} reduce(f32[256,2,1,64]{3,2,1,0:T(1,128)S(1)} %bitcast.295, f32[]{:T(128)} %broadcast.3586), dimensions={2}, to_apply=%bitcast.276.reduce_sub_computation | reduce | bytes 262148
  52.1 0.9 reshape.5112
  53.0 5.2 %all-to-all-start.1 = ((f32[32,1,1024]{2,1,0:T(1,128)}), f32[32,1,1024]{2,1,0:T(1,128)S(1)}, u32[]{:S(2)}, u32[]{:S(2)}) async-start(f32[32,1,1024]{2,1,0:T(1,128)} %reshape.5112), calls=%async_computation.1 | async-start | bytes 262144 | tf_op jit(solution)/shard_map/all_to_all | solution.py:159
  58.3 6.5 %all-to-all-done.1 = f32[32,1,1024]{2,1,0:T(1,128)S(1)} async-done(((f32[32,1,1024]{2,1,0:T(1,128)}), f32[32,1,1024]{2,1,0:T(1,128)S(1)}, u32[]{:S(2)}, u32[]{:S(2)}) %all-to-all-start.1) | async-done | bytes 131104 | tf_op jit(solution)/shard_map/all_to_all | solution.py:159
  64.8 1.0 reduce.2
  69.9 2.0 %collective-permute-start.3 = (f32[2,8,2048]{2,1,0:T(8,128)S(1)}, f32[2,8,2048]{2,1,0:T(8,128)S(1)}, u32[]{:S(2)}, u32[]{:S(2)}) collective-permute-start(f32[2,8,2048]{2,1,0:T(8,128)S(1)} %pad_maximum_fusion.4), channel_id=1, source_target_pairs={{0,32},{32,0},{64,96},{96,64},{128,160},{160,128},{192,224},{224,1... | collective-permute-start | bytes 393224 | tf_op jit(solution)/shard_map/ppermute | solution.py:18
  72.0 3.8 %collective-permute-done.3 = f32[2,8,2048]{2,1,0:T(8,128)S(1)} collective-permute-done((f32[2,8,2048]{2,1,0:T(8,128)S(1)}, f32[2,8,2048]{2,1,0:T(8,128)S(1)}, u32[]{:S(2)}, u32[]{:S(2)}) %collective-permute-start.3) | collective-permute-done | bytes 131104 | tf_op jit(solution)/shard_map/ppermute | solution.py:18
  75.8 3.3 %collective-permute-start.4 = (f32[2,8,2048]{2,1,0:T(8,128)S(1)}, f32[2,8,2048]{2,1,0:T(8,128)S(1)}, u32[]{:S(2)}, u32[]{:S(2)}) collective-permute-start(f32[2,8,2048]{2,1,0:T(8,128)S(1)} %pad_maximum_fusion.5), channel_id=1, source_target_pairs={{0,64},{64,0},{32,96},{96,32},{128,192},{192,128},{160,224},{224,1... | collective-permute-start | bytes 393224 | tf_op jit(solution)/shard_map/ppermute | solution.py:18
  79.1 5.7 %collective-permute-done.4 = f32[2,8,2048]{2,1,0:T(8,128)S(1)} collective-permute-done((f32[2,8,2048]{2,1,0:T(8,128)S(1)}, f32[2,8,2048]{2,1,0:T(8,128)S(1)}, u32[]{:S(2)}, u32[]{:S(2)}) %collective-permute-start.4) | collective-permute-done | bytes 131104 | tf_op jit(solution)/shard_map/ppermute | solution.py:18
  84.9 6.6 %collective-permute-start.5 = (f32[2,8,2048]{2,1,0:T(8,128)S(1)}, f32[2,8,2048]{2,1,0:T(8,128)S(1)}, u32[]{:S(2)}, u32[]{:S(2)}) collective-permute-start(f32[2,8,2048]{2,1,0:T(8,128)S(1)} %pad_maximum_fusion.6), channel_id=1, source_target_pairs={{0,128},{128,0},{32,160},{160,32},{64,192},{192,64},{96,224},{224,... | collective-permute-start | bytes 393224 | tf_op jit(solution)/shard_map/ppermute | solution.py:18
  91.8 6.2 %collective-permute-done.5 = f32[2,8,2048]{2,1,0:T(8,128)S(1)} collective-permute-done((f32[2,8,2048]{2,1,0:T(8,128)S(1)}, f32[2,8,2048]{2,1,0:T(8,128)S(1)}, u32[]{:S(2)}, u32[]{:S(2)}) %collective-permute-start.5) | collective-permute-done | bytes 131104 | tf_op jit(solution)/shard_map/ppermute | solution.py:18
  98.0 0.7 select_multiply_fusion
  (77 shorter events, 9.1 us)
Async XLA Ops:
  0.9 10.9 %collective-permute-start = (f32[2,8,2048]{2,1,0:T(8,128)S(1)}, f32[2,8,2048]{2,1,0:T(8,128)S(1)}, u32[]{:S(2)}, u32[]{:S(2)}) collective-permute-start(f32[2,8,2048]{2,1,0:T(8,128)S(1)} %stack.58), channel_id=1, source_target_pairs={{0,128},{128,0},{32,160},{160,32},{64,192},{192,64},{96,224},{224,... | collective-permute-start | bytes 393224 | tf_op jit(solution)/shard_map/ppermute | solution.py:18
  8.2 0.8 copy-start.1
  8.3 3.4 %copy-start = (f32[8,2048]{1,0:T(8,128)S(1)}, f32[8,2048]{1,0:T(8,128)}, u32[]{:S(2)}) copy-start(f32[8,2048]{1,0:T(8,128)} %param.4) | copy-start | bytes 196612
  9.0 0.7 copy-start.2
  11.8 4.7 %copy-start.3 = (s32[1,64]{1,0:T(1,128)S(1)}, s32[1,64]{1,0:T(1,128)}, u32[]{:S(2)}) copy-start(s32[1,64]{1,0:T(1,128)} %param.7) | copy-start | bytes 772
  11.8 7.8 %collective-permute-start.1 = (f32[2,8,2048]{2,1,0:T(8,128)S(1)}, f32[2,8,2048]{2,1,0:T(8,128)S(1)}, u32[]{:S(2)}, u32[]{:S(2)}) collective-permute-start(f32[2,8,2048]{2,1,0:T(8,128)S(1)} %pad_maximum_fusion.1), channel_id=1, source_target_pairs={{0,64},{64,0},{32,96},{96,32},{128,192},{192,128},{160,224},{224,1... | collective-permute-start | bytes 393224 | tf_op jit(solution)/shard_map/ppermute | solution.py:18
  19.6 5.1 %collective-permute-start.2 = (f32[2,8,2048]{2,1,0:T(8,128)S(1)}, f32[2,8,2048]{2,1,0:T(8,128)S(1)}, u32[]{:S(2)}, u32[]{:S(2)}) collective-permute-start(f32[2,8,2048]{2,1,0:T(8,128)S(1)} %pad_maximum_fusion.2), channel_id=1, source_target_pairs={{0,32},{32,0},{64,96},{96,64},{128,160},{160,128},{192,224},{224,1... | collective-permute-start | bytes 393224 | tf_op jit(solution)/shard_map/ppermute | solution.py:18
  29.8 14.2 %all-to-all-start = ((f32[32,1,1024]{2,1,0:T(1,128)}), f32[32,1,1024]{2,1,0:T(1,128)S(1)}, u32[]{:S(2)}, u32[]{:S(2)}) async-start(f32[32,1,1024]{2,1,0:T(1,128)} %reshape.5110), calls=%async_computation | async-start | bytes 262144 | tf_op jit(solution)/shard_map/all_to_all | solution.py:155
  53.0 11.9 %all-to-all-start.1 = ((f32[32,1,1024]{2,1,0:T(1,128)}), f32[32,1,1024]{2,1,0:T(1,128)S(1)}, u32[]{:S(2)}, u32[]{:S(2)}) async-start(f32[32,1,1024]{2,1,0:T(1,128)} %reshape.5112), calls=%async_computation.1 | async-start | bytes 262144 | tf_op jit(solution)/shard_map/all_to_all | solution.py:159
  69.9 5.8 %collective-permute-start.3 = (f32[2,8,2048]{2,1,0:T(8,128)S(1)}, f32[2,8,2048]{2,1,0:T(8,128)S(1)}, u32[]{:S(2)}, u32[]{:S(2)}) collective-permute-start(f32[2,8,2048]{2,1,0:T(8,128)S(1)} %pad_maximum_fusion.4), channel_id=1, source_target_pairs={{0,32},{32,0},{64,96},{96,64},{128,160},{160,128},{192,224},{224,1... | collective-permute-start | bytes 393224 | tf_op jit(solution)/shard_map/ppermute | solution.py:18
  75.8 9.0 %collective-permute-start.4 = (f32[2,8,2048]{2,1,0:T(8,128)S(1)}, f32[2,8,2048]{2,1,0:T(8,128)S(1)}, u32[]{:S(2)}, u32[]{:S(2)}) collective-permute-start(f32[2,8,2048]{2,1,0:T(8,128)S(1)} %pad_maximum_fusion.5), channel_id=1, source_target_pairs={{0,64},{64,0},{32,96},{96,32},{128,192},{192,128},{160,224},{224,1... | collective-permute-start | bytes 393224 | tf_op jit(solution)/shard_map/ppermute | solution.py:18
  84.9 13.2 %collective-permute-start.5 = (f32[2,8,2048]{2,1,0:T(8,128)S(1)}, f32[2,8,2048]{2,1,0:T(8,128)S(1)}, u32[]{:S(2)}, u32[]{:S(2)}) collective-permute-start(f32[2,8,2048]{2,1,0:T(8,128)S(1)} %pad_maximum_fusion.6), channel_id=1, source_target_pairs={{0,128},{128,0},{32,160},{160,32},{64,192},{192,64},{96,224},{224,... | collective-permute-start | bytes 393224 | tf_op jit(solution)/shard_map/ppermute | solution.py:18
where the time goes:
time: 99.2 us; the launch traced here: 98.8 us
  starting transfers between devices  38.7 us (39%)
  waiting for transfers between devices  36.8 us (37%)
  local copies, waits for them, and re-layouts  7.85 us (8%)
  other arithmetic  7.79 us (8%)
  matrix products  6.74 us (7%)
    ppermute x6, starting transfers between devices, from_partner(): return lax.ppermute(block, axis, route)  25.9 us
    ppermute x6, waiting for transfers between devices, from_partner(): return lax.ppermute(block, axis, route)  23.7 us
    all_to_all x1, starting transfers between devices, per_device(): lax.all_to_all(jnp.stack([spec_real, spec_imag]), 'chan', split_axis=1, c...  7.62 us
    all_to_all x1, waiting for transfers between devices, per_device(): lax.all_to_all(jnp.stack([spec_real, spec_imag]), 'chan', split_axis=1, c...  6.59 us
    all_to_all x1, waiting for transfers between devices, per_device(): lax.all_to_all(jnp.stack([mixed_real, mixed_imag]), 'chan', split_axis=2,...  6.54 us
    all_to_all x1, starting transfers between devices, per_device(): lax.all_to_all(jnp.stack([mixed_real, mixed_imag]), 'chan', split_axis=2,...  5.17 us
    unnamed x12, local copies, waits for them, and re-layouts  3.32 us
    another operation x3, other arithmetic, per_device(): jnp.stack([mixed_real, mixed_imag])  2.31 us
  transfers between devices with their start and end apart: 8, of which 8 were waited for; matrix products, arithmetic and copies ran while one was open for 1% of the time, Pallas kernels for 0%

commit v1 on v0

--- a/solution.py
+++ b/solution.py
@@ -135,22 +135,18 @@
     channel_count, length = signal.shape
     total_len = length * blocks
     inner_len = math.gcd(128, length // lax.axis_size("chan"))
-    real_part = signal
-    imag_part = jnp.zeros_like(signal)
-    for bit_index in range(levels - 1, -1, -1):
-        half_span = 1 << bit_index
-        partner = from_partner(jnp.stack([real_part, imag_part]), "tm", bit_index)
-        upper_half = device_pos // half_span % 2 == 1
-        cosine, sine_part = twiddle(device_pos % half_span, 2 * half_span)
-        diff_real = partner[0] - real_part
-        diff_imag = partner[1] - imag_part
-        new_real = jnp.where(
-            upper_half, diff_real * cosine - diff_imag * sine_part, real_part + partner[0]
-        )
-        new_imag = jnp.where(
-            upper_half, diff_real * sine_part + diff_imag * cosine, imag_part + partner[1]
-        )
-        real_part, imag_part = (new_real, new_imag)
+    piece = length // blocks
+    block_ids = lax.iota(jnp.int32, blocks)
+    residues = reverse_bits(block_ids, levels)
+    pieces = signal.reshape(channel_count, blocks, piece).transpose(1, 0, 2)
+    gathered = lax.all_to_all(pieces, "tm", 0, 0, tiled=True)
+    cosine, sine_part = twiddle(residues[:, None] * block_ids[None, :] % blocks, blocks)
+    part_real = jnp.einsum("rb,bcs->rcs", cosine, gathered, precision=PRECISE)
+    part_imag = jnp.einsum("rb,bcs->rcs", sine_part, gathered, precision=PRECISE)
+    sent = jnp.stack([part_real, part_imag], axis=1)
+    spread_time = lax.all_to_all(sent, "tm", 0, 0, tiled=True)
+    real_part = spread_time[:, 0].transpose(1, 0, 2).reshape(channel_count, length)
+    imag_part = spread_time[:, 1].transpose(1, 0, 2).reshape(channel_count, length)
     spec_real, spec_imag = forward_local(real_part, imag_part, phase_bin, total_len, inner_len)
     spread = lax.all_to_all(
         jnp.stack([spec_real, spec_imag]), "chan", split_axis=1, concat_axis=2, tiled=True
@@ -160,22 +156,21 @@
         jnp.stack([mixed_real, mixed_imag]), "chan", split_axis=2, concat_axis=1, tiled=True
     )
     real_part, imag_part = inverse_local(returned[0], returned[1], phase_bin, total_len)
-    for bit_index in range(levels):
-        half_span = 1 << bit_index
-        partner = from_partner(jnp.stack([real_part, imag_part]), "tm", bit_index)
-        upper_half = device_pos // half_span % 2 == 1
-        cosine, sine_part = twiddle(device_pos % half_span, 2 * half_span)
-        sine_part = -sine_part
-        base_real = jnp.where(upper_half, partner[0], real_part)
-        base_imag = jnp.where(upper_half, partner[1], imag_part)
-        scaled_real = jnp.where(upper_half, real_part, partner[0])
-        scaled_imag = jnp.where(upper_half, imag_part, partner[1])
-        prod_real = scaled_real * cosine - scaled_imag * sine_part
-        prod_imag = scaled_real * sine_part + scaled_imag * cosine
-        real_part = jnp.where(upper_half, base_real - prod_real, base_real + prod_real)
-        imag_part = jnp.where(upper_half, base_imag - prod_imag, base_imag + prod_imag)
-    smoothed = real_part / total_len
-    return smoothed
+    back = jnp.stack(
+        [
+            real_part.reshape(channel_count, blocks, piece).transpose(1, 0, 2),
+            imag_part.reshape(channel_count, blocks, piece).transpose(1, 0, 2),
+        ],
+        axis=1,
+    )
+    by_residue = lax.all_to_all(back, "tm", 0, 0, tiled=True)
+    cosine, sine_part = twiddle(block_ids[:, None] * residues[None, :] % blocks, blocks)
+    combined = jnp.einsum(
+        "br,rcs->bcs", cosine, by_residue[:, 0], precision=PRECISE
+    ) + jnp.einsum("br,rcs->bcs", sine_part, by_residue[:, 1], precision=PRECISE)
+    returned_time = lax.all_to_all(combined, "tm", 0, 0, tiled=True)
+    smoothed = returned_time.transpose(1, 0, 2).reshape(channel_count, length)
+    return smoothed / total_len
 
 
 def solution(mesh):

time: 99.2 us -> 100 us (level)
  blocking collectives: 0 us -> 22.8 us
  starting transfers between devices: 38.7 us -> 24.5 us
  waiting for transfers between devices: 36.8 us -> 28.8 us
  matrix products: 6.74 us -> 7.84 us
    ppermute x6 -> x0, starting transfers between devices: 25.9 us -> none  [from_partner(): return lax.ppermute(block, axis, route)]
    ppermute x6 -> x0, waiting for transfers between devices: 23.7 us -> none  [from_partner(): return lax.ppermute(block, axis, route)]
    all_to_all x0 -> x2, blocking collectives: none -> 22.8 us  [the longest x1 12 us: per_device(): by_residue = lax.all_to_all(back, 'tm', 0, 0, tiled=True)]
    all_to_all x0 -> x2, waiting for transfers between devices: none -> 15.6 us  [the longest x1 8.89 us: per_device(): spread_time = lax.all_to_all(sent, 'tm', 0, 0, tiled=True)]
    all_to_all x0 -> x2, starting transfers between devices: none -> 11.8 us  [the longest x1 8.47 us: per_device(): gathered = lax.all_to_all(pieces, 'tm', 0, 0, tiled=True)]
    dot_general x0 -> x4, matrix products: none -> 1.1 us  [the longest x1 0.31 us: per_device(): part_real = jnp.einsum('rb,bcs->rcs', cosine, gathered, precision=PRECISE)]
    unnamed x12 -> x10, local copies, waits for them, and re-layouts: 3.32 us -> 3.48 us
  transfers between devices with their start and end apart: 8 -> 4, of which waited for: 8 -> 4; matrix products, arithmetic and copies ran while one was open for 1% -> 0% of each run, Pallas kernels for 0% -> 0%
where the time goes in v1:
time: 100 us; the launch traced here: 99.7 us
  waiting for transfers between devices  28.8 us (29%)
  starting transfers between devices  24.5 us (24%)
  blocking collectives  22.8 us (23%)
  matrix products  7.84 us (8%)
  local copies, waits for them, and re-layouts  7.68 us (8%)
  other arithmetic  7.57 us (8%)
    all_to_all x1, blocking collectives, per_device(): by_residue = lax.all_to_all(back, 'tm', 0, 0, tiled=True)  12 us
    all_to_all x1, blocking collectives, per_device(): returned_time = lax.all_to_all(combined, 'tm', 0, 0, tiled=True)  10.7 us
    all_to_all x1, waiting for transfers between devices, per_device(): spread_time = lax.all_to_all(sent, 'tm', 0, 0, tiled=True)  8.89 us
    all_to_all x1, starting transfers between devices, per_device(): gathered = lax.all_to_all(pieces, 'tm', 0, 0, tiled=True)  8.47 us
    all_to_all x1, starting transfers between devices, per_device(): lax.all_to_all(jnp.stack([spec_real, spec_imag]), 'chan', split_axis=1, c...  7.62 us
    all_to_all x1, waiting for transfers between devices, per_device(): gathered = lax.all_to_all(pieces, 'tm', 0, 0, tiled=True)  6.76 us
    all_to_all x1, waiting for transfers between devices, per_device(): lax.all_to_all(jnp.stack([spec_real, spec_imag]), 'chan', split_axis=1, c...  6.59 us
    all_to_all x1, waiting for transfers between devices, per_device(): lax.all_to_all(jnp.stack([mixed_real, mixed_imag]), 'chan', split_axis=2,...  6.53 us
  transfers between devices with their start and end apart: 4, of which 4 were waited for; matrix products, arithmetic and copies ran while one was open for 0% of the time, Pallas kernels for 0%

profile of v1, /device:TPU:2, one launch (start us, length us, event | category | flops | bytes accessed | tf_op | source)
XLA Modules:
  0.0 99.7 jit_solution(3705574331181759486)
XLA Ops:
  0.0 8.5 %all-to-all-start = ((f32[8,8,256]{2,1,0:T(8,128)}), f32[8,8,256]{2,1,0:T(8,128)S(1)}, u32[]{:S(2)}, u32[]{:S(2)}) async-start(f32[8,8,256]{2,1,0:T(8,128)} %bitcast.231), calls=%async_computation | async-start | bytes 131072 | tf_op jit(solution)/shard_map/all_to_all | solution.py:142
  8.5 0.7 copy-done.1
  9.2 0.6 copy-done.2
  10.1 6.8 %all-to-all-done = f32[8,8,256]{2,1,0:T(8,128)S(1)} async-done(((f32[8,8,256]{2,1,0:T(8,128)}), f32[8,8,256]{2,1,0:T(8,128)S(1)}, u32[]{:S(2)}, u32[]{:S(2)}) %all-to-all-start) | async-done | bytes 65568 | tf_op jit(solution)/shard_map/all_to_all | solution.py:142
  17.5 0.7 copy.48
  18.2 3.4 %all-to-all-start.1 = ((f32[8,2,8,256]{3,2,1,0:T(8,128)}), f32[8,2,8,256]{3,2,1,0:T(8,128)S(1)}, u32[]{:S(2)}, u32[]{:S(2)}) async-start(f32[8,2,8,256]{3,2,1,0:T(8,128)} %copy.48), calls=%async_computation.1 | async-start | bytes 262144 | tf_op jit(solution)/shard_map/all_to_all | solution.py:147
  21.7 8.9 %all-to-all-done.1 = f32[8,2,8,256]{3,2,1,0:T(8,128)S(1)} async-done(((f32[8,2,8,256]{3,2,1,0:T(8,128)}), f32[8,2,8,256]{3,2,1,0:T(8,128)S(1)}, u32[]{:S(2)}, u32[]{:S(2)}) %all-to-all-start.1) | async-done | bytes 131104 | tf_op jit(solution)/shard_map/all_to_all | solution.py:147
  30.9 0.6 fusion.49
  31.5 0.6 fusion.48
  32.1 0.6 convolution_subtract_fusion.3
  32.7 0.6 convolution_add_fusion.3
  34.9 0.8 reshape.5042
  35.7 7.6 %all-to-all-start.2 = ((f32[32,1,1024]{2,1,0:T(1,128)}), f32[32,1,1024]{2,1,0:T(1,128)S(1)}, u32[]{:S(2)}, u32[]{:S(2)}) async-start(f32[32,1,1024]{2,1,0:T(1,128)} %reshape.5042), calls=%async_computation.2 | async-start | bytes 262144 | tf_op jit(solution)/shard_map/all_to_all | solution.py:151
  43.4 6.6 %all-to-all-done.2 = f32[32,1,1024]{2,1,0:T(1,128)S(1)} async-done(((f32[32,1,1024]{2,1,0:T(1,128)}), f32[32,1,1024]{2,1,0:T(1,128)S(1)}, u32[]{:S(2)}, u32[]{:S(2)}) %all-to-all-start.2) | async-done | bytes 131104 | tf_op jit(solution)/shard_map/all_to_all | solution.py:151
  49.9 0.5 broadcast.3743
  50.5 0.9 reduce
  53.2 0.7 maximum_select_fusion
  53.9 1.2 %subtract_bitcast_fusion.1 = f32[1,1,256,64]{2,3,1,0:T(8,128)S(1)} fusion(f32[1,256,64]{1,2,0:T(8,128)S(1)} %get-tuple-element.13, f32[1,256,64]{1,2,0:T(8,128)S(1)} %get-tuple-element.14, f32[1,15,64]{1,2,0:T(8,128)S(1)} %slice.651, f32[1,15,64]{1,2,0:T(8,128)S(1)} %slice.654, f32[64]{0:T(128)S(1)} %get-tuple-element.82, f32[256]{0:T(256)S(1)} %bitcast.294, ...), kind=kLoop, calls=%fused_computation.151 | loop fusion | flops 3096576 | bytes 245248 | tf_op jit(solution)/shard_map/stack | solution.py:156
  55.1 1.1 %add_bitcast_fusion.1 = f32[1,1,256,64]{2,3,1,0:T(8,128)S(1)} fusion(f32[1,256,64]{1,2,0:T(8,128)S(1)} %get-tuple-element.14, f32[1,256,64]{1,2,0:T(8,128)S(1)} %get-tuple-element.13, f32[1,15,64]{1,2,0:T(8,128)S(1)} %slice.651, f32[1,15,64]{1,2,0:T(8,128)S(1)} %slice.654, f32[64]{0:T(128)S(1)} %get-tuple-element.82, f32[256]{0:T(256)S(1)} %bitcast.295, ...), kind=kLoop, calls=%fused_computation.150 | loop fusion | flops 3096576 | bytes 245248 | tf_op jit(solution)/shard_map/stack | solution.py:156
  56.4 1.5 %reduce.1 = f32[256,2,64]{2,1,0:T(2,128)S(1)} reduce(f32[256,2,1,64]{3,2,1,0:T(1,128)S(1)} %bitcast.228, f32[]{:T(128)} %broadcast.3743), dimensions={2}, to_apply=%bitcast.217.reduce_sub_computation | reduce | bytes 262148
  58.0 0.9 reshape.5044
  58.9 5.0 %all-to-all-start.3 = ((f32[32,1,1024]{2,1,0:T(1,128)}), f32[32,1,1024]{2,1,0:T(1,128)S(1)}, u32[]{:S(2)}, u32[]{:S(2)}) async-start(f32[32,1,1024]{2,1,0:T(1,128)} %reshape.5044), calls=%async_computation.3 | async-start | bytes 262144 | tf_op jit(solution)/shard_map/all_to_all | solution.py:155
  64.0 6.5 %all-to-all-done.3 = f32[32,1,1024]{2,1,0:T(1,128)S(1)} async-done(((f32[32,1,1024]{2,1,0:T(1,128)}), f32[32,1,1024]{2,1,0:T(1,128)S(1)}, u32[]{:S(2)}, u32[]{:S(2)}) %all-to-all-start.3) | async-done | bytes 131104 | tf_op jit(solution)/shard_map/all_to_all | solution.py:155
  70.6 1.0 reduce.2
  73.1 0.4 convolution_add_fusion.1
  73.4 0.4 fusion.9
  73.8 0.4 fusion.7
  74.2 0.4 fusion.1
  74.9 0.4 fusion
  75.7 12.0 %all_to_all.41 = f32[8,2,8,256]{3,2,1,0:T(8,128)S(1)} all-to-all(f32[8,2,8,256]{3,2,1,0:T(8,128)S(1)} %copy.99), channel_id=1, replica_groups=mesh['tm'=8,'chan'=32] {'tm'}, dimensions={0} | all-to-all | bytes 262144 | tf_op jit(solution)/shard_map/all_to_all | solution.py:166
  88.3 10.7 %all_to_all.42 = f32[8,8,256]{2,1,0:T(8,128)S(1)} all-to-all(f32[8,8,256]{2,1,0:T(8,128)S(1)} %copy.102), channel_id=1, replica_groups=mesh['tm'=8,'chan'=32] {'tm'}, dimensions={0} | all-to-all | bytes 131072 | tf_op jit(solution)/shard_map/all_to_all | solution.py:171
  99.0 0.6 broadcast_multiply_fusion
  (69 shorter events, 7.4 us)
Async XLA Ops:
  0.0 16.8 %all-to-all-start = ((f32[8,8,256]{2,1,0:T(8,128)}), f32[8,8,256]{2,1,0:T(8,128)S(1)}, u32[]{:S(2)}, u32[]{:S(2)}) async-start(f32[8,8,256]{2,1,0:T(8,128)} %bitcast.231), calls=%async_computation | async-start | bytes 131072 | tf_op jit(solution)/shard_map/all_to_all | solution.py:142
  8.5 0.7 copy-start.1
  8.5 1.4 %copy-start = (f32[2,16,256]{2,1,0:T(8,128)S(1)}, f32[2,16,256]{2,1,0:T(8,128)}, u32[]{:S(2)}) copy-start(f32[2,16,256]{2,1,0:T(8,128)} %param.5) | copy-start | bytes 98308
  9.2 0.7 copy-start.2
  18.2 12.4 %all-to-all-start.1 = ((f32[8,2,8,256]{3,2,1,0:T(8,128)}), f32[8,2,8,256]{3,2,1,0:T(8,128)S(1)}, u32[]{:S(2)}, u32[]{:S(2)}) async-start(f32[8,2,8,256]{3,2,1,0:T(8,128)} %copy.48), calls=%async_computation.1 | async-start | bytes 262144 | tf_op jit(solution)/shard_map/all_to_all | solution.py:147
  35.7 14.2 %all-to-all-start.2 = ((f32[32,1,1024]{2,1,0:T(1,128)}), f32[32,1,1024]{2,1,0:T(1,128)S(1)}, u32[]{:S(2)}, u32[]{:S(2)}) async-start(f32[32,1,1024]{2,1,0:T(1,128)} %reshape.5042), calls=%async_computation.2 | async-start | bytes 262144 | tf_op jit(solution)/shard_map/all_to_all | solution.py:151
  58.9 11.7 %all-to-all-start.3 = ((f32[32,1,1024]{2,1,0:T(1,128)}), f32[32,1,1024]{2,1,0:T(1,128)S(1)}, u32[]{:S(2)}, u32[]{:S(2)}) async-start(f32[32,1,1024]{2,1,0:T(1,128)} %reshape.5044), calls=%async_computation.3 | async-start | bytes 262144 | tf_op jit(solution)/shard_map/all_to_all | solution.py:155

commit v2 on v0

--- a/solution.py
+++ b/solution.py
@@ -98,30 +98,39 @@
     return (real_part * cosine - imag_part * sine_part, real_part * sine_part + imag_part * cosine)
 
 
-def mix_bins(spread, band, response, offsets):
-    fine_len, channel_all, inner_len = (spread.shape[1], spread.shape[2], spread.shape[3])
-    band_width = band.shape[1]
+def from_offset(block, axis, delta):
+    count = lax.axis_size(axis)
+    return lax.ppermute(block, axis, [((i + delta) % count, i) for i in range(count)])
+
+
+def mix_halo(window, band_rows, table, halo_below, channel_all):
+    _, outer_len, _, inner_len = window.shape
+    band_width = band_rows.shape[1]
     half_width = band_width // 2
-    shift_cols = offsets.reshape(1, fine_len, 1, inner_len)
-    centered = (shift_cols + half_width) % channel_all - half_width
-    moved = jnp.zeros_like(spread)
+    own = band_rows.shape[2]
+    span = own + band_width - 1
+    if table.shape[0] != outer_len:
+        rows = table.shape[1]
+        table = table.transpose(1, 0, 2).reshape(rows, outer_len, inner_len).transpose(1, 0, 2)
+    responses = table[:, : 2 * band_width].reshape(outer_len, 2, band_width, inner_len)
+    shift = table[:, 2 * band_width].astype(jnp.int32)
+    centered = (shift + half_width) % channel_all - half_width
+    moved = jnp.zeros(window.shape[:2] + (span, inner_len), window.dtype)
     for shift_amount in range(-half_width, half_width + 1):
-        rolled = jnp.roll(spread, -shift_amount, axis=2)
-        moved = jnp.where(centered == shift_amount, rolled, moved)
-    moved_real = moved[0]
-    moved_imag = moved[1]
-    wide_real = jnp.concatenate([moved_real, moved_real[:, : band_width - 1]], axis=1)
-    wide_imag = jnp.concatenate([moved_imag, moved_imag[:, : band_width - 1]], axis=1)
-    responses = response.reshape(2, band_width, fine_len, 1, inner_len)
-    acc_real = jnp.zeros_like(moved_real)
-    acc_imag = jnp.zeros_like(moved_imag)
+        lo = halo_below + shift_amount
+        piece = window[:, :, lo : lo + span]
+        moved = jnp.where((centered == shift_amount)[None, :, None, :], piece, moved)
+    acc_real = jnp.zeros((outer_len, own, inner_len), window.dtype)
+    acc_imag = jnp.zeros((outer_len, own, inner_len), window.dtype)
     for lag_index in range(band_width):
-        value_real = wide_real[:, lag_index : lag_index + channel_all]
-        value_imag = wide_imag[:, lag_index : lag_index + channel_all]
-        gain_real = band[0, lag_index][None, :, None]
-        gain_imag = band[1, lag_index][None, :, None]
-        coef_real = gain_real * responses[0, lag_index] - gain_imag * responses[1, lag_index]
-        coef_imag = gain_real * responses[1, lag_index] + gain_imag * responses[0, lag_index]
+        value_real = moved[0, :, lag_index : lag_index + own]
+        value_imag = moved[1, :, lag_index : lag_index + own]
+        gain_real = band_rows[0, lag_index][None, :, None]
+        gain_imag = band_rows[1, lag_index][None, :, None]
+        resp_real = responses[:, 0, lag_index][:, None, :]
+        resp_imag = responses[:, 1, lag_index][:, None, :]
+        coef_real = gain_real * resp_real - gain_imag * resp_imag
+        coef_imag = gain_real * resp_imag + gain_imag * resp_real
         acc_real = acc_real + coef_real * value_real - coef_imag * value_imag
         acc_imag = acc_imag + coef_real * value_imag + coef_imag * value_real
     return (acc_real, acc_imag)
@@ -152,14 +161,19 @@
         )
         real_part, imag_part = (new_real, new_imag)
     spec_real, spec_imag = forward_local(real_part, imag_part, phase_bin, total_len, inner_len)
-    spread = lax.all_to_all(
-        jnp.stack([spec_real, spec_imag]), "chan", split_axis=1, concat_axis=2, tiled=True
-    )
-    mixed_real, mixed_imag = mix_bins(spread, band, response, offsets)
-    returned = lax.all_to_all(
-        jnp.stack([mixed_real, mixed_imag]), "chan", split_axis=2, concat_axis=1, tiled=True
-    )
-    real_part, imag_part = inverse_local(returned[0], returned[1], phase_bin, total_len)
+    own = channel_count
+    band_width = band.shape[1]
+    chan_pos = lax.axis_index("chan")
+    band_rows = lax.dynamic_slice_in_dim(band, chan_pos * own, own, axis=2)
+    packed = jnp.concatenate(
+        [response.reshape(2 * band_width, -1), offsets.reshape(1, -1).astype(jnp.float32)], axis=0
+    )
+    table = lax.all_gather(packed, "chan")
+    spectra = jnp.stack([spec_real, spec_imag])
+    neighbours = [from_offset(spectra, "chan", delta) for delta in (-1, 1, 2, 3)]
+    window = jnp.concatenate([neighbours[0], spectra] + neighbours[1:], axis=2)
+    mixed_real, mixed_imag = mix_halo(window, band_rows, table, own, band.shape[2])
+    real_part, imag_part = inverse_local(mixed_real, mixed_imag, phase_bin, total_len)
     for bit_index in range(levels):
         half_span = 1 << bit_index
         partner = from_partner(jnp.stack([real_part, imag_part]), "tm", bit_index)

time: 99.2 us -> 106 us (1.069)
  blocking collectives: 0 us -> 24.8 us
  starting transfers between devices: 38.7 us -> 14.9 us
  waiting for transfers between devices: 36.8 us -> 49.6 us
  other arithmetic: 7.79 us -> 4.16 us
  local copies, waits for them, and re-layouts: 7.85 us -> 4.5 us
    all_gather x0 -> x1, blocking collectives: none -> 24.8 us  [per_device(): table = lax.all_gather(packed, 'chan')]
    ppermute x6, starting transfers between devices: 25.9 us -> 10.3 us  [from_partner(): return lax.ppermute(block, axis, route)]
    ppermute x0 -> x4, waiting for transfers between devices: none -> 14.9 us  [from_offset(): lax.ppermute(block, axis, [((i + delta) % count, i) for i in range(count)])]
    all_to_all x2 -> x0, waiting for transfers between devices: 13.1 us -> none  [the longest x1 6.59 us: per_device(): lax.all_to_all(jnp.stack([spec_real, spec_imag]), 'chan', split_axis=1, c...]
    all_to_all x2 -> x0, starting transfers between devices: 12.8 us -> none  [the longest x1 7.62 us: per_device(): lax.all_to_all(jnp.stack([spec_real, spec_imag]), 'chan', split_axis=1, c...]
    ppermute x6, waiting for transfers between devices: 23.7 us -> 34.7 us  [from_partner(): return lax.ppermute(block, axis, route)]
    ppermute x0 -> x4, starting transfers between devices: none -> 4.66 us  [from_offset(): lax.ppermute(block, axis, [((i + delta) % count, i) for i in range(count)])]
    another operation x4 -> x1, other arithmetic: 2.33 us -> 0.02 us  [per_device(): spectra = jnp.stack([spec_real, spec_imag])]
  transfers between devices with their start and end apart: 8 -> 10, of which waited for: 8 -> 9; matrix products, arithmetic and copies ran while one was open for 1% -> 1% of each run, Pallas kernels for 0% -> 0%
where the time goes in v2:
time: 106 us
  waiting for transfers between devices  49.6 us (47%)
  blocking collectives  24.8 us (23%)
  starting transfers between devices  14.9 us (14%)
  matrix products  6.72 us (6%)
  local copies, waits for them, and re-layouts  4.5 us (4%)
  other arithmetic  4.16 us (4%)
    ppermute x6, waiting for transfers between devices, from_partner(): return lax.ppermute(block, axis, route)  34.7 us
    all_gather x1, blocking collectives, per_device(): table = lax.all_gather(packed, 'chan')  24.8 us
    ppermute x4, waiting for transfers between devices, from_offset(): lax.ppermute(block, axis, [((i + delta) % count, i) for i in range(count)])  14.9 us
    ppermute x6, starting transfers between devices, from_partner(): return lax.ppermute(block, axis, route)  10.3 us
    ppermute x4, starting transfers between devices, from_offset(): lax.ppermute(block, axis, [((i + delta) % count, i) for i in range(count)])  4.66 us
  transfers between devices with their start and end apart: 10, of which 9 were waited for; matrix products, arithmetic and copies ran while one was open for 1% of the time, Pallas kernels for 0%

profile of v2, /device:TPU:2, one launch (start us, length us, event | category | flops | bytes accessed | tf_op | source)
XLA Modules:
  0.0 105.5 jit_solution(8379092941251316191)
XLA Ops:
  0.0 0.8 stack.49
  0.9 7.3 %collective-permute-start = (f32[2,8,2048]{2,1,0:T(8,128)S(1)}, f32[2,8,2048]{2,1,0:T(8,128)S(1)}, u32[]{:S(2)}, u32[]{:S(2)}) collective-permute-start(f32[2,8,2048]{2,1,0:T(8,128)S(1)} %stack.49), channel_id=1, source_target_pairs={{0,128},{128,0},{32,160},{160,32},{64,192},{192,64},{96,224},{224,... | collective-permute-start | bytes 393224 | tf_op jit(solution)/shard_map/ppermute | solution.py:18
  8.3 0.6 copy-done.3
  9.0 24.8 %all-gather.1 = f32[32,33,64]{2,1,0:T(8,128)S(1)} all-gather(f32[1,33,64]{2,1,0:T(8,128)S(1)} %maximum_bitcast_fusion), channel_id=2, replica_groups=mesh['tm'=8,'chan'=32] {'chan'}, dimensions={0}, use_global_device_ids=true | all-gather | bytes 278784 | tf_op jit(solution)/shard_map/all_gather | solution.py:171
  34.5 0.5 copy-done
  35.0 1.6 %collective-permute-start.1 = (f32[2,8,2048]{2,1,0:T(8,128)S(1)}, f32[2,8,2048]{2,1,0:T(8,128)S(1)}, u32[]{:S(2)}, u32[]{:S(2)}) collective-permute-start(f32[2,8,2048]{2,1,0:T(8,128)S(1)} %pad_maximum_fusion.7), channel_id=1, source_target_pairs={{0,64},{64,0},{32,96},{96,32},{128,192},{192,128},{160,224},{224,1... | collective-permute-start | bytes 393224 | tf_op jit(solution)/shard_map/ppermute | solution.py:18
  36.9 7.6 %collective-permute-done.1 = f32[2,8,2048]{2,1,0:T(8,128)S(1)} collective-permute-done((f32[2,8,2048]{2,1,0:T(8,128)S(1)}, f32[2,8,2048]{2,1,0:T(8,128)S(1)}, u32[]{:S(2)}, u32[]{:S(2)}) %collective-permute-start.1) | collective-permute-done | bytes 131104 | tf_op jit(solution)/shard_map/ppermute | solution.py:18
  44.9 4.8 %collective-permute-done.2 = f32[2,8,2048]{2,1,0:T(8,128)S(1)} collective-permute-done((f32[2,8,2048]{2,1,0:T(8,128)S(1)}, f32[2,8,2048]{2,1,0:T(8,128)S(1)}, u32[]{:S(2)}, u32[]{:S(2)}) %collective-permute-start.2) | collective-permute-done | bytes 131104 | tf_op jit(solution)/shard_map/ppermute | solution.py:18
  49.8 0.6 fusion.39
  50.4 0.6 fusion.45
  51.1 0.6 convolution_add_fusion.3
  51.8 0.6 convolution_subtract_fusion.3
  53.9 2.8 %collective-permute-start.4 = (f32[2,32,8,64]{3,1,2,0:T(8,128)S(1)}, f32[2,32,8,64]{3,1,2,0:T(8,128)S(1)}, u32[]{:S(2)}, u32[]{:S(2)}) collective-permute-start(f32[2,32,8,64]{3,1,2,0:T(8,128)S(1)} %pad_maximum_fusion.6), channel_id=1, source_target_pairs={{2,0},{3,1},{4,2},{5,3},{6,4},{7,5},{8,6},{9,7},{10,8},{11,9},{12,... | collective-permute-start | bytes 393224 | tf_op jit(solution)/shard_map/ppermute | solution.py:103
  56.7 1.4 %collective-permute-start.3 = (f32[2,32,8,64]{3,1,2,0:T(8,128)S(1)}, f32[2,32,8,64]{3,1,2,0:T(8,128)S(1)}, u32[]{:S(2)}, u32[]{:S(2)}) collective-permute-start(f32[2,32,8,64]{3,1,2,0:T(8,128)S(1)} %pad_maximum_fusion.6), channel_id=1, source_target_pairs={{1,0},{2,1},{3,2},{4,3},{5,4},{6,5},{7,6},{8,7},{9,8},{10,9},{11,1... | collective-permute-start | bytes 393224 | tf_op jit(solution)/shard_map/ppermute | solution.py:103
  58.1 0.7 copy-done.2
  59.0 0.4 collective-permute-start.5
  59.4 2.3 %collective-permute-done.6 = f32[2,32,8,64]{3,1,2,0:T(8,128)S(1)} collective-permute-done((f32[2,32,8,64]{3,1,2,0:T(8,128)S(1)}, f32[2,32,8,64]{3,1,2,0:T(8,128)S(1)}, u32[]{:S(2)}, u32[]{:S(2)}) %collective-permute-start.6) | collective-permute-done | bytes 131104 | tf_op jit(solution)/shard_map/ppermute | solution.py:103
  61.8 1.6 %collective-permute-done.4 = f32[2,32,8,64]{3,1,2,0:T(8,128)S(1)} collective-permute-done((f32[2,32,8,64]{3,1,2,0:T(8,128)S(1)}, f32[2,32,8,64]{3,1,2,0:T(8,128)S(1)}, u32[]{:S(2)}, u32[]{:S(2)}) %collective-permute-start.4) | collective-permute-done | bytes 131104 | tf_op jit(solution)/shard_map/ppermute | solution.py:103
  63.4 7.8 %collective-permute-done.3 = f32[2,32,8,64]{3,1,2,0:T(8,128)S(1)} collective-permute-done((f32[2,32,8,64]{3,1,2,0:T(8,128)S(1)}, f32[2,32,8,64]{3,1,2,0:T(8,128)S(1)}, u32[]{:S(2)}, u32[]{:S(2)}) %collective-permute-start.3) | collective-permute-done | bytes 131104 | tf_op jit(solution)/shard_map/ppermute | solution.py:103
  71.4 3.1 %collective-permute-done.5 = f32[2,32,8,64]{3,1,2,0:T(8,128)S(1)} collective-permute-done((f32[2,32,8,64]{3,1,2,0:T(8,128)S(1)}, f32[2,32,8,64]{3,1,2,0:T(8,128)S(1)}, u32[]{:S(2)}, u32[]{:S(2)}) %collective-permute-start.5) | collective-permute-done | bytes 131104 | tf_op jit(solution)/shard_map/ppermute | solution.py:103
  74.8 0.6 fusion.19
  75.4 0.9 multiply_add_fusion.1
  76.3 0.9 multiply_subtract_fusion.1
  78.5 0.4 fusion.22
  78.9 0.4 fusion.24
  79.3 0.4 fusion
  80.0 0.4 fusion.1
  81.1 4.7 %collective-permute-done.7 = f32[2,8,2048]{2,1,0:T(8,128)S(1)} collective-permute-done((f32[2,8,2048]{2,1,0:T(8,128)S(1)}, f32[2,8,2048]{2,1,0:T(8,128)S(1)}, u32[]{:S(2)}, u32[]{:S(2)}) %collective-permute-start.7) | collective-permute-done | bytes 131104 | tf_op jit(solution)/shard_map/ppermute | solution.py:18
  85.9 0.9 collective-permute-start.8
  86.8 9.0 %collective-permute-done.8 = f32[2,8,2048]{2,1,0:T(8,128)S(1)} collective-permute-done((f32[2,8,2048]{2,1,0:T(8,128)S(1)}, f32[2,8,2048]{2,1,0:T(8,128)S(1)}, u32[]{:S(2)}, u32[]{:S(2)}) %collective-permute-start.8) | collective-permute-done | bytes 131104 | tf_op jit(solution)/shard_map/ppermute | solution.py:18
  96.2 8.6 %collective-permute-done.9 = f32[2,8,2048]{2,1,0:T(8,128)S(1)} collective-permute-done((f32[2,8,2048]{2,1,0:T(8,128)S(1)}, f32[2,8,2048]{2,1,0:T(8,128)S(1)}, u32[]{:S(2)}, u32[]{:S(2)}) %collective-permute-start.9) | collective-permute-done | bytes 131104 | tf_op jit(solution)/shard_map/ppermute | solution.py:18
  104.8 0.7 select_multiply_fusion
  (54 shorter events, 6.3 us)
Async XLA Ops:
  0.9 33.6 %collective-permute-start = (f32[2,8,2048]{2,1,0:T(8,128)S(1)}, f32[2,8,2048]{2,1,0:T(8,128)S(1)}, u32[]{:S(2)}, u32[]{:S(2)}) collective-permute-start(f32[2,8,2048]{2,1,0:T(8,128)S(1)} %stack.49), channel_id=1, source_target_pairs={{0,128},{128,0},{32,160},{160,32},{64,192},{192,64},{96,224},{224,... | collective-permute-start | bytes 393224 | tf_op jit(solution)/shard_map/ppermute | solution.py:18
  8.3 0.7 copy-start.1
  8.3 0.7 copy-start.3
  34.1 0.8 copy-start
  35.0 9.5 %collective-permute-start.1 = (f32[2,8,2048]{2,1,0:T(8,128)S(1)}, f32[2,8,2048]{2,1,0:T(8,128)S(1)}, u32[]{:S(2)}, u32[]{:S(2)}) collective-permute-start(f32[2,8,2048]{2,1,0:T(8,128)S(1)} %pad_maximum_fusion.7), channel_id=1, source_target_pairs={{0,64},{64,0},{32,96},{96,32},{128,192},{192,128},{160,224},{224,1... | collective-permute-start | bytes 393224 | tf_op jit(solution)/shard_map/ppermute | solution.py:18
  44.6 5.1 %collective-permute-start.2 = (f32[2,8,2048]{2,1,0:T(8,128)S(1)}, f32[2,8,2048]{2,1,0:T(8,128)S(1)}, u32[]{:S(2)}, u32[]{:S(2)}) collective-permute-start(f32[2,8,2048]{2,1,0:T(8,128)S(1)} %pad_maximum_fusion.8), channel_id=1, source_target_pairs={{0,32},{32,0},{64,96},{96,64},{128,160},{160,128},{192,224},{224,1... | collective-permute-start | bytes 393224 | tf_op jit(solution)/shard_map/ppermute | solution.py:18
  53.8 8.0 %collective-permute-start.6 = (f32[2,32,8,64]{3,1,2,0:T(8,128)S(1)}, f32[2,32,8,64]{3,1,2,0:T(8,128)S(1)}, u32[]{:S(2)}, u32[]{:S(2)}) collective-permute-start(f32[2,32,8,64]{3,1,2,0:T(8,128)S(1)} %pad_maximum_fusion.6), channel_id=1, source_target_pairs={{31,0},{0,1},{1,2},{2,3},{3,4},{4,5},{5,6},{6,7},{7,8},{8,9},{9,10... | collective-permute-start | bytes 393224 | tf_op jit(solution)/shard_map/ppermute | solution.py:103
  53.9 9.5 %collective-permute-start.4 = (f32[2,32,8,64]{3,1,2,0:T(8,128)S(1)}, f32[2,32,8,64]{3,1,2,0:T(8,128)S(1)}, u32[]{:S(2)}, u32[]{:S(2)}) collective-permute-start(f32[2,32,8,64]{3,1,2,0:T(8,128)S(1)} %pad_maximum_fusion.6), channel_id=1, source_target_pairs={{2,0},{3,1},{4,2},{5,3},{6,4},{7,5},{8,6},{9,7},{10,8},{11,9},{12,... | collective-permute-start | bytes 393224 | tf_op jit(solution)/shard_map/ppermute | solution.py:103
  56.7 14.6 %collective-permute-start.3 = (f32[2,32,8,64]{3,1,2,0:T(8,128)S(1)}, f32[2,32,8,64]{3,1,2,0:T(8,128)S(1)}, u32[]{:S(2)}, u32[]{:S(2)}) collective-permute-start(f32[2,32,8,64]{3,1,2,0:T(8,128)S(1)} %pad_maximum_fusion.6), channel_id=1, source_target_pairs={{1,0},{2,1},{3,2},{4,3},{5,4},{6,5},{7,6},{8,7},{9,8},{10,9},{11,1... | collective-permute-start | bytes 393224 | tf_op jit(solution)/shard_map/ppermute | solution.py:103
  58.1 0.8 copy-start.2
  59.0 15.5 %collective-permute-start.5 = (f32[2,32,8,64]{3,1,2,0:T(8,128)S(1)}, f32[2,32,8,64]{3,1,2,0:T(8,128)S(1)}, u32[]{:S(2)}, u32[]{:S(2)}) collective-permute-start(f32[2,32,8,64]{3,1,2,0:T(8,128)S(1)} %pad_maximum_fusion.6), channel_id=1, source_target_pairs={{3,0},{4,1},{5,2},{6,3},{7,4},{8,5},{9,6},{10,7},{11,8},{12,9},{13... | collective-permute-start | bytes 393224 | tf_op jit(solution)/shard_map/ppermute | solution.py:103
  80.7 5.1 %collective-permute-start.7 = (f32[2,8,2048]{2,1,0:T(8,128)S(1)}, f32[2,8,2048]{2,1,0:T(8,128)S(1)}, u32[]{:S(2)}, u32[]{:S(2)}) collective-permute-start(f32[2,8,2048]{2,1,0:T(8,128)S(1)} %pad_maximum_fusion.9), channel_id=1, source_target_pairs={{0,32},{32,0},{64,96},{96,64},{128,160},{160,128},{192,224},{224,1... | collective-permute-start | bytes 393224 | tf_op jit(solution)/shard_map/ppermute | solution.py:18
  85.9 9.9 %collective-permute-start.8 = (f32[2,8,2048]{2,1,0:T(8,128)S(1)}, f32[2,8,2048]{2,1,0:T(8,128)S(1)}, u32[]{:S(2)}, u32[]{:S(2)}) collective-permute-start(f32[2,8,2048]{2,1,0:T(8,128)S(1)} %pad_maximum_fusion.10), channel_id=1, source_target_pairs={{0,64},{64,0},{32,96},{96,32},{128,192},{192,128},{160,224},{224,1... | collective-permute-start | bytes 393224 | tf_op jit(solution)/shard_map/ppermute | solution.py:18
  95.8 9.0 %collective-permute-start.9 = (f32[2,8,2048]{2,1,0:T(8,128)S(1)}, f32[2,8,2048]{2,1,0:T(8,128)S(1)}, u32[]{:S(2)}, u32[]{:S(2)}) collective-permute-start(f32[2,8,2048]{2,1,0:T(8,128)S(1)} %pad_maximum_fusion.11), channel_id=1, source_target_pairs={{0,128},{128,0},{32,160},{160,32},{64,192},{192,64},{96,224},{224,... | collective-permute-start | bytes 393224 | tf_op jit(solution)/shard_map/ppermute | solution.py:18

commit v3 on v2

--- a/solution.py
+++ b/solution.py
@@ -101,6 +101,18 @@
 def from_offset(block, axis, delta):
     count = lax.axis_size(axis)
     return lax.ppermute(block, axis, [((i + delta) % count, i) for i in range(count)])
+
+
+def gather_doubling(block, axis):
+    count = lax.axis_size(axis)
+    me = lax.axis_index(axis)
+    stride = 1
+    while stride < count:
+        partner = from_partner(block, axis, stride.bit_length() - 1)
+        upper = me // stride % 2 == 1
+        block = jnp.where(upper, jnp.concatenate([partner, block]), jnp.concatenate([block, partner]))
+        stride *= 2
+    return block
 
 
 def mix_halo(window, band_rows, table, halo_below, channel_all):
@@ -168,7 +180,7 @@
     packed = jnp.concatenate(
         [response.reshape(2 * band_width, -1), offsets.reshape(1, -1).astype(jnp.float32)], axis=0
     )
-    table = lax.all_gather(packed, "chan")
+    table = gather_doubling(packed[None], "chan")
     spectra = jnp.stack([spec_real, spec_imag])
     neighbours = [from_offset(spectra, "chan", delta) for delta in (-1, 1, 2, 3)]
     window = jnp.concatenate([neighbours[0], spectra] + neighbours[1:], axis=2)

time: 106 us -> 97.7 us (0.922)
  blocking collectives: 24.8 us -> 0 us
  starting transfers between devices: 14.9 us -> 26.7 us
  waiting for transfers between devices: 49.6 us -> 56 us
  local copies, waits for them, and re-layouts: 4.5 us -> 1.31 us
  other arithmetic: 4.16 us -> 5.85 us
    all_gather x1 -> x0, blocking collectives: 24.8 us -> none  [per_device(): table = lax.all_gather(packed, 'chan')]
    ppermute x6 -> x11, starting transfers between devices: 10.3 us -> 21.4 us  [from_partner(): return lax.ppermute(block, axis, route)]
    ppermute x6 -> x11, waiting for transfers between devices: 34.7 us -> 40.4 us  [from_partner(): return lax.ppermute(block, axis, route)]
    unnamed x8 -> x4, local copies, waits for them, and re-layouts: 1.93 us -> 0.01 us
  transfers between devices with their start and end apart: 10 -> 15, of which waited for: 9 -> 13; matrix products, arithmetic and copies ran while one was open for 1% -> 1% of each run, Pallas kernels for 0% -> 0%
where the time goes in v3:
time: 97.7 us; the launch traced here: 97.5 us
  waiting for transfers between devices  56 us (57%)
  starting transfers between devices  26.7 us (27%)
  matrix products  6.72 us (7%)
  other arithmetic  5.85 us (6%)
  local copies, waits for them, and re-layouts  1.31 us (1%)
    ppermute x11, waiting for transfers between devices, from_partner(): return lax.ppermute(block, axis, route)  40.4 us
    ppermute x11, starting transfers between devices, from_partner(): return lax.ppermute(block, axis, route)  21.4 us
    ppermute x4, waiting for transfers between devices, from_offset(): lax.ppermute(block, axis, [((i + delta) % count, i) for i in range(count)])  15.6 us
    ppermute x4, starting transfers between devices, from_offset(): lax.ppermute(block, axis, [((i + delta) % count, i) for i in range(count)])  5.34 us
  transfers between devices with their start and end apart: 15, of which 13 were waited for; matrix products, arithmetic and copies ran while one was open for 1% of the time, Pallas kernels for 0%

profile of v3, /device:TPU:2, one launch (start us, length us, event | category | flops | bytes accessed | tf_op | source)
XLA Modules:
  0.0 97.5 jit_solution(10439297384380625157)
XLA Ops:
  0.0 0.7 convert_element_type.149
  0.7 0.7 pad_maximum_fusion.12
  1.6 7.3 %collective-permute-start.5 = (f32[2,8,2048]{2,1,0:T(8,128)S(1)}, f32[2,8,2048]{2,1,0:T(8,128)S(1)}, u32[]{:S(2)}, u32[]{:S(2)}) collective-permute-start(f32[2,8,2048]{2,1,0:T(8,128)S(1)} %stack.49), channel_id=1, source_target_pairs={{0,128},{128,0},{32,160},{160,32},{64,192},{192,64},{96,224},{224,... | collective-permute-start | bytes 393224 | tf_op jit(solution)/shard_map/ppermute | solution.py:18
  9.2 1.7 %collective-permute-start.1 = (f32[2,33,64]{2,0,1:T(2,128)S(1)}, f32[2,33,64]{2,0,1:T(2,128)S(1)}, u32[]{:S(2)}, u32[]{:S(2)}) collective-permute-start(f32[2,33,64]{2,0,1:T(2,128)S(1)} %maximum_select_fusion.4), channel_id=1, source_target_pairs={{0,2},{2,0},{1,3},{3,1},{4,6},{6,4},{5,7},{7,5},{8,10},{10,8},{9,1... | collective-permute-start | bytes 50696 | tf_op jit(solution)/shard_map/ppermute | solution.py:18
  10.9 2.2 %collective-permute-done.1 = f32[2,33,64]{2,0,1:T(2,128)S(1)} collective-permute-done((f32[2,33,64]{2,0,1:T(2,128)S(1)}, f32[2,33,64]{2,0,1:T(2,128)S(1)}, u32[]{:S(2)}, u32[]{:S(2)}) %collective-permute-start.1) | collective-permute-done | bytes 16928 | tf_op jit(solution)/shard_map/ppermute | solution.py:18
  13.3 3.3 %collective-permute-start.2 = (f32[4,33,64]{2,0,1:T(4,128)S(1)}, f32[4,33,64]{2,0,1:T(4,128)S(1)}, u32[]{:S(2)}, u32[]{:S(2)}) collective-permute-start(f32[4,33,64]{2,0,1:T(4,128)S(1)} %maximum_select_fusion.3), channel_id=1, source_target_pairs={{0,4},{4,0},{1,5},{5,1},{2,6},{6,2},{3,7},{7,3},{8,12},{12,8},{9,1... | collective-permute-start | bytes 101384 | tf_op jit(solution)/shard_map/ppermute | solution.py:18
  16.7 2.4 %collective-permute-done.2 = f32[4,33,64]{2,0,1:T(4,128)S(1)} collective-permute-done((f32[4,33,64]{2,0,1:T(4,128)S(1)}, f32[4,33,64]{2,0,1:T(4,128)S(1)}, u32[]{:S(2)}, u32[]{:S(2)}) %collective-permute-start.2) | collective-permute-done | bytes 33824 | tf_op jit(solution)/shard_map/ppermute | solution.py:18
  19.2 0.6 collective-permute-start.3
  20.3 4.0 %collective-permute-done.3 = f32[8,33,64]{2,0,1:T(8,128)S(1)} collective-permute-done((f32[8,33,64]{2,0,1:T(8,128)S(1)}, f32[8,33,64]{2,0,1:T(8,128)S(1)}, u32[]{:S(2)}, u32[]{:S(2)}) %collective-permute-start.3) | collective-permute-done | bytes 67616 | tf_op jit(solution)/shard_map/ppermute | solution.py:18
  24.3 3.1 %collective-permute-start.4 = (f32[16,33,64]{2,0,1:T(8,128)S(1)}, f32[16,33,64]{2,0,1:T(8,128)S(1)}, u32[]{:S(2)}, u32[]{:S(2)}) collective-permute-start(f32[16,33,64]{2,0,1:T(8,128)S(1)} %maximum_select_fusion.1), channel_id=1, source_target_pairs={{0,16},{16,0},{1,17},{17,1},{2,18},{18,2},{3,19},{19,3},{4,20},{20... | collective-permute-start | bytes 405512 | tf_op jit(solution)/shard_map/ppermute | solution.py:18
  27.5 1.6 %collective-permute-start.6 = (f32[2,8,2048]{2,1,0:T(8,128)S(1)}, f32[2,8,2048]{2,1,0:T(8,128)S(1)}, u32[]{:S(2)}, u32[]{:S(2)}) collective-permute-start(f32[2,8,2048]{2,1,0:T(8,128)S(1)} %pad_maximum_fusion.7), channel_id=1, source_target_pairs={{0,64},{64,0},{32,96},{96,32},{128,192},{192,128},{160,224},{224,1... | collective-permute-start | bytes 393224 | tf_op jit(solution)/shard_map/ppermute | solution.py:18
  29.1 3.3 %collective-permute-done.4 = f32[16,33,64]{2,0,1:T(8,128)S(1)} collective-permute-done((f32[16,33,64]{2,0,1:T(8,128)S(1)}, f32[16,33,64]{2,0,1:T(8,128)S(1)}, u32[]{:S(2)}, u32[]{:S(2)}) %collective-permute-start.4) | collective-permute-done | bytes 135200 | tf_op jit(solution)/shard_map/ppermute | solution.py:18
  32.6 2.1 %collective-permute-done.6 = f32[2,8,2048]{2,1,0:T(8,128)S(1)} collective-permute-done((f32[2,8,2048]{2,1,0:T(8,128)S(1)}, f32[2,8,2048]{2,1,0:T(8,128)S(1)}, u32[]{:S(2)}, u32[]{:S(2)}) %collective-permute-start.6) | collective-permute-done | bytes 131104 | tf_op jit(solution)/shard_map/ppermute | solution.py:18
  34.7 1.0 %collective-permute-start.7 = (f32[2,8,2048]{2,1,0:T(8,128)S(1)}, f32[2,8,2048]{2,1,0:T(8,128)S(1)}, u32[]{:S(2)}, u32[]{:S(2)}) collective-permute-start(f32[2,8,2048]{2,1,0:T(8,128)S(1)} %pad_maximum_fusion.8), channel_id=1, source_target_pairs={{0,32},{32,0},{64,96},{96,64},{128,160},{160,128},{192,224},{224,1... | collective-permute-start | bytes 393224 | tf_op jit(solution)/shard_map/ppermute | solution.py:18
  35.8 4.0 %collective-permute-done.7 = f32[2,8,2048]{2,1,0:T(8,128)S(1)} collective-permute-done((f32[2,8,2048]{2,1,0:T(8,128)S(1)}, f32[2,8,2048]{2,1,0:T(8,128)S(1)}, u32[]{:S(2)}, u32[]{:S(2)}) %collective-permute-start.7) | collective-permute-done | bytes 131104 | tf_op jit(solution)/shard_map/ppermute | solution.py:18
  40.0 0.6 fusion.45
  40.6 0.6 fusion.39
  41.3 0.6 convolution_subtract_fusion.3
  44.0 3.8 %collective-permute-start.8 = (f32[2,32,8,64]{3,1,2,0:T(8,128)S(1)}, f32[2,32,8,64]{3,1,2,0:T(8,128)S(1)}, u32[]{:S(2)}, u32[]{:S(2)}) collective-permute-start(f32[2,32,8,64]{3,1,2,0:T(8,128)S(1)} %pad_maximum_fusion.6), channel_id=1, source_target_pairs={{1,0},{2,1},{3,2},{4,3},{5,4},{6,5},{7,6},{8,7},{9,8},{10,9},{11,1... | collective-permute-start | bytes 393224 | tf_op jit(solution)/shard_map/ppermute | solution.py:103
  47.9 1.1 %collective-permute-start.9 = (f32[2,32,8,64]{3,1,2,0:T(8,128)S(1)}, f32[2,32,8,64]{3,1,2,0:T(8,128)S(1)}, u32[]{:S(2)}, u32[]{:S(2)}) collective-permute-start(f32[2,32,8,64]{3,1,2,0:T(8,128)S(1)} %pad_maximum_fusion.6), channel_id=1, source_target_pairs={{2,0},{3,1},{4,2},{5,3},{6,4},{7,5},{8,6},{9,7},{10,8},{11,9},{12,... | collective-permute-start | bytes 393224 | tf_op jit(solution)/shard_map/ppermute | solution.py:103
  49.3 2.6 %collective-permute-done.11 = f32[2,32,8,64]{3,1,2,0:T(8,128)S(1)} collective-permute-done((f32[2,32,8,64]{3,1,2,0:T(8,128)S(1)}, f32[2,32,8,64]{3,1,2,0:T(8,128)S(1)}, u32[]{:S(2)}, u32[]{:S(2)}) %collective-permute-start.11) | collective-permute-done | bytes 131104 | tf_op jit(solution)/shard_map/ppermute | solution.py:103
  51.9 5.4 %collective-permute-done.8 = f32[2,32,8,64]{3,1,2,0:T(8,128)S(1)} collective-permute-done((f32[2,32,8,64]{3,1,2,0:T(8,128)S(1)}, f32[2,32,8,64]{3,1,2,0:T(8,128)S(1)}, u32[]{:S(2)}, u32[]{:S(2)}) %collective-permute-start.8) | collective-permute-done | bytes 131104 | tf_op jit(solution)/shard_map/ppermute | solution.py:103
  57.3 5.0 %collective-permute-done.9 = f32[2,32,8,64]{3,1,2,0:T(8,128)S(1)} collective-permute-done((f32[2,32,8,64]{3,1,2,0:T(8,128)S(1)}, f32[2,32,8,64]{3,1,2,0:T(8,128)S(1)}, u32[]{:S(2)}, u32[]{:S(2)}) %collective-permute-start.9) | collective-permute-done | bytes 131104 | tf_op jit(solution)/shard_map/ppermute | solution.py:103
  62.6 2.6 %collective-permute-done.10 = f32[2,32,8,64]{3,1,2,0:T(8,128)S(1)} collective-permute-done((f32[2,32,8,64]{3,1,2,0:T(8,128)S(1)}, f32[2,32,8,64]{3,1,2,0:T(8,128)S(1)}, u32[]{:S(2)}, u32[]{:S(2)}) %collective-permute-start.10) | collective-permute-done | bytes 131104 | tf_op jit(solution)/shard_map/ppermute | solution.py:103
  66.0 0.8 multiply_add_fusion.1
  66.9 0.9 multiply_subtract_fusion.1
  71.4 1.0 %collective-permute-start.12 = (f32[2,8,2048]{2,1,0:T(8,128)S(1)}, f32[2,8,2048]{2,1,0:T(8,128)S(1)}, u32[]{:S(2)}, u32[]{:S(2)}) collective-permute-start(f32[2,8,2048]{2,1,0:T(8,128)S(1)} %pad_maximum_fusion.9), channel_id=1, source_target_pairs={{0,32},{32,0},{64,96},{96,64},{128,160},{160,128},{192,224},{224,1... | collective-permute-start | bytes 393224 | tf_op jit(solution)/shard_map/ppermute | solution.py:18
  72.4 5.2 %collective-permute-done.12 = f32[2,8,2048]{2,1,0:T(8,128)S(1)} collective-permute-done((f32[2,8,2048]{2,1,0:T(8,128)S(1)}, f32[2,8,2048]{2,1,0:T(8,128)S(1)}, u32[]{:S(2)}, u32[]{:S(2)}) %collective-permute-start.12) | collective-permute-done | bytes 131104 | tf_op jit(solution)/shard_map/ppermute | solution.py:18
  77.7 1.6 %collective-permute-start.13 = (f32[2,8,2048]{2,1,0:T(8,128)S(1)}, f32[2,8,2048]{2,1,0:T(8,128)S(1)}, u32[]{:S(2)}, u32[]{:S(2)}) collective-permute-start(f32[2,8,2048]{2,1,0:T(8,128)S(1)} %pad_maximum_fusion.10), channel_id=1, source_target_pairs={{0,64},{64,0},{32,96},{96,32},{128,192},{192,128},{160,224},{224,1... | collective-permute-start | bytes 393224 | tf_op jit(solution)/shard_map/ppermute | solution.py:18
  79.2 8.5 %collective-permute-done.13 = f32[2,8,2048]{2,1,0:T(8,128)S(1)} collective-permute-done((f32[2,8,2048]{2,1,0:T(8,128)S(1)}, f32[2,8,2048]{2,1,0:T(8,128)S(1)}, u32[]{:S(2)}, u32[]{:S(2)}) %collective-permute-start.13) | collective-permute-done | bytes 131104 | tf_op jit(solution)/shard_map/ppermute | solution.py:18
  88.2 8.6 %collective-permute-done.14 = f32[2,8,2048]{2,1,0:T(8,128)S(1)} collective-permute-done((f32[2,8,2048]{2,1,0:T(8,128)S(1)}, f32[2,8,2048]{2,1,0:T(8,128)S(1)}, u32[]{:S(2)}, u32[]{:S(2)}) %collective-permute-start.14) | collective-permute-done | bytes 131104 | tf_op jit(solution)/shard_map/ppermute | solution.py:18
  96.8 0.7 select_multiply_fusion
  (64 shorter events, 8.8 us)
Async XLA Ops:
  0.0 1.5 %copy-start = (f32[8,2048]{1,0:T(8,128)S(1)}, f32[8,2048]{1,0:T(8,128)}, u32[]{:S(2)}) copy-start(f32[8,2048]{1,0:T(8,128)} %param.4) | copy-start | bytes 196612
  1.4 7.6 %collective-permute-start = (f32[1,33,64]{2,0,1:T(1,128)S(1)}, f32[1,33,64]{2,0,1:T(1,128)S(1)}, u32[]{:S(2)}, u32[]{:S(2)}) collective-permute-start(f32[1,33,64]{2,0,1:T(1,128)S(1)} %broadcast_in_dim.139), channel_id=1, source_target_pairs={{0,1},{1,0},{2,3},{3,2},{4,5},{5,4},{6,7},{7,6},{8,9},{9,8},{10,11... | collective-permute-start | bytes 25352 | tf_op jit(solution)/shard_map/ppermute | solution.py:18
  1.6 25.9 %collective-permute-start.5 = (f32[2,8,2048]{2,1,0:T(8,128)S(1)}, f32[2,8,2048]{2,1,0:T(8,128)S(1)}, u32[]{:S(2)}, u32[]{:S(2)}) collective-permute-start(f32[2,8,2048]{2,1,0:T(8,128)S(1)} %stack.49), channel_id=1, source_target_pairs={{0,128},{128,0},{32,160},{160,32},{64,192},{192,64},{96,224},{224,... | collective-permute-start | bytes 393224 | tf_op jit(solution)/shard_map/ppermute | solution.py:18
  9.2 4.0 %collective-permute-start.1 = (f32[2,33,64]{2,0,1:T(2,128)S(1)}, f32[2,33,64]{2,0,1:T(2,128)S(1)}, u32[]{:S(2)}, u32[]{:S(2)}) collective-permute-start(f32[2,33,64]{2,0,1:T(2,128)S(1)} %maximum_select_fusion.4), channel_id=1, source_target_pairs={{0,2},{2,0},{1,3},{3,1},{4,6},{6,4},{5,7},{7,5},{8,10},{10,8},{9,1... | collective-permute-start | bytes 50696 | tf_op jit(solution)/shard_map/ppermute | solution.py:18
  10.9 5.6 %copy-start.1 = (f32[2,16,256]{2,1,0:T(8,128)S(1)}, f32[2,16,256]{2,1,0:T(8,128)}, u32[]{:S(2)}) copy-start(f32[2,16,256]{2,1,0:T(8,128)} %param.5) | copy-start | bytes 98308
  13.3 5.9 %collective-permute-start.2 = (f32[4,33,64]{2,0,1:T(4,128)S(1)}, f32[4,33,64]{2,0,1:T(4,128)S(1)}, u32[]{:S(2)}, u32[]{:S(2)}) collective-permute-start(f32[4,33,64]{2,0,1:T(4,128)S(1)} %maximum_select_fusion.3), channel_id=1, source_target_pairs={{0,4},{4,0},{1,5},{5,1},{2,6},{6,2},{3,7},{7,3},{8,12},{12,8},{9,1... | collective-permute-start | bytes 101384 | tf_op jit(solution)/shard_map/ppermute | solution.py:18
  19.2 5.1 %collective-permute-start.3 = (f32[8,33,64]{2,0,1:T(8,128)S(1)}, f32[8,33,64]{2,0,1:T(8,128)S(1)}, u32[]{:S(2)}, u32[]{:S(2)}) collective-permute-start(f32[8,33,64]{2,0,1:T(8,128)S(1)} %maximum_select_fusion.2), channel_id=1, source_target_pairs={{0,8},{8,0},{1,9},{9,1},{2,10},{10,2},{3,11},{11,3},{4,12},{12,4},... | collective-permute-start | bytes 202760 | tf_op jit(solution)/shard_map/ppermute | solution.py:18
  24.3 8.1 %collective-permute-start.4 = (f32[16,33,64]{2,0,1:T(8,128)S(1)}, f32[16,33,64]{2,0,1:T(8,128)S(1)}, u32[]{:S(2)}, u32[]{:S(2)}) collective-permute-start(f32[16,33,64]{2,0,1:T(8,128)S(1)} %maximum_select_fusion.1), channel_id=1, source_target_pairs={{0,16},{16,0},{1,17},{17,1},{2,18},{18,2},{3,19},{19,3},{4,20},{20... | collective-permute-start | bytes 405512 | tf_op jit(solution)/shard_map/ppermute | solution.py:18
  27.5 7.2 %collective-permute-start.6 = (f32[2,8,2048]{2,1,0:T(8,128)S(1)}, f32[2,8,2048]{2,1,0:T(8,128)S(1)}, u32[]{:S(2)}, u32[]{:S(2)}) collective-permute-start(f32[2,8,2048]{2,1,0:T(8,128)S(1)} %pad_maximum_fusion.7), channel_id=1, source_target_pairs={{0,64},{64,0},{32,96},{96,32},{128,192},{192,128},{160,224},{224,1... | collective-permute-start | bytes 393224 | tf_op jit(solution)/shard_map/ppermute | solution.py:18
  34.7 5.1 %collective-permute-start.7 = (f32[2,8,2048]{2,1,0:T(8,128)S(1)}, f32[2,8,2048]{2,1,0:T(8,128)S(1)}, u32[]{:S(2)}, u32[]{:S(2)}) collective-permute-start(f32[2,8,2048]{2,1,0:T(8,128)S(1)} %pad_maximum_fusion.8), channel_id=1, source_target_pairs={{0,32},{32,0},{64,96},{96,64},{128,160},{160,128},{192,224},{224,1... | collective-permute-start | bytes 393224 | tf_op jit(solution)/shard_map/ppermute | solution.py:18
  43.9 8.0 %collective-permute-start.11 = (f32[2,32,8,64]{3,1,2,0:T(8,128)S(1)}, f32[2,32,8,64]{3,1,2,0:T(8,128)S(1)}, u32[]{:S(2)}, u32[]{:S(2)}) collective-permute-start(f32[2,32,8,64]{3,1,2,0:T(8,128)S(1)} %pad_maximum_fusion.6), channel_id=1, source_target_pairs={{31,0},{0,1},{1,2},{2,3},{3,4},{4,5},{5,6},{6,7},{7,8},{8,9},{9,10... | collective-permute-start | bytes 393224 | tf_op jit(solution)/shard_map/ppermute | solution.py:103
  44.0 13.3 %collective-permute-start.8 = (f32[2,32,8,64]{3,1,2,0:T(8,128)S(1)}, f32[2,32,8,64]{3,1,2,0:T(8,128)S(1)}, u32[]{:S(2)}, u32[]{:S(2)}) collective-permute-start(f32[2,32,8,64]{3,1,2,0:T(8,128)S(1)} %pad_maximum_fusion.6), channel_id=1, source_target_pairs={{1,0},{2,1},{3,2},{4,3},{5,4},{6,5},{7,6},{8,7},{9,8},{10,9},{11,1... | collective-permute-start | bytes 393224 | tf_op jit(solution)/shard_map/ppermute | solution.py:103
  47.9 14.5 %collective-permute-start.9 = (f32[2,32,8,64]{3,1,2,0:T(8,128)S(1)}, f32[2,32,8,64]{3,1,2,0:T(8,128)S(1)}, u32[]{:S(2)}, u32[]{:S(2)}) collective-permute-start(f32[2,32,8,64]{3,1,2,0:T(8,128)S(1)} %pad_maximum_fusion.6), channel_id=1, source_target_pairs={{2,0},{3,1},{4,2},{5,3},{6,4},{7,5},{8,6},{9,7},{10,8},{11,9},{12,... | collective-permute-start | bytes 393224 | tf_op jit(solution)/shard_map/ppermute | solution.py:103
  49.1 16.1 %collective-permute-start.10 = (f32[2,32,8,64]{3,1,2,0:T(8,128)S(1)}, f32[2,32,8,64]{3,1,2,0:T(8,128)S(1)}, u32[]{:S(2)}, u32[]{:S(2)}) collective-permute-start(f32[2,32,8,64]{3,1,2,0:T(8,128)S(1)} %pad_maximum_fusion.6), channel_id=1, source_target_pairs={{3,0},{4,1},{5,2},{6,3},{7,4},{8,5},{9,6},{10,7},{11,8},{12,9},{13... | collective-permute-start | bytes 393224 | tf_op jit(solution)/shard_map/ppermute | solution.py:103
  71.4 6.2 %collective-permute-start.12 = (f32[2,8,2048]{2,1,0:T(8,128)S(1)}, f32[2,8,2048]{2,1,0:T(8,128)S(1)}, u32[]{:S(2)}, u32[]{:S(2)}) collective-permute-start(f32[2,8,2048]{2,1,0:T(8,128)S(1)} %pad_maximum_fusion.9), channel_id=1, source_target_pairs={{0,32},{32,0},{64,96},{96,64},{128,160},{160,128},{192,224},{224,1... | collective-permute-start | bytes 393224 | tf_op jit(solution)/shard_map/ppermute | solution.py:18
  77.7 10.1 %collective-permute-start.13 = (f32[2,8,2048]{2,1,0:T(8,128)S(1)}, f32[2,8,2048]{2,1,0:T(8,128)S(1)}, u32[]{:S(2)}, u32[]{:S(2)}) collective-permute-start(f32[2,8,2048]{2,1,0:T(8,128)S(1)} %pad_maximum_fusion.10), channel_id=1, source_target_pairs={{0,64},{64,0},{32,96},{96,32},{128,192},{192,128},{160,224},{224,1... | collective-permute-start | bytes 393224 | tf_op jit(solution)/shard_map/ppermute | solution.py:18
  87.8 9.0 %collective-permute-start.14 = (f32[2,8,2048]{2,1,0:T(8,128)S(1)}, f32[2,8,2048]{2,1,0:T(8,128)S(1)}, u32[]{:S(2)}, u32[]{:S(2)}) collective-permute-start(f32[2,8,2048]{2,1,0:T(8,128)S(1)} %pad_maximum_fusion.11), channel_id=1, source_target_pairs={{0,128},{128,0},{32,160},{160,32},{64,192},{192,64},{96,224},{224,... | collective-permute-start | bytes 393224 | tf_op jit(solution)/shard_map/ppermute | solution.py:18

commit v4 on v3

--- a/solution.py
+++ b/solution.py
@@ -3,6 +3,8 @@
 import jax
 import jax.numpy as jnp
 from jax import lax
+from jax.experimental import pallas as pl
+from jax.experimental.pallas import tpu as pltpu
 from jax.sharding import PartitionSpec as P
 
 PRECISE = lax.Precision.HIGHEST
@@ -96,6 +98,125 @@
     cosine, sine_part = twiddle(sample_pos * phase_bin % total_len, total_len)
     sine_part = -sine_part
     return (real_part * cosine - imag_part * sine_part, real_part * sine_part + imag_part * cosine)
+
+
+LANES = 128
+
+
+def cdot(left_real, left_imag, right_real, right_imag):
+    def dot(a, b):
+        return jnp.dot(a, b, precision=PRECISE, preferred_element_type=jnp.float32)
+
+    return (
+        dot(left_real, right_real) - dot(left_imag, right_imag),
+        dot(left_real, right_imag) + dot(left_imag, right_real),
+    )
+
+
+def forward_kernel(xr_ref, xi_ref, twr_ref, twi_ref, kr_ref, ki_ref, t2r_ref, t2i_ref, wr_ref, wi_ref, yr_ref, yi_ref):
+    own, outer, inner = xr_ref.shape
+    xr = xr_ref[...]
+    xi = xi_ref[...]
+    twr = twr_ref[...][None]
+    twi = twi_ref[...][None]
+    ur = (xr * twr - xi * twi).reshape(own * outer, inner)
+    ui = (xr * twi + xi * twr).reshape(own * outer, inner)
+    zr, zi = cdot(kr_ref[...], ki_ref[...], ur, ui)
+    t2r = t2r_ref[...]
+    t2i = t2i_ref[...]
+    zr, zi = (zr * t2r - zi * t2i, zr * t2i + zi * t2r)
+    yr, yi = cdot(zr, zi, wr_ref[...], wi_ref[...])
+    yr_ref[...] = yr.reshape(own, outer, inner)
+    yi_ref[...] = yi.reshape(own, outer, inner)
+
+
+def inverse_kernel(win_ref, shift_ref, resp_ref, band_ref, twr_ref, twi_ref, kr_ref, ki_ref, t2r_ref, t2i_ref, wr_ref, wi_ref, xr_ref, xi_ref):
+    own, outer, inner = xr_ref.shape
+    band_width = resp_ref.shape[1]
+    half_width = band_width // 2
+    span = own + band_width - 1
+    shift = shift_ref[...]
+    masks = [shift == amount for amount in range(-half_width, half_width + 1)]
+    moved = []
+    for row in range(span):
+        mr = jnp.zeros((outer, inner), jnp.float32)
+        mi = jnp.zeros((outer, inner), jnp.float32)
+        for index, amount in enumerate(range(-half_width, half_width + 1)):
+            source = own + amount + row
+            mr = jnp.where(masks[index], win_ref[0, source], mr)
+            mi = jnp.where(masks[index], win_ref[1, source], mi)
+        moved.append((mr, mi))
+    rows_real = []
+    rows_imag = []
+    for channel in range(own):
+        acc_r = jnp.zeros((outer, inner), jnp.float32)
+        acc_i = jnp.zeros((outer, inner), jnp.float32)
+        for lag in range(band_width):
+            br = band_ref[lag * own + channel]
+            bi = band_ref[(band_width + lag) * own + channel]
+            rr = resp_ref[0, lag]
+            ri = resp_ref[1, lag]
+            cr = br * rr - bi * ri
+            ci = br * ri + bi * rr
+            vr, vi = moved[channel + lag]
+            acc_r = acc_r + cr * vr - ci * vi
+            acc_i = acc_i + cr * vi + ci * vr
+        rows_real.append(acc_r)
+        rows_imag.append(acc_i)
+    mr = jnp.concatenate(rows_real, axis=0)
+    mi = jnp.concatenate(rows_imag, axis=0)
+    yr, yi = cdot(mr, mi, wr_ref[...], -wi_ref[...])
+    t2r = t2r_ref[...]
+    t2i = -t2i_ref[...]
+    yr, yi = (yr * t2r - yi * t2i, yr * t2i + yi * t2r)
+    xr, xi = cdot(kr_ref[...], -ki_ref[...], yr, yi)
+    xr = xr.reshape(own, outer, inner)
+    xi = xi.reshape(own, outer, inner)
+    twr = twr_ref[...][None]
+    twi = -twi_ref[...][None]
+    xr_ref[...] = xr * twr - xi * twi
+    xi_ref[...] = xr * twi + xi * twr
+
+
+def local_tables(own, outer, inner, phase_bin, total_len):
+    length = outer * inner
+    rows = lax.iota(jnp.int32, outer)[:, None]
+    cols = lax.iota(jnp.int32, inner)[None, :]
+    twr, twi = twiddle((rows * inner + cols) * phase_bin % total_len, total_len)
+    small_r, small_i = dft_table(outer)
+    eye = jnp.eye(own, dtype=jnp.float32)
+    kr = jnp.kron(eye, small_r)
+    ki = jnp.kron(eye, small_i)
+    t2r, t2i = twiddle(rows * cols % length, length)
+    t2r = jnp.tile(t2r, (own, 1))
+    t2i = jnp.tile(t2i, (own, 1))
+    wr, wi = dft_table(inner)
+    return (twr, twi, kr, ki, t2r, t2i, wr, wi)
+
+
+def vmem_specs(count):
+    return [pl.BlockSpec(memory_space=pltpu.VMEM)] * count
+
+
+def forward_call(xr, xi, tables):
+    shape = jax.ShapeDtypeStruct(xr.shape, jnp.float32)
+    return pl.pallas_call(
+        forward_kernel,
+        out_shape=(shape, shape),
+        in_specs=vmem_specs(2 + len(tables)),
+        out_specs=tuple(vmem_specs(2)),
+    )(xr, xi, *tables)
+
+
+def inverse_call(window, shift, responses, band_flat, tables, own):
+    shape = jax.ShapeDtypeStruct((own,) + window.shape[2:], jnp.float32)
+    specs = vmem_specs(3) + [pl.BlockSpec(memory_space=pltpu.SMEM)] + vmem_specs(len(tables))
+    return pl.pallas_call(
+        inverse_kernel,
+        out_shape=(shape, shape),
+        in_specs=specs,
+        out_specs=tuple(vmem_specs(2)),
+    )(window, shift, responses, band_flat, *tables)
 
 
 def from_offset(block, axis, delta):
@@ -113,39 +234,6 @@
         block = jnp.where(upper, jnp.concatenate([partner, block]), jnp.concatenate([block, partner]))
         stride *= 2
     return block
-
-
-def mix_halo(window, band_rows, table, halo_below, channel_all):
-    _, outer_len, _, inner_len = window.shape
-    band_width = band_rows.shape[1]
-    half_width = band_width // 2
-    own = band_rows.shape[2]
-    span = own + band_width - 1
-    if table.shape[0] != outer_len:
-        rows = table.shape[1]
-        table = table.transpose(1, 0, 2).reshape(rows, outer_len, inner_len).transpose(1, 0, 2)
-    responses = table[:, : 2 * band_width].reshape(outer_len, 2, band_width, inner_len)
-    shift = table[:, 2 * band_width].astype(jnp.int32)
-    centered = (shift + half_width) % channel_all - half_width
-    moved = jnp.zeros(window.shape[:2] + (span, inner_len), window.dtype)
-    for shift_amount in range(-half_width, half_width + 1):
-        lo = halo_below + shift_amount
-        piece = window[:, :, lo : lo + span]
-        moved = jnp.where((centered == shift_amount)[None, :, None, :], piece, moved)
-    acc_real = jnp.zeros((outer_len, own, inner_len), window.dtype)
-    acc_imag = jnp.zeros((outer_len, own, inner_len), window.dtype)
-    for lag_index in range(band_width):
-        value_real = moved[0, :, lag_index : lag_index + own]
-        value_imag = moved[1, :, lag_index : lag_index + own]
-        gain_real = band_rows[0, lag_index][None, :, None]
-        gain_imag = band_rows[1, lag_index][None, :, None]
-        resp_real = responses[:, 0, lag_index][:, None, :]
-        resp_imag = responses[:, 1, lag_index][:, None, :]
-        coef_real = gain_real * resp_real - gain_imag * resp_imag
-        coef_imag = gain_real * resp_imag + gain_imag * resp_real
-        acc_real = acc_real + coef_real * value_real - coef_imag * value_imag
-        acc_imag = acc_imag + coef_real * value_imag + coef_imag * value_real
-    return (acc_real, acc_imag)
 
 
 def per_device(signal, band, response, offsets):
@@ -172,20 +260,32 @@
             upper_half, diff_real * sine_part + diff_imag * cosine, imag_part + partner[1]
         )
         real_part, imag_part = (new_real, new_imag)
-    spec_real, spec_imag = forward_local(real_part, imag_part, phase_bin, total_len, inner_len)
+    inner = LANES
+    outer = length // inner
     own = channel_count
     band_width = band.shape[1]
+    half_width = band_width // 2
+    channel_all = band.shape[2]
+    tables = local_tables(own, outer, inner, phase_bin, total_len)
+    spec_real, spec_imag = forward_call(
+        real_part.reshape(own, outer, inner), imag_part.reshape(own, outer, inner), tables
+    )
     chan_pos = lax.axis_index("chan")
     band_rows = lax.dynamic_slice_in_dim(band, chan_pos * own, own, axis=2)
     packed = jnp.concatenate(
         [response.reshape(2 * band_width, -1), offsets.reshape(1, -1).astype(jnp.float32)], axis=0
     )
     table = gather_doubling(packed[None], "chan")
+    entries = table.shape[1]
+    table = table.transpose(1, 0, 2).reshape(entries, inner, outer).transpose(0, 2, 1)
+    responses = table[: 2 * band_width].reshape(2, band_width, outer, inner)
+    shift = (table[2 * band_width].astype(jnp.int32) + half_width) % channel_all - half_width
     spectra = jnp.stack([spec_real, spec_imag])
     neighbours = [from_offset(spectra, "chan", delta) for delta in (-1, 1, 2, 3)]
-    window = jnp.concatenate([neighbours[0], spectra] + neighbours[1:], axis=2)
-    mixed_real, mixed_imag = mix_halo(window, band_rows, table, own, band.shape[2])
-    real_part, imag_part = inverse_local(mixed_real, mixed_imag, phase_bin, total_len)
+    window = jnp.concatenate([neighbours[0], spectra] + neighbours[1:], axis=1)
+    real_part, imag_part = inverse_call(window, shift, responses, band_rows.reshape(-1), tables, own)
+    real_part = real_part.reshape(own, length)
+    imag_part = imag_part.reshape(own, length)
     for bit_index in range(levels):
         half_span = 1 << bit_index
         partner = from_partner(jnp.stack([real_part, imag_part]), "tm", bit_index)

time: 97.7 us -> 92.2 us (0.944)
  the two profiles are of different devices: /device:TPU:2 before, /device:TPU:30 now
where the time goes in v4:
time: 92.2 us; the launch traced here: 91.8 us
  waiting for transfers between devices  52.5 us (57%)
  starting transfers between devices  18.5 us (20%)
  local copies, waits for them, and re-layouts  8.73 us (9%)
  Pallas kernels  5.91 us (6%)
  other arithmetic  5.44 us (6%)
    ppermute x11, waiting for transfers between devices, from_partner(): return lax.ppermute(block, axis, route)  41.1 us
    ppermute x11, starting transfers between devices, from_partner(): return lax.ppermute(block, axis, route)  15.8 us
    ppermute x4, waiting for transfers between devices, from_offset(): lax.ppermute(block, axis, [((i + delta) % count, i) for i in range(count)])  11.4 us
    pallas_call x1, Pallas kernels, inverse_call(): pl.pallas_call(inverse_kernel, out_shape=(shape, shape), in_specs=specs,...  3.44 us
    ppermute x4, starting transfers between devices, from_offset(): lax.ppermute(block, axis, [((i + delta) % count, i) for i in range(count)])  2.77 us
    pallas_call x1, Pallas kernels, forward_call(): pl.pallas_call(forward_kernel, out_shape=(shape, shape), in_specs=vmem_sp...  2.46 us
    unnamed x19, local copies, waits for them, and re-layouts  2.13 us
  transfers between devices with their start and end apart: 15, of which 11 were waited for; matrix products, arithmetic and copies ran while one was open for 7% of the time, Pallas kernels for 0%

profile of v4, /device:TPU:30, one launch (start us, length us, event | category | flops | bytes accessed | tf_op | source)
XLA Modules:
  0.0 91.8 jit_solution(18171293512638449175)
XLA Ops:
  2.2 7.3 %collective-permute-start = (f32[2,8,2048]{2,1,0:T(8,128)S(1)}, f32[2,8,2048]{2,1,0:T(8,128)S(1)}, u32[]{:S(2)}, u32[]{:S(2)}) collective-permute-start(f32[2,8,2048]{2,1,0:T(8,128)S(1)} %stack.47), channel_id=1, source_target_pairs={{0,128},{128,0},{32,160},{160,32},{64,192},{192,64},{96,224},{224,... | collective-permute-start | bytes 393224 | tf_op jit(solution)/shard_map/ppermute | solution.py:20
  9.6 0.7 fusion.35
  10.5 0.9 %fusion.14 = (f32[128,128]{1,0:T(8,128)}, f32[128,128]{1,0:T(8,128)}) fusion(), kind=kLoop, calls=%fused_computation.64 | loop fusion | flops 229376 | bytes 131072 | tf_op jit(solution)/shard_map/sin | solution.py:25
  11.5 0.8 collective-permute-start.8
  12.4 3.4 %collective-permute-done.8 = f32[2,33,64]{1,2,0:T(8,128)S(1)} collective-permute-done((f32[2,33,64]{1,2,0:T(8,128)S(1)}, f32[2,33,64]{1,2,0:T(8,128)S(1)}, u32[]{:S(2)}, u32[]{:S(2)}) %collective-permute-start.8) | collective-permute-done | bytes 16928 | tf_op jit(solution)/shard_map/ppermute | solution.py:20
  15.8 1.3 %collective-permute-start.9 = (f32[4,33,64]{1,2,0:T(8,128)S(1)}, f32[4,33,64]{1,2,0:T(8,128)S(1)}, u32[]{:S(2)}, u32[]{:S(2)}) collective-permute-start(f32[4,33,64]{1,2,0:T(8,128)S(1)} %maximum_select_fusion.3), channel_id=1, source_target_pairs={{0,4},{4,0},{1,5},{5,1},{2,6},{6,2},{3,7},{7,3},{8,12},{12,8},{9,1... | collective-permute-start | bytes 101384 | tf_op jit(solution)/shard_map/ppermute | solution.py:20
  17.4 5.0 %collective-permute-done.9 = f32[4,33,64]{1,2,0:T(8,128)S(1)} collective-permute-done((f32[4,33,64]{1,2,0:T(8,128)S(1)}, f32[4,33,64]{1,2,0:T(8,128)S(1)}, u32[]{:S(2)}, u32[]{:S(2)}) %collective-permute-start.9) | collective-permute-done | bytes 33824 | tf_op jit(solution)/shard_map/ppermute | solution.py:20
  22.4 0.9 collective-permute-start.10
  23.4 1.6 %collective-permute-start.1 = (f32[2,8,2048]{2,1,0:T(8,128)S(1)}, f32[2,8,2048]{2,1,0:T(8,128)S(1)}, u32[]{:S(2)}, u32[]{:S(2)}) collective-permute-start(f32[2,8,2048]{2,1,0:T(8,128)S(1)} %pad_maximum_fusion), channel_id=1, source_target_pairs={{0,64},{64,0},{32,96},{96,32},{128,192},{192,128},{160,224},{224,1... | collective-permute-start | bytes 393224 | tf_op jit(solution)/shard_map/ppermute | solution.py:20
  25.2 0.8 mul.407.kr_ref
  26.1 0.8 mul.410.ki_ref
  27.5 3.0 %collective-permute-done.10 = f32[8,33,64]{1,2,0:T(8,128)S(1)} collective-permute-done((f32[8,33,64]{1,2,0:T(8,128)S(1)}, f32[8,33,64]{1,2,0:T(8,128)S(1)}, u32[]{:S(2)}, u32[]{:S(2)}) %collective-permute-start.10) | collective-permute-done | bytes 67616 | tf_op jit(solution)/shard_map/ppermute | solution.py:20
  30.9 0.8 collective-permute-start.2
  31.7 9.6 %collective-permute-done.11 = f32[16,33,64]{1,2,0:T(8,128)S(1)} collective-permute-done((f32[16,33,64]{1,2,0:T(8,128)S(1)}, f32[16,33,64]{1,2,0:T(8,128)S(1)}, u32[]{:S(2)}, u32[]{:S(2)}) %collective-permute-start.11) | collective-permute-done | bytes 135200 | tf_op jit(solution)/shard_map/ppermute | solution.py:20
  42.0 0.7 slice.74
  42.8 0.7 copy_bitcast_fusion
  44.7 2.5 %shard_map.46 = (f32[8,16,128]{2,1,0:T(8,128)}, f32[8,16,128]{2,1,0:T(8,128)}) custom-call(f32[8,16,128]{2,1,0:T(8,128)} %get-tuple-element.28.xr_ref, f32[8,16,128]{2,1,0:T(8,128)} %get-tuple-element.27.xi_ref, f32[16,128]{1,0:T(8,128)} %get-tuple-element.26.twr_ref, f32[16,128]{1,0:T(8,128)} %get-tuple-element.25.twi_ref, f32[128,128]{1,0:T(8,128)} %mul.407.kr_ref, ...), custom_call_target="tpu_custom_call" | custom-call | tf_op jit(solution)/shard_map/pallas_call | solution.py:203
  47.2 0.9 pad_maximum_fusion.2
  48.8 1.7 %collective-permute-start.4 = (f32[2,8,16,128]{3,2,1,0:T(8,128)S(1)}, f32[2,8,16,128]{3,2,1,0:T(8,128)S(1)}, u32[]{:S(2)}, u32[]{:S(2)}) collective-permute-start(f32[2,8,16,128]{3,2,1,0:T(8,128)S(1)} %pad_maximum_fusion.2), channel_id=1, source_target_pairs={{1,0},{2,1},{3,2},{4,3},{5,4},{6,5},{7,6},{8,7},{9,8},{10,9},{11,1... | collective-permute-start | bytes 393224 | tf_op jit(solution)/shard_map/ppermute | solution.py:224
  50.5 0.7 collective-permute-start.5
  51.5 1.1 %collective-permute-done.3 = f32[2,8,16,128]{3,2,1,0:T(8,128)S(1)} collective-permute-done((f32[2,8,16,128]{3,2,1,0:T(8,128)S(1)}, f32[2,8,16,128]{3,2,1,0:T(8,128)S(1)}, u32[]{:S(2)}, u32[]{:S(2)}) %collective-permute-start.3) | collective-permute-done | bytes 131104 | tf_op jit(solution)/shard_map/ppermute | solution.py:224
  52.6 1.8 %collective-permute-done.4 = f32[2,8,16,128]{3,2,1,0:T(8,128)S(1)} collective-permute-done((f32[2,8,16,128]{3,2,1,0:T(8,128)S(1)}, f32[2,8,16,128]{3,2,1,0:T(8,128)S(1)}, u32[]{:S(2)}, u32[]{:S(2)}) %collective-permute-start.4) | collective-permute-done | bytes 131104 | tf_op jit(solution)/shard_map/ppermute | solution.py:224
  54.4 8.5 %collective-permute-done.5 = f32[2,8,16,128]{3,2,1,0:T(8,128)S(1)} collective-permute-done((f32[2,8,16,128]{3,2,1,0:T(8,128)S(1)}, f32[2,8,16,128]{3,2,1,0:T(8,128)S(1)}, u32[]{:S(2)}, u32[]{:S(2)}) %collective-permute-start.5) | collective-permute-done | bytes 131104 | tf_op jit(solution)/shard_map/ppermute | solution.py:224
  62.9 0.8 copy-done.1
  63.8 3.4 %shard_map.47 = (f32[8,16,128]{2,1,0:T(8,128)}, f32[8,16,128]{2,1,0:T(8,128)}) custom-call(f32[2,40,16,128]{3,2,1,0:T(8,128)} %copy-done.1, s32[16,128]{1,0:T(8,128)} %fusion.26.shift_ref, f32[2,16,16,128]{3,2,1,0:T(8,128)} %bitcast.152, f32[256]{0:T(256)} %reshape.140.band_ref, f32[16,128]{1,0:T(8,128)} %get-tuple-element.26.twr_ref, ...), custom_call_target="tpu_custom_call" | custom-call | tf_op jit(solution)/shard_map/pallas_call | solution.py:214
  67.2 0.9 stack_reshape.6
  68.2 1.1 %collective-permute-start.12 = (f32[2,8,2048]{2,1,0:T(8,128)S(1)}, f32[2,8,2048]{2,1,0:T(8,128)S(1)}, u32[]{:S(2)}, u32[]{:S(2)}) collective-permute-start(f32[2,8,2048]{2,1,0:T(8,128)S(1)} %pad_maximum_fusion.3), channel_id=1, source_target_pairs={{0,32},{32,0},{64,96},{96,64},{128,160},{160,128},{192,224},{224,1... | collective-permute-start | bytes 393224 | tf_op jit(solution)/shard_map/ppermute | solution.py:20
  69.3 3.9 %collective-permute-done.12 = f32[2,8,2048]{2,1,0:T(8,128)S(1)} collective-permute-done((f32[2,8,2048]{2,1,0:T(8,128)S(1)}, f32[2,8,2048]{2,1,0:T(8,128)S(1)}, u32[]{:S(2)}, u32[]{:S(2)}) %collective-permute-start.12) | collective-permute-done | bytes 131104 | tf_op jit(solution)/shard_map/ppermute | solution.py:20
  73.3 1.7 %collective-permute-start.13 = (f32[2,8,2048]{2,1,0:T(8,128)S(1)}, f32[2,8,2048]{2,1,0:T(8,128)S(1)}, u32[]{:S(2)}, u32[]{:S(2)}) collective-permute-start(f32[2,8,2048]{2,1,0:T(8,128)S(1)} %pad_maximum_fusion.4), channel_id=1, source_target_pairs={{0,64},{64,0},{32,96},{96,32},{128,192},{192,128},{160,224},{224,1... | collective-permute-start | bytes 393224 | tf_op jit(solution)/shard_map/ppermute | solution.py:20
  75.0 7.1 %collective-permute-done.13 = f32[2,8,2048]{2,1,0:T(8,128)S(1)} collective-permute-done((f32[2,8,2048]{2,1,0:T(8,128)S(1)}, f32[2,8,2048]{2,1,0:T(8,128)S(1)}, u32[]{:S(2)}, u32[]{:S(2)}) %collective-permute-start.13) | collective-permute-done | bytes 131104 | tf_op jit(solution)/shard_map/ppermute | solution.py:20
  82.2 8.9 %collective-permute-done.14 = f32[2,8,2048]{2,1,0:T(8,128)S(1)} collective-permute-done((f32[2,8,2048]{2,1,0:T(8,128)S(1)}, f32[2,8,2048]{2,1,0:T(8,128)S(1)}, u32[]{:S(2)}, u32[]{:S(2)}) %collective-permute-start.14) | collective-permute-done | bytes 131104 | tf_op jit(solution)/shard_map/ppermute | solution.py:20
  91.1 0.7 select_multiply_fusion
  (63 shorter events, 6.8 us)
Async XLA Ops:
  0.0 12.3 %copy-start = (f32[2,16,256]{2,1,0:T(8,128)S(1)}, f32[2,16,256]{2,1,0:T(8,128)}, u32[]{:S(2)}) copy-start(f32[2,16,256]{2,1,0:T(8,128)} %param.5) | copy-start | bytes 98308
  0.7 0.7 copy-start.7
  1.4 0.8 copy-start.2
  1.5 9.9 %collective-permute-start.7 = (f32[1,33,64]{1,2,0:T(8,128)S(1)}, f32[1,33,64]{1,2,0:T(8,128)S(1)}, u32[]{:S(2)}, u32[]{:S(2)}) collective-permute-start(f32[1,33,64]{1,2,0:T(8,128)S(1)} %maximum_bitcast_fusion), channel_id=1, source_target_pairs={{0,1},{1,0},{2,3},{3,2},{4,5},{5,4},{6,7},{7,6},{8,9},{9,8},{10,11... | collective-permute-start | bytes 25352 | tf_op jit(solution)/shard_map/ppermute | solution.py:20
  2.2 21.1 %collective-permute-start = (f32[2,8,2048]{2,1,0:T(8,128)S(1)}, f32[2,8,2048]{2,1,0:T(8,128)S(1)}, u32[]{:S(2)}, u32[]{:S(2)}) collective-permute-start(f32[2,8,2048]{2,1,0:T(8,128)S(1)} %stack.47), channel_id=1, source_target_pairs={{0,128},{128,0},{32,160},{160,32},{64,192},{192,64},{96,224},{224,... | collective-permute-start | bytes 393224 | tf_op jit(solution)/shard_map/ppermute | solution.py:20
  11.5 4.4 %collective-permute-start.8 = (f32[2,33,64]{1,2,0:T(8,128)S(1)}, f32[2,33,64]{1,2,0:T(8,128)S(1)}, u32[]{:S(2)}, u32[]{:S(2)}) collective-permute-start(f32[2,33,64]{1,2,0:T(8,128)S(1)} %maximum_select_fusion.4), channel_id=1, source_target_pairs={{0,2},{2,0},{1,3},{3,1},{4,6},{6,4},{5,7},{7,5},{8,10},{10,8},{9,1... | collective-permute-start | bytes 50696 | tf_op jit(solution)/shard_map/ppermute | solution.py:20
  15.8 6.6 %collective-permute-start.9 = (f32[4,33,64]{1,2,0:T(8,128)S(1)}, f32[4,33,64]{1,2,0:T(8,128)S(1)}, u32[]{:S(2)}, u32[]{:S(2)}) collective-permute-start(f32[4,33,64]{1,2,0:T(8,128)S(1)} %maximum_select_fusion.3), channel_id=1, source_target_pairs={{0,4},{4,0},{1,5},{5,1},{2,6},{6,2},{3,7},{7,3},{8,12},{12,8},{9,1... | collective-permute-start | bytes 101384 | tf_op jit(solution)/shard_map/ppermute | solution.py:20
  22.4 8.1 %collective-permute-start.10 = (f32[8,33,64]{1,2,0:T(8,128)S(1)}, f32[8,33,64]{1,2,0:T(8,128)S(1)}, u32[]{:S(2)}, u32[]{:S(2)}) collective-permute-start(f32[8,33,64]{1,2,0:T(8,128)S(1)} %maximum_select_fusion.2), channel_id=1, source_target_pairs={{0,8},{8,0},{1,9},{9,1},{2,10},{10,2},{3,11},{11,3},{4,12},{12,4},... | collective-permute-start | bytes 202760 | tf_op jit(solution)/shard_map/ppermute | solution.py:20
  23.4 7.5 %collective-permute-start.1 = (f32[2,8,2048]{2,1,0:T(8,128)S(1)}, f32[2,8,2048]{2,1,0:T(8,128)S(1)}, u32[]{:S(2)}, u32[]{:S(2)}) collective-permute-start(f32[2,8,2048]{2,1,0:T(8,128)S(1)} %pad_maximum_fusion), channel_id=1, source_target_pairs={{0,64},{64,0},{32,96},{96,32},{128,192},{192,128},{160,224},{224,1... | collective-permute-start | bytes 393224 | tf_op jit(solution)/shard_map/ppermute | solution.py:20
  30.6 10.8 %collective-permute-start.11 = (f32[16,33,64]{1,2,0:T(8,128)S(1)}, f32[16,33,64]{1,2,0:T(8,128)S(1)}, u32[]{:S(2)}, u32[]{:S(2)}) collective-permute-start(f32[16,33,64]{1,2,0:T(8,128)S(1)} %maximum_select_fusion.1), channel_id=1, source_target_pairs={{0,16},{16,0},{1,17},{17,1},{2,18},{18,2},{3,19},{19,3},{4,20},{20... | collective-permute-start | bytes 405512 | tf_op jit(solution)/shard_map/ppermute | solution.py:20
  30.9 11.8 %collective-permute-start.2 = (f32[2,8,2048]{2,1,0:T(8,128)S(1)}, f32[2,8,2048]{2,1,0:T(8,128)S(1)}, u32[]{:S(2)}, u32[]{:S(2)}) collective-permute-start(f32[2,8,2048]{2,1,0:T(8,128)S(1)} %pad_maximum_fusion.1), channel_id=1, source_target_pairs={{0,32},{32,0},{64,96},{96,64},{128,160},{160,128},{192,224},{224,1... | collective-permute-start | bytes 393224 | tf_op jit(solution)/shard_map/ppermute | solution.py:20
  48.1 4.5 %collective-permute-start.3 = (f32[2,8,16,128]{3,2,1,0:T(8,128)S(1)}, f32[2,8,16,128]{3,2,1,0:T(8,128)S(1)}, u32[]{:S(2)}, u32[]{:S(2)}) collective-permute-start(f32[2,8,16,128]{3,2,1,0:T(8,128)S(1)} %pad_maximum_fusion.2), channel_id=1, source_target_pairs={{31,0},{0,1},{1,2},{2,3},{3,4},{4,5},{5,6},{6,7},{7,8},{8,9},{9,10... | collective-permute-start | bytes 393224 | tf_op jit(solution)/shard_map/ppermute | solution.py:224
  48.8 3.8 %copy-start.3 = (f32[8,16,128]{2,1,0:T(8,128)S(1)}, f32[8,16,128]{2,1,0:T(8,128)}, u32[]{:S(2)}) copy-start(f32[8,16,128]{2,1,0:T(8,128)} %get-tuple-element.9) | copy-start | bytes 196612
  48.8 3.8 %copy-start.4 = (f32[8,16,128]{2,1,0:T(8,128)S(1)}, f32[8,16,128]{2,1,0:T(8,128)}, u32[]{:S(2)}) copy-start(f32[8,16,128]{2,1,0:T(8,128)} %get-tuple-element.10) | copy-start | bytes 196612
  48.8 5.6 %collective-permute-start.4 = (f32[2,8,16,128]{3,2,1,0:T(8,128)S(1)}, f32[2,8,16,128]{3,2,1,0:T(8,128)S(1)}, u32[]{:S(2)}, u32[]{:S(2)}) collective-permute-start(f32[2,8,16,128]{3,2,1,0:T(8,128)S(1)} %pad_maximum_fusion.2), channel_id=1, source_target_pairs={{1,0},{2,1},{3,2},{4,3},{5,4},{6,5},{7,6},{8,7},{9,8},{10,9},{11,1... | collective-permute-start | bytes 393224 | tf_op jit(solution)/shard_map/ppermute | solution.py:224
  50.5 12.4 %collective-permute-start.5 = (f32[2,8,16,128]{3,2,1,0:T(8,128)S(1)}, f32[2,8,16,128]{3,2,1,0:T(8,128)S(1)}, u32[]{:S(2)}, u32[]{:S(2)}) collective-permute-start(f32[2,8,16,128]{3,2,1,0:T(8,128)S(1)} %pad_maximum_fusion.2), channel_id=1, source_target_pairs={{2,0},{3,1},{4,2},{5,3},{6,4},{7,5},{8,6},{9,7},{10,8},{11,9},{12,... | collective-permute-start | bytes 393224 | tf_op jit(solution)/shard_map/ppermute | solution.py:224
  51.2 11.7 %collective-permute-start.6 = (f32[2,8,16,128]{3,2,1,0:T(8,128)S(1)}, f32[2,8,16,128]{3,2,1,0:T(8,128)S(1)}, u32[]{:S(2)}, u32[]{:S(2)}) collective-permute-start(f32[2,8,16,128]{3,2,1,0:T(8,128)S(1)} %pad_maximum_fusion.2), channel_id=1, source_target_pairs={{3,0},{4,1},{5,2},{6,3},{7,4},{8,5},{9,6},{10,7},{11,8},{12,9},{13... | collective-permute-start | bytes 393224 | tf_op jit(solution)/shard_map/ppermute | solution.py:224
  62.9 0.8 copy-start.1
  67.2 0.9 copy-start.6
  68.2 5.1 %collective-permute-start.12 = (f32[2,8,2048]{2,1,0:T(8,128)S(1)}, f32[2,8,2048]{2,1,0:T(8,128)S(1)}, u32[]{:S(2)}, u32[]{:S(2)}) collective-permute-start(f32[2,8,2048]{2,1,0:T(8,128)S(1)} %pad_maximum_fusion.3), channel_id=1, source_target_pairs={{0,32},{32,0},{64,96},{96,64},{128,160},{160,128},{192,224},{224,1... | collective-permute-start | bytes 393224 | tf_op jit(solution)/shard_map/ppermute | solution.py:20
  73.3 8.8 %collective-permute-start.13 = (f32[2,8,2048]{2,1,0:T(8,128)S(1)}, f32[2,8,2048]{2,1,0:T(8,128)S(1)}, u32[]{:S(2)}, u32[]{:S(2)}) collective-permute-start(f32[2,8,2048]{2,1,0:T(8,128)S(1)} %pad_maximum_fusion.4), channel_id=1, source_target_pairs={{0,64},{64,0},{32,96},{96,32},{128,192},{192,128},{160,224},{224,1... | collective-permute-start | bytes 393224 | tf_op jit(solution)/shard_map/ppermute | solution.py:20
  82.1 9.0 %copy-start.5 = (f32[8,16,128]{2,1,0:T(8,128)S(1)}, f32[8,16,128]{2,1,0:T(8,128)}, u32[]{:S(2)}) copy-start(f32[8,16,128]{2,1,0:T(8,128)} %get-tuple-element.11) | copy-start | bytes 196612
  82.1 9.0 %collective-permute-start.14 = (f32[2,8,2048]{2,1,0:T(8,128)S(1)}, f32[2,8,2048]{2,1,0:T(8,128)S(1)}, u32[]{:S(2)}, u32[]{:S(2)}) collective-permute-start(f32[2,8,2048]{2,1,0:T(8,128)S(1)} %pad_maximum_fusion.5), channel_id=1, source_target_pairs={{0,128},{128,0},{32,160},{160,32},{64,192},{192,64},{96,224},{224,... | collective-permute-start | bytes 393224 | tf_op jit(solution)/shard_map/ppermute | solution.py:20

commit v5 on v4

--- a/solution.py
+++ b/solution.py
@@ -1,4 +1,6 @@
 import math
+
+import numpy as np
 
 import jax
 import jax.numpy as jnp
@@ -117,8 +119,9 @@
     own, outer, inner = xr_ref.shape
     xr = xr_ref[...]
     xi = xi_ref[...]
-    twr = twr_ref[...][None]
-    twi = twi_ref[...][None]
+    position = lax.axis_index("tm")
+    twr = twr_ref[position][None]
+    twi = twi_ref[position][None]
     ur = (xr * twr - xi * twi).reshape(own * outer, inner)
     ui = (xr * twi + xi * twr).reshape(own * outer, inner)
     zr, zi = cdot(kr_ref[...], ki_ref[...], ur, ui)
@@ -148,12 +151,14 @@
         moved.append((mr, mi))
     rows_real = []
     rows_imag = []
+    channel_all = band_ref.shape[0] // (2 * band_width)
+    first = lax.axis_index("chan") * own
     for channel in range(own):
         acc_r = jnp.zeros((outer, inner), jnp.float32)
         acc_i = jnp.zeros((outer, inner), jnp.float32)
         for lag in range(band_width):
-            br = band_ref[lag * own + channel]
-            bi = band_ref[(band_width + lag) * own + channel]
+            br = band_ref[lag * channel_all + first + channel]
+            bi = band_ref[(band_width + lag) * channel_all + first + channel]
             rr = resp_ref[0, lag]
             ri = resp_ref[1, lag]
             cr = br * rr - bi * ri
@@ -172,26 +177,35 @@
     xr, xi = cdot(kr_ref[...], -ki_ref[...], yr, yi)
     xr = xr.reshape(own, outer, inner)
     xi = xi.reshape(own, outer, inner)
-    twr = twr_ref[...][None]
-    twi = -twi_ref[...][None]
+    position = lax.axis_index("tm")
+    twr = twr_ref[position][None]
+    twi = -twi_ref[position][None]
     xr_ref[...] = xr * twr - xi * twi
     xi_ref[...] = xr * twi + xi * twr
 
 
-def local_tables(own, outer, inner, phase_bin, total_len):
+def dft_constant(length, numer):
+    angle = -2.0 * np.pi / length * (numer % length)
+    return (np.cos(angle).astype(np.float32), np.sin(angle).astype(np.float32))
+
+
+def local_tables(own, outer, inner, blocks, levels):
     length = outer * inner
-    rows = lax.iota(jnp.int32, outer)[:, None]
-    cols = lax.iota(jnp.int32, inner)[None, :]
-    twr, twi = twiddle((rows * inner + cols) * phase_bin % total_len, total_len)
-    small_r, small_i = dft_table(outer)
-    eye = jnp.eye(own, dtype=jnp.float32)
-    kr = jnp.kron(eye, small_r)
-    ki = jnp.kron(eye, small_i)
-    t2r, t2i = twiddle(rows * cols % length, length)
-    t2r = jnp.tile(t2r, (own, 1))
-    t2i = jnp.tile(t2i, (own, 1))
-    wr, wi = dft_table(inner)
-    return (twr, twi, kr, ki, t2r, t2i, wr, wi)
+    total_len = length * blocks
+    rows = np.arange(outer)[:, None]
+    cols = np.arange(inner)[None, :]
+    residues = [reverse_bits(position, levels) for position in range(blocks)]
+    phase = np.stack([(rows * inner + cols) * residue for residue in residues])
+    twr, twi = dft_constant(total_len, phase)
+    small_r, small_i = dft_constant(outer, rows * np.arange(outer)[None, :])
+    eye = np.eye(own, dtype=np.float32)
+    kr = np.kron(eye, small_r)
+    ki = np.kron(eye, small_i)
+    t2r, t2i = dft_constant(length, rows * cols)
+    t2r = np.tile(t2r, (own, 1))
+    t2i = np.tile(t2i, (own, 1))
+    wr, wi = dft_constant(inner, np.arange(inner)[:, None] * cols)
+    return tuple(jnp.asarray(table) for table in (twr, twi, kr, ki, t2r, t2i, wr, wi))
 
 
 def vmem_specs(count):
@@ -266,15 +280,14 @@
     band_width = band.shape[1]
     half_width = band_width // 2
     channel_all = band.shape[2]
-    tables = local_tables(own, outer, inner, phase_bin, total_len)
+    tables = local_tables(own, outer, inner, blocks, levels)
     spec_real, spec_imag = forward_call(
         real_part.reshape(own, outer, inner), imag_part.reshape(own, outer, inner), tables
     )
-    chan_pos = lax.axis_index("chan")
-    band_rows = lax.dynamic_slice_in_dim(band, chan_pos * own, own, axis=2)
     packed = jnp.concatenate(
         [response.reshape(2 * band_width, -1), offsets.reshape(1, -1).astype(jnp.float32)], axis=0
     )
+    packed, _ = lax.optimization_barrier((packed, real_part))
     table = gather_doubling(packed[None], "chan")
     entries = table.shape[1]
     table = table.transpose(1, 0, 2).reshape(entries, inner, outer).transpose(0, 2, 1)
@@ -283,7 +296,7 @@
     spectra = jnp.stack([spec_real, spec_imag])
     neighbours = [from_offset(spectra, "chan", delta) for delta in (-1, 1, 2, 3)]
     window = jnp.concatenate([neighbours[0], spectra] + neighbours[1:], axis=1)
-    real_part, imag_part = inverse_call(window, shift, responses, band_rows.reshape(-1), tables, own)
+    real_part, imag_part = inverse_call(window, shift, responses, band.reshape(-1), tables, own)
     real_part = real_part.reshape(own, length)
     imag_part = imag_part.reshape(own, length)
     for bit_index in range(levels):

time: 92.2 us -> 97.6 us (1.059)
  the two profiles are of different devices: /device:TPU:30 before, /device:TPU:2 now
where the time goes in v5:
time: 97.6 us; the launch traced here: 97.1 us
  waiting for transfers between devices  41.6 us (43%)
  starting transfers between devices  41.1 us (42%)
  Pallas kernels  5.95 us (6%)
  local copies, waits for them, and re-layouts  5.93 us (6%)
  other arithmetic  1.89 us (2%)
    ppermute x11, starting transfers between devices, from_partner(): return lax.ppermute(block, axis, route)  35.5 us
    ppermute x11, waiting for transfers between devices, from_partner(): return lax.ppermute(block, axis, route)  34.9 us
    ppermute x4, waiting for transfers between devices, from_offset(): lax.ppermute(block, axis, [((i + delta) % count, i) for i in range(count)])  6.76 us
    ppermute x4, starting transfers between devices, from_offset(): lax.ppermute(block, axis, [((i + delta) % count, i) for i in range(count)])  5.66 us
    pallas_call x1, Pallas kernels, inverse_call(): pl.pallas_call(inverse_kernel, out_shape=(shape, shape), in_specs=specs,...  3.47 us
    pallas_call x1, Pallas kernels, forward_call(): pl.pallas_call(forward_kernel, out_shape=(shape, shape), in_specs=vmem_sp...  2.47 us
    unnamed x22, local copies, waits for them, and re-layouts  2.1 us
  transfers between devices with their start and end apart: 15, of which 12 were waited for; matrix products, arithmetic and copies ran while one was open for 2% of the time, Pallas kernels for 3%

profile of v5, /device:TPU:2, one launch (start us, length us, event | category | flops | bytes accessed | tf_op | source)
XLA Modules:
  0.0 97.1 jit_solution(8967780885938587315)
XLA Ops:
  0.0 0.8 stack.47
  0.9 7.3 %collective-permute-start = (f32[2,8,2048]{2,1,0:T(8,128)S(1)}, f32[2,8,2048]{2,1,0:T(8,128)S(1)}, u32[]{:S(2)}, u32[]{:S(2)}) collective-permute-start(f32[2,8,2048]{2,1,0:T(8,128)S(1)} %stack.47), channel_id=1, source_target_pairs={{0,128},{128,0},{32,160},{160,32},{64,192},{192,64},{96,224},{224,... | collective-permute-start | bytes 393224 | tf_op jit(solution)/shard_map/ppermute | solution.py:22
  8.3 3.4 %collective-permute-done = f32[2,8,2048]{2,1,0:T(8,128)S(1)} collective-permute-done((f32[2,8,2048]{2,1,0:T(8,128)S(1)}, f32[2,8,2048]{2,1,0:T(8,128)S(1)}, u32[]{:S(2)}, u32[]{:S(2)}) %collective-permute-start) | collective-permute-done | bytes 131104 | tf_op jit(solution)/shard_map/ppermute | solution.py:22
  11.8 4.7 %collective-permute-start.1 = (f32[2,8,2048]{2,1,0:T(8,128)S(1)}, f32[2,8,2048]{2,1,0:T(8,128)S(1)}, u32[]{:S(2)}, u32[]{:S(2)}) collective-permute-start(f32[2,8,2048]{2,1,0:T(8,128)S(1)} %pad_maximum_fusion), channel_id=1, source_target_pairs={{0,64},{64,0},{32,96},{96,32},{128,192},{192,128},{160,224},{224,1... | collective-permute-start | bytes 393224 | tf_op jit(solution)/shard_map/ppermute | solution.py:22
  16.6 2.9 %collective-permute-done.1 = f32[2,8,2048]{2,1,0:T(8,128)S(1)} collective-permute-done((f32[2,8,2048]{2,1,0:T(8,128)S(1)}, f32[2,8,2048]{2,1,0:T(8,128)S(1)}, u32[]{:S(2)}, u32[]{:S(2)}) %collective-permute-start.1) | collective-permute-done | bytes 131104 | tf_op jit(solution)/shard_map/ppermute | solution.py:22
  19.6 2.0 %collective-permute-start.2 = (f32[2,8,2048]{2,1,0:T(8,128)S(1)}, f32[2,8,2048]{2,1,0:T(8,128)S(1)}, u32[]{:S(2)}, u32[]{:S(2)}) collective-permute-start(f32[2,8,2048]{2,1,0:T(8,128)S(1)} %pad_maximum_fusion.1), channel_id=1, source_target_pairs={{0,32},{32,0},{64,96},{96,64},{128,160},{160,128},{192,224},{224,1... | collective-permute-start | bytes 393224 | tf_op jit(solution)/shard_map/ppermute | solution.py:22
  21.8 0.6 copy-done.7
  22.6 2.1 %collective-permute-done.2 = f32[2,8,2048]{2,1,0:T(8,128)S(1)} collective-permute-done((f32[2,8,2048]{2,1,0:T(8,128)S(1)}, f32[2,8,2048]{2,1,0:T(8,128)S(1)}, u32[]{:S(2)}, u32[]{:S(2)}) %collective-permute-start.2) | collective-permute-done | bytes 131104 | tf_op jit(solution)/shard_map/ppermute | solution.py:22
  24.8 1.2 %collective-permute-done.7 = f32[1,33,64]{1,2,0:T(8,128)S(1)} collective-permute-done((f32[1,33,64]{1,2,0:T(8,128)S(1)}, f32[1,33,64]{1,2,0:T(8,128)S(1)}, u32[]{:S(2)}, u32[]{:S(2)}) %collective-permute-start.7) | collective-permute-done | bytes 8480 | tf_op jit(solution)/shard_map/ppermute | solution.py:22
  26.0 1.7 %collective-permute-start.8 = (f32[2,33,64]{1,2,0:T(8,128)S(1)}, f32[2,33,64]{1,2,0:T(8,128)S(1)}, u32[]{:S(2)}, u32[]{:S(2)}) collective-permute-start(f32[2,33,64]{1,2,0:T(8,128)S(1)} %maximum_select_fusion.4), channel_id=1, source_target_pairs={{0,2},{2,0},{1,3},{3,1},{4,6},{6,4},{5,7},{7,5},{8,10},{10,8},{9,1... | collective-permute-start | bytes 50696 | tf_op jit(solution)/shard_map/ppermute | solution.py:22
  27.7 2.7 %collective-permute-done.8 = f32[2,33,64]{1,2,0:T(8,128)S(1)} collective-permute-done((f32[2,33,64]{1,2,0:T(8,128)S(1)}, f32[2,33,64]{1,2,0:T(8,128)S(1)}, u32[]{:S(2)}, u32[]{:S(2)}) %collective-permute-start.8) | collective-permute-done | bytes 16928 | tf_op jit(solution)/shard_map/ppermute | solution.py:22
  30.4 3.3 %collective-permute-start.9 = (f32[4,33,64]{1,2,0:T(8,128)S(1)}, f32[4,33,64]{1,2,0:T(8,128)S(1)}, u32[]{:S(2)}, u32[]{:S(2)}) collective-permute-start(f32[4,33,64]{1,2,0:T(8,128)S(1)} %maximum_select_fusion.3), channel_id=1, source_target_pairs={{0,4},{4,0},{1,5},{5,1},{2,6},{6,2},{3,7},{7,3},{8,12},{12,8},{9,1... | collective-permute-start | bytes 101384 | tf_op jit(solution)/shard_map/ppermute | solution.py:22
  33.7 0.7 copy_bitcast_fusion
  34.3 2.5 %shard_map.118 = (f32[8,16,128]{2,1,0:T(8,128)}, f32[8,16,128]{2,1,0:T(8,128)}) custom-call(f32[8,16,128]{2,1,0:T(8,128)} %get-tuple-element.26.xr_ref, f32[8,16,128]{2,1,0:T(8,128)} %get-tuple-element.25.xi_ref, f32[8,16,128]{2,1,0:T(8,128)} %constant.208.clone.twr_ref, f32[8,16,128]{2,1,0:T(8,128)} %constant.209.clone.twi_ref, ...), custom_call_target="tpu_custom_call" | custom-call | tf_op jit(solution)/shard_map/pallas_call | solution.py:217
  37.0 0.6 collective-permute-start.10
  37.9 0.7 copy-done.6
  39.2 3.8 %collective-permute-start.4 = (f32[2,8,16,128]{3,2,1,0:T(8,128)S(1)}, f32[2,8,16,128]{3,2,1,0:T(8,128)S(1)}, u32[]{:S(2)}, u32[]{:S(2)}) collective-permute-start(f32[2,8,16,128]{3,2,1,0:T(8,128)S(1)} %pad_maximum_fusion.2), channel_id=1, source_target_pairs={{1,0},{2,1},{3,2},{4,3},{5,4},{6,5},{7,6},{8,7},{9,8},{10,9},{11,1... | collective-permute-start | bytes 393224 | tf_op jit(solution)/shard_map/ppermute | solution.py:238
  43.0 1.8 %collective-permute-start.5 = (f32[2,8,16,128]{3,2,1,0:T(8,128)S(1)}, f32[2,8,16,128]{3,2,1,0:T(8,128)S(1)}, u32[]{:S(2)}, u32[]{:S(2)}) collective-permute-start(f32[2,8,16,128]{3,2,1,0:T(8,128)S(1)} %pad_maximum_fusion.2), channel_id=1, source_target_pairs={{2,0},{3,1},{4,2},{5,3},{6,4},{7,5},{8,6},{9,7},{10,8},{11,9},{12,... | collective-permute-start | bytes 393224 | tf_op jit(solution)/shard_map/ppermute | solution.py:238
  44.8 2.2 %collective-permute-start.11 = (f32[16,33,64]{1,2,0:T(8,128)S(1)}, f32[16,33,64]{1,2,0:T(8,128)S(1)}, u32[]{:S(2)}, u32[]{:S(2)}) collective-permute-start(f32[16,33,64]{1,2,0:T(8,128)S(1)} %maximum_select_fusion.1), channel_id=1, source_target_pairs={{0,16},{16,0},{1,17},{17,1},{2,18},{18,2},{3,19},{19,3},{4,20},{20... | collective-permute-start | bytes 405512 | tf_op jit(solution)/shard_map/ppermute | solution.py:22
  47.1 4.0 %collective-permute-done.5 = f32[2,8,16,128]{3,2,1,0:T(8,128)S(1)} collective-permute-done((f32[2,8,16,128]{3,2,1,0:T(8,128)S(1)}, f32[2,8,16,128]{3,2,1,0:T(8,128)S(1)}, u32[]{:S(2)}, u32[]{:S(2)}) %collective-permute-start.5) | collective-permute-done | bytes 131104 | tf_op jit(solution)/shard_map/ppermute | solution.py:238
  51.1 2.8 %collective-permute-done.6 = f32[2,8,16,128]{3,2,1,0:T(8,128)S(1)} collective-permute-done((f32[2,8,16,128]{3,2,1,0:T(8,128)S(1)}, f32[2,8,16,128]{3,2,1,0:T(8,128)S(1)}, u32[]{:S(2)}, u32[]{:S(2)}) %collective-permute-start.6) | collective-permute-done | bytes 131104 | tf_op jit(solution)/shard_map/ppermute | solution.py:238
  53.9 12.0 %collective-permute-done.11 = f32[16,33,64]{1,2,0:T(8,128)S(1)} collective-permute-done((f32[16,33,64]{1,2,0:T(8,128)S(1)}, f32[16,33,64]{1,2,0:T(8,128)S(1)}, u32[]{:S(2)}, u32[]{:S(2)}) %collective-permute-start.11) | collective-permute-done | bytes 135200 | tf_op jit(solution)/shard_map/ppermute | solution.py:22
  66.6 0.7 slice.74
  67.9 3.5 %shard_map.119 = (f32[8,16,128]{2,1,0:T(8,128)}, f32[8,16,128]{2,1,0:T(8,128)}) custom-call(f32[2,40,16,128]{3,2,1,0:T(8,128)} %copy-done, s32[16,128]{1,0:T(8,128)} %fusion.9.shift_ref, f32[2,16,16,128]{3,2,1,0:T(8,128)} %bitcast.146, f32[8192]{0:T(1024)} %bitcast.159, f32[8,16,128]{2,1,0:T(8,128)} %constant.208.clone.twr_ref, ...), custom_call_target="tpu_custom_call" | custom-call | tf_op jit(solution)/shard_map/pallas_call | solution.py:228
  71.4 0.9 stack_reshape.6
  72.3 2.0 %collective-permute-start.12 = (f32[2,8,2048]{2,1,0:T(8,128)S(1)}, f32[2,8,2048]{2,1,0:T(8,128)S(1)}, u32[]{:S(2)}, u32[]{:S(2)}) collective-permute-start(f32[2,8,2048]{2,1,0:T(8,128)S(1)} %pad_maximum_fusion.3), channel_id=1, source_target_pairs={{0,32},{32,0},{64,96},{96,64},{128,160},{160,128},{192,224},{224,1... | collective-permute-start | bytes 393224 | tf_op jit(solution)/shard_map/ppermute | solution.py:22
  74.4 3.0 %collective-permute-done.12 = f32[2,8,2048]{2,1,0:T(8,128)S(1)} collective-permute-done((f32[2,8,2048]{2,1,0:T(8,128)S(1)}, f32[2,8,2048]{2,1,0:T(8,128)S(1)}, u32[]{:S(2)}, u32[]{:S(2)}) %collective-permute-start.12) | collective-permute-done | bytes 131104 | tf_op jit(solution)/shard_map/ppermute | solution.py:22
  77.4 4.1 %collective-permute-start.13 = (f32[2,8,2048]{2,1,0:T(8,128)S(1)}, f32[2,8,2048]{2,1,0:T(8,128)S(1)}, u32[]{:S(2)}, u32[]{:S(2)}) collective-permute-start(f32[2,8,2048]{2,1,0:T(8,128)S(1)} %pad_maximum_fusion.4), channel_id=1, source_target_pairs={{0,64},{64,0},{32,96},{96,32},{128,192},{192,128},{160,224},{224,1... | collective-permute-start | bytes 393224 | tf_op jit(solution)/shard_map/ppermute | solution.py:22
  81.6 4.4 %collective-permute-done.13 = f32[2,8,2048]{2,1,0:T(8,128)S(1)} collective-permute-done((f32[2,8,2048]{2,1,0:T(8,128)S(1)}, f32[2,8,2048]{2,1,0:T(8,128)S(1)}, u32[]{:S(2)}, u32[]{:S(2)}) %collective-permute-start.13) | collective-permute-done | bytes 131104 | tf_op jit(solution)/shard_map/ppermute | solution.py:22
  86.0 7.4 %collective-permute-start.14 = (f32[2,8,2048]{2,1,0:T(8,128)S(1)}, f32[2,8,2048]{2,1,0:T(8,128)S(1)}, u32[]{:S(2)}, u32[]{:S(2)}) collective-permute-start(f32[2,8,2048]{2,1,0:T(8,128)S(1)} %pad_maximum_fusion.5), channel_id=1, source_target_pairs={{0,128},{128,0},{32,160},{160,32},{64,192},{192,64},{96,224},{224,... | collective-permute-start | bytes 393224 | tf_op jit(solution)/shard_map/ppermute | solution.py:22
  93.5 2.9 %collective-permute-done.14 = f32[2,8,2048]{2,1,0:T(8,128)S(1)} collective-permute-done((f32[2,8,2048]{2,1,0:T(8,128)S(1)}, f32[2,8,2048]{2,1,0:T(8,128)S(1)}, u32[]{:S(2)}, u32[]{:S(2)}) %collective-permute-start.14) | collective-permute-done | bytes 131104 | tf_op jit(solution)/shard_map/ppermute | solution.py:22
  96.4 0.7 select_multiply_fusion
  (52 shorter events, 2.9 us)
Async XLA Ops:
  0.9 10.9 %copy-start.1 = (f32[8,2048]{1,0:T(8,128)S(1)}, f32[8,2048]{1,0:T(8,128)}, u32[]{:S(2)}) copy-start(f32[8,2048]{1,0:T(8,128)} %param.12) | copy-start | bytes 196612
  0.9 10.9 %collective-permute-start = (f32[2,8,2048]{2,1,0:T(8,128)S(1)}, f32[2,8,2048]{2,1,0:T(8,128)S(1)}, u32[]{:S(2)}, u32[]{:S(2)}) collective-permute-start(f32[2,8,2048]{2,1,0:T(8,128)S(1)} %stack.47), channel_id=1, source_target_pairs={{0,128},{128,0},{32,160},{160,32},{64,192},{192,64},{96,224},{224,... | collective-permute-start | bytes 393224 | tf_op jit(solution)/shard_map/ppermute | solution.py:22
  11.8 7.8 %collective-permute-start.1 = (f32[2,8,2048]{2,1,0:T(8,128)S(1)}, f32[2,8,2048]{2,1,0:T(8,128)S(1)}, u32[]{:S(2)}, u32[]{:S(2)}) collective-permute-start(f32[2,8,2048]{2,1,0:T(8,128)S(1)} %pad_maximum_fusion), channel_id=1, source_target_pairs={{0,64},{64,0},{32,96},{96,32},{128,192},{192,128},{160,224},{224,1... | collective-permute-start | bytes 393224 | tf_op jit(solution)/shard_map/ppermute | solution.py:22
  19.6 2.1 %copy-start.8 = (s32[1,64]{1,0:T(1,128)S(1)}, s32[1,64]{1,0:T(1,128)}, u32[]{:S(2)}) copy-start(s32[1,64]{1,0:T(1,128)} %param.15) | copy-start | bytes 772
  19.6 5.1 %collective-permute-start.2 = (f32[2,8,2048]{2,1,0:T(8,128)S(1)}, f32[2,8,2048]{2,1,0:T(8,128)S(1)}, u32[]{:S(2)}, u32[]{:S(2)}) collective-permute-start(f32[2,8,2048]{2,1,0:T(8,128)S(1)} %pad_maximum_fusion.1), channel_id=1, source_target_pairs={{0,32},{32,0},{64,96},{96,64},{128,160},{160,128},{192,224},{224,1... | collective-permute-start | bytes 393224 | tf_op jit(solution)/shard_map/ppermute | solution.py:22
  21.7 0.7 copy-start.7
  24.7 1.3 %collective-permute-start.7 = (f32[1,33,64]{1,2,0:T(8,128)S(1)}, f32[1,33,64]{1,2,0:T(8,128)S(1)}, u32[]{:S(2)}, u32[]{:S(2)}) collective-permute-start(f32[1,33,64]{1,2,0:T(8,128)S(1)} %bitcast.160), channel_id=1, source_target_pairs={{0,1},{1,0},{2,3},{3,2},{4,5},{5,4},{6,7},{7,6},{8,9},{9,8},{10,11... | collective-permute-start | bytes 25352 | tf_op jit(solution)/shard_map/ppermute | solution.py:22
  26.0 4.4 %collective-permute-start.8 = (f32[2,33,64]{1,2,0:T(8,128)S(1)}, f32[2,33,64]{1,2,0:T(8,128)S(1)}, u32[]{:S(2)}, u32[]{:S(2)}) collective-permute-start(f32[2,33,64]{1,2,0:T(8,128)S(1)} %maximum_select_fusion.4), channel_id=1, source_target_pairs={{0,2},{2,0},{1,3},{3,1},{4,6},{6,4},{5,7},{7,5},{8,10},{10,8},{9,1... | collective-permute-start | bytes 50696 | tf_op jit(solution)/shard_map/ppermute | solution.py:22
  30.4 6.6 %collective-permute-start.9 = (f32[4,33,64]{1,2,0:T(8,128)S(1)}, f32[4,33,64]{1,2,0:T(8,128)S(1)}, u32[]{:S(2)}, u32[]{:S(2)}) collective-permute-start(f32[4,33,64]{1,2,0:T(8,128)S(1)} %maximum_select_fusion.3), channel_id=1, source_target_pairs={{0,4},{4,0},{1,5},{5,1},{2,6},{6,2},{3,7},{7,3},{8,12},{12,8},{9,1... | collective-permute-start | bytes 101384 | tf_op jit(solution)/shard_map/ppermute | solution.py:22
  36.8 0.8 copy-start.2
  36.8 0.9 copy-start.3
  37.0 7.8 %collective-permute-start.10 = (f32[8,33,64]{1,2,0:T(8,128)S(1)}, f32[8,33,64]{1,2,0:T(8,128)S(1)}, u32[]{:S(2)}, u32[]{:S(2)}) collective-permute-start(f32[8,33,64]{1,2,0:T(8,128)S(1)} %maximum_select_fusion.2), channel_id=1, source_target_pairs={{0,8},{8,0},{1,9},{9,1},{2,10},{10,2},{3,11},{11,3},{4,12},{12,4},... | collective-permute-start | bytes 202760 | tf_op jit(solution)/shard_map/ppermute | solution.py:22
  37.7 9.3 %collective-permute-start.3 = (f32[2,8,16,128]{3,2,1,0:T(8,128)S(1)}, f32[2,8,16,128]{3,2,1,0:T(8,128)S(1)}, u32[]{:S(2)}, u32[]{:S(2)}) collective-permute-start(f32[2,8,16,128]{3,2,1,0:T(8,128)S(1)} %pad_maximum_fusion.2), channel_id=1, source_target_pairs={{31,0},{0,1},{1,2},{2,3},{3,4},{4,5},{5,6},{6,7},{7,8},{8,9},{9,10... | collective-permute-start | bytes 393224 | tf_op jit(solution)/shard_map/ppermute | solution.py:238
  37.8 0.8 copy-start.6
  39.2 7.9 %collective-permute-start.4 = (f32[2,8,16,128]{3,2,1,0:T(8,128)S(1)}, f32[2,8,16,128]{3,2,1,0:T(8,128)S(1)}, u32[]{:S(2)}, u32[]{:S(2)}) collective-permute-start(f32[2,8,16,128]{3,2,1,0:T(8,128)S(1)} %pad_maximum_fusion.2), channel_id=1, source_target_pairs={{1,0},{2,1},{3,2},{4,3},{5,4},{6,5},{7,6},{8,7},{9,8},{10,9},{11,1... | collective-permute-start | bytes 393224 | tf_op jit(solution)/shard_map/ppermute | solution.py:238
  43.0 8.0 %collective-permute-start.5 = (f32[2,8,16,128]{3,2,1,0:T(8,128)S(1)}, f32[2,8,16,128]{3,2,1,0:T(8,128)S(1)}, u32[]{:S(2)}, u32[]{:S(2)}) collective-permute-start(f32[2,8,16,128]{3,2,1,0:T(8,128)S(1)} %pad_maximum_fusion.2), channel_id=1, source_target_pairs={{2,0},{3,1},{4,2},{5,3},{6,4},{7,5},{8,6},{9,7},{10,8},{11,9},{12,... | collective-permute-start | bytes 393224 | tf_op jit(solution)/shard_map/ppermute | solution.py:238
  44.8 9.1 %collective-permute-start.6 = (f32[2,8,16,128]{3,2,1,0:T(8,128)S(1)}, f32[2,8,16,128]{3,2,1,0:T(8,128)S(1)}, u32[]{:S(2)}, u32[]{:S(2)}) collective-permute-start(f32[2,8,16,128]{3,2,1,0:T(8,128)S(1)} %pad_maximum_fusion.2), channel_id=1, source_target_pairs={{3,0},{4,1},{5,2},{6,3},{7,4},{8,5},{9,6},{10,7},{11,8},{12,9},{13... | collective-permute-start | bytes 393224 | tf_op jit(solution)/shard_map/ppermute | solution.py:238
  44.8 21.1 %collective-permute-start.11 = (f32[16,33,64]{1,2,0:T(8,128)S(1)}, f32[16,33,64]{1,2,0:T(8,128)S(1)}, u32[]{:S(2)}, u32[]{:S(2)}) collective-permute-start(f32[16,33,64]{1,2,0:T(8,128)S(1)} %maximum_select_fusion.1), channel_id=1, source_target_pairs={{0,16},{16,0},{1,17},{17,1},{2,18},{18,2},{3,19},{19,3},{4,20},{20... | collective-permute-start | bytes 405512 | tf_op jit(solution)/shard_map/ppermute | solution.py:22
  53.9 12.2 %copy-start = (f32[2,40,16,128]{3,2,1,0:T(8,128)}, f32[2,40,16,128]{3,2,1,0:T(8,128)S(1)}, u32[]{:S(2)}) copy-start(f32[2,40,16,128]{3,2,1,0:T(8,128)S(1)} %constant_dynamic-update-slice_fusion.win_ref) | copy-start | bytes 1966084
  71.4 0.9 copy-start.5
  72.3 5.1 %collective-permute-start.12 = (f32[2,8,2048]{2,1,0:T(8,128)S(1)}, f32[2,8,2048]{2,1,0:T(8,128)S(1)}, u32[]{:S(2)}, u32[]{:S(2)}) collective-permute-start(f32[2,8,2048]{2,1,0:T(8,128)S(1)} %pad_maximum_fusion.3), channel_id=1, source_target_pairs={{0,32},{32,0},{64,96},{96,64},{128,160},{160,128},{192,224},{224,1... | collective-permute-start | bytes 393224 | tf_op jit(solution)/shard_map/ppermute | solution.py:22
  77.4 8.5 %collective-permute-start.13 = (f32[2,8,2048]{2,1,0:T(8,128)S(1)}, f32[2,8,2048]{2,1,0:T(8,128)S(1)}, u32[]{:S(2)}, u32[]{:S(2)}) collective-permute-start(f32[2,8,2048]{2,1,0:T(8,128)S(1)} %pad_maximum_fusion.4), channel_id=1, source_target_pairs={{0,64},{64,0},{32,96},{96,32},{128,192},{192,128},{160,224},{224,1... | collective-permute-start | bytes 393224 | tf_op jit(solution)/shard_map/ppermute | solution.py:22
  86.0 10.4 %copy-start.4 = (f32[8,16,128]{2,1,0:T(8,128)S(1)}, f32[8,16,128]{2,1,0:T(8,128)}, u32[]{:S(2)}) copy-start(f32[8,16,128]{2,1,0:T(8,128)} %get-tuple-element.13) | copy-start | bytes 196612
  86.0 10.4 %collective-permute-start.14 = (f32[2,8,2048]{2,1,0:T(8,128)S(1)}, f32[2,8,2048]{2,1,0:T(8,128)S(1)}, u32[]{:S(2)}, u32[]{:S(2)}) collective-permute-start(f32[2,8,2048]{2,1,0:T(8,128)S(1)} %pad_maximum_fusion.5), channel_id=1, source_target_pairs={{0,128},{128,0},{32,160},{160,32},{64,192},{192,64},{96,224},{224,... | collective-permute-start | bytes 393224 | tf_op jit(solution)/shard_map/ppermute | solution.py:22

commit v6 on v5

--- a/solution.py
+++ b/solution.py
@@ -287,8 +287,8 @@
     packed = jnp.concatenate(
         [response.reshape(2 * band_width, -1), offsets.reshape(1, -1).astype(jnp.float32)], axis=0
     )
-    packed, _ = lax.optimization_barrier((packed, real_part))
-    table = gather_doubling(packed[None], "chan")
+    slots = jnp.zeros((lax.axis_size("chan"),) + packed.shape, packed.dtype)
+    table = lax.psum(lax.dynamic_update_index_in_dim(slots, packed, lax.axis_index("chan"), 0), "chan")
     entries = table.shape[1]
     table = table.transpose(1, 0, 2).reshape(entries, inner, outer).transpose(0, 2, 1)
     responses = table[: 2 * band_width].reshape(2, band_width, outer, inner)

time: 97.6 us -> 197 us (2.02)
  the two profiles are of different devices: /device:TPU:2 before, /device:TPU:8 now
where the time goes in v6:
time: 197 us
  waiting for transfers between devices  135 us (69%)
  starting transfers between devices  29.9 us (15%)
  between operations  14 us (7%)
  local copies, waits for them, and re-layouts  8.38 us (4%)
  Pallas kernels  5.97 us (3%)
  other arithmetic  3.23 us (2%)
    psum x1, waiting for transfers between devices, per_device(): lax.psum(lax.dynamic_update_index_in_dim(slots, packed, lax.axis_index('c...  110 us
    ppermute x6, starting transfers between devices, from_partner(): return lax.ppermute(block, axis, route)  24.1 us
    ppermute x6, waiting for transfers between devices, from_partner(): return lax.ppermute(block, axis, route)  21.2 us
    ppermute x4, starting transfers between devices, from_offset(): lax.ppermute(block, axis, [((i + delta) % count, i) for i in range(count)])  5.76 us
    ppermute x4, waiting for transfers between devices, from_offset(): lax.ppermute(block, axis, [((i + delta) % count, i) for i in range(count)])  4.64 us
  transfers between devices with their start and end apart: 11, of which 6 were waited for; matrix products, arithmetic and copies ran while one was open for 3% of the time, Pallas kernels for 0%

profile of v6, /device:TPU:8, one launch (start us, length us, event | category | flops | bytes accessed | tf_op | source)
XLA Modules:
  0.0 196.9 jit_solution(3446178766907234516)
XLA Ops:
  6.5 0.8 stack.47
  7.4 7.3 %collective-permute-start = (f32[2,8,2048]{2,1,0:T(8,128)S(1)}, f32[2,8,2048]{2,1,0:T(8,128)S(1)}, u32[]{:S(2)}, u32[]{:S(2)}) collective-permute-start(f32[2,8,2048]{2,1,0:T(8,128)S(1)} %stack.47), channel_id=1, source_target_pairs={{0,128},{128,0},{32,160},{160,32},{64,192},{192,64},{96,224},{224,... | collective-permute-start | bytes 393224 | tf_op jit(solution)/shard_map/ppermute | solution.py:22
  14.8 3.4 %collective-permute-done = f32[2,8,2048]{2,1,0:T(8,128)S(1)} collective-permute-done((f32[2,8,2048]{2,1,0:T(8,128)S(1)}, f32[2,8,2048]{2,1,0:T(8,128)S(1)}, u32[]{:S(2)}, u32[]{:S(2)}) %collective-permute-start) | collective-permute-done | bytes 131104 | tf_op jit(solution)/shard_map/ppermute | solution.py:22
  18.3 4.7 %collective-permute-start.1 = (f32[2,8,2048]{2,1,0:T(8,128)S(1)}, f32[2,8,2048]{2,1,0:T(8,128)S(1)}, u32[]{:S(2)}, u32[]{:S(2)}) collective-permute-start(f32[2,8,2048]{2,1,0:T(8,128)S(1)} %pad_maximum_fusion), channel_id=1, source_target_pairs={{0,64},{64,0},{32,96},{96,32},{128,192},{192,128},{160,224},{224,1... | collective-permute-start | bytes 393224 | tf_op jit(solution)/shard_map/ppermute | solution.py:22
  23.0 0.7 copy-done.8
  23.7 0.1 copy.14
  23.8 0.6 copy-done.7
  24.5 0.1 broadcast_in_dim.7
  24.6 0.1 fusion.8
  24.7 1.2 copy.15
  26.1 2.1 %collective-permute-start.2 = (f32[2,8,2048]{2,1,0:T(8,128)S(1)}, f32[2,8,2048]{2,1,0:T(8,128)S(1)}, u32[]{:S(2)}, u32[]{:S(2)}) collective-permute-start(f32[2,8,2048]{2,1,0:T(8,128)S(1)} %pad_maximum_fusion.1), channel_id=1, source_target_pairs={{0,32},{32,0},{64,96},{96,64},{128,160},{160,128},{192,224},{224,1... | collective-permute-start | bytes 393224 | tf_op jit(solution)/shard_map/ppermute | solution.py:22
  28.2 0.6 copy.18
  28.8 109.7 %all-reduce.3.cloned.1.call-done = f32[33,16,128]{2,1,0:T(8,128)} async-done(((f32[33,16,128]{2,1,0:T(8,128)}), f32[33,16,128]{2,1,0:T(8,128)}) %all-reduce.3.cloned.1.call-update) | async-done | bytes 270352 | tf_op jit(solution)/shard_map/psum | solution.py:291
  138.5 1.7 slice.74
  140.2 0.7 copy_bitcast_fusion
  140.9 2.5 %shard_map.118 = (f32[8,16,128]{2,1,0:T(8,128)}, f32[8,16,128]{2,1,0:T(8,128)}) custom-call(f32[8,16,128]{2,1,0:T(8,128)} %get-tuple-element.24.xr_ref, f32[8,16,128]{2,1,0:T(8,128)} %get-tuple-element.23.xi_ref, f32[8,16,128]{2,1,0:T(8,128)} %constant.153.clone.twr_ref, f32[8,16,128]{2,1,0:T(8,128)} %constant.154.clone.twi_ref, ...), custom_call_target="tpu_custom_call" | custom-call | tf_op jit(solution)/shard_map/pallas_call | solution.py:217
  143.4 0.9 pad_maximum_fusion.2
  144.2 0.1 collective-permute-start.3
  144.3 1.3 fusion.10.shift_ref
  145.6 1.7 collective-permute-start.4
  147.4 3.9 %collective-permute-start.5 = (f32[2,8,16,128]{3,2,1,0:T(8,128)S(1)}, f32[2,8,16,128]{3,2,1,0:T(8,128)S(1)}, u32[]{:S(2)}, u32[]{:S(2)}) collective-permute-start(f32[2,8,16,128]{3,2,1,0:T(8,128)S(1)} %pad_maximum_fusion.2), channel_id=1, source_target_pairs={{2,0},{3,1},{4,2},{5,3},{6,4},{7,5},{8,6},{9,7},{10,8},{11,9},{12,... | collective-permute-start | bytes 393224 | tf_op jit(solution)/shard_map/ppermute | solution.py:238
  151.4 4.6 %collective-permute-done.5 = f32[2,8,16,128]{3,2,1,0:T(8,128)S(1)} collective-permute-done((f32[2,8,16,128]{3,2,1,0:T(8,128)S(1)}, f32[2,8,16,128]{3,2,1,0:T(8,128)S(1)}, u32[]{:S(2)}, u32[]{:S(2)}) %collective-permute-start.5) | collective-permute-done | bytes 131104 | tf_op jit(solution)/shard_map/ppermute | solution.py:238
  156.1 0.8 copy-done
  156.9 3.5 %shard_map.119 = (f32[8,16,128]{2,1,0:T(8,128)}, f32[8,16,128]{2,1,0:T(8,128)}) custom-call(f32[2,40,16,128]{3,2,1,0:T(8,128)} %copy-done, s32[16,128]{1,0:T(8,128)} %fusion.10.shift_ref, f32[2,16,16,128]{3,2,1,0:T(8,128)} %bitcast.149, f32[8192]{0:T(1024)} %bitcast.161, f32[8,16,128]{2,1,0:T(8,128)} %constant.153.clone.twr_ref, ...), custom_call_target="tpu_custom_call" | custom-call | tf_op jit(solution)/shard_map/pallas_call | solution.py:228
  160.4 0.9 stack_reshape.6
  161.3 1.6 collective-permute-start.7
  163.0 4.7 %collective-permute-done.7 = f32[2,8,2048]{2,1,0:T(8,128)S(1)} collective-permute-done((f32[2,8,2048]{2,1,0:T(8,128)S(1)}, f32[2,8,2048]{2,1,0:T(8,128)S(1)}, u32[]{:S(2)}, u32[]{:S(2)}) %collective-permute-start.7) | collective-permute-done | bytes 131104 | tf_op jit(solution)/shard_map/ppermute | solution.py:22
  167.8 2.6 %collective-permute-start.8 = (f32[2,8,2048]{2,1,0:T(8,128)S(1)}, f32[2,8,2048]{2,1,0:T(8,128)S(1)}, u32[]{:S(2)}, u32[]{:S(2)}) collective-permute-start(f32[2,8,2048]{2,1,0:T(8,128)S(1)} %pad_maximum_fusion.4), channel_id=1, source_target_pairs={{0,64},{64,0},{32,96},{96,32},{128,192},{192,128},{160,224},{224,1... | collective-permute-start | bytes 393224 | tf_op jit(solution)/shard_map/ppermute | solution.py:22
  170.4 6.6 %collective-permute-done.8 = f32[2,8,2048]{2,1,0:T(8,128)S(1)} collective-permute-done((f32[2,8,2048]{2,1,0:T(8,128)S(1)}, f32[2,8,2048]{2,1,0:T(8,128)S(1)}, u32[]{:S(2)}, u32[]{:S(2)}) %collective-permute-start.8) | collective-permute-done | bytes 131104 | tf_op jit(solution)/shard_map/ppermute | solution.py:22
  177.1 5.8 %collective-permute-start.9 = (f32[2,8,2048]{2,1,0:T(8,128)S(1)}, f32[2,8,2048]{2,1,0:T(8,128)S(1)}, u32[]{:S(2)}, u32[]{:S(2)}) collective-permute-start(f32[2,8,2048]{2,1,0:T(8,128)S(1)} %pad_maximum_fusion.5), channel_id=1, source_target_pairs={{0,128},{128,0},{32,160},{160,32},{64,192},{192,64},{96,224},{224,... | collective-permute-start | bytes 393224 | tf_op jit(solution)/shard_map/ppermute | solution.py:22
  182.9 6.4 %collective-permute-done.9 = f32[2,8,2048]{2,1,0:T(8,128)S(1)} collective-permute-done((f32[2,8,2048]{2,1,0:T(8,128)S(1)}, f32[2,8,2048]{2,1,0:T(8,128)S(1)}, u32[]{:S(2)}, u32[]{:S(2)}) %collective-permute-start.9) | collective-permute-done | bytes 131104 | tf_op jit(solution)/shard_map/ppermute | solution.py:22
  189.3 0.7 select_multiply_fusion
  (41 shorter events, 0.4 us)
Async XLA Ops:
  6.5 132.0 %all-reduce.3.cloned.1.call-start = ((), (), s32[]{:S(2)}) async-start(), calls=%async_computation | async-start | bytes 540672 | tf_op jit(solution)/shard_map/psum | solution.py:291
  7.4 10.9 %copy-start.1 = (f32[8,2048]{1,0:T(8,128)S(1)}, f32[8,2048]{1,0:T(8,128)}, u32[]{:S(2)}) copy-start(f32[8,2048]{1,0:T(8,128)} %param.12) | copy-start | bytes 196612
  7.4 10.9 %collective-permute-start = (f32[2,8,2048]{2,1,0:T(8,128)S(1)}, f32[2,8,2048]{2,1,0:T(8,128)S(1)}, u32[]{:S(2)}, u32[]{:S(2)}) collective-permute-start(f32[2,8,2048]{2,1,0:T(8,128)S(1)} %stack.47), channel_id=1, source_target_pairs={{0,128},{128,0},{32,160},{160,32},{64,192},{192,64},{96,224},{224,... | collective-permute-start | bytes 393224 | tf_op jit(solution)/shard_map/ppermute | solution.py:22
  18.3 7.7 %collective-permute-start.1 = (f32[2,8,2048]{2,1,0:T(8,128)S(1)}, f32[2,8,2048]{2,1,0:T(8,128)S(1)}, u32[]{:S(2)}, u32[]{:S(2)}) collective-permute-start(f32[2,8,2048]{2,1,0:T(8,128)S(1)} %pad_maximum_fusion), channel_id=1, source_target_pairs={{0,64},{64,0},{32,96},{96,32},{128,192},{192,128},{160,224},{224,1... | collective-permute-start | bytes 393224 | tf_op jit(solution)/shard_map/ppermute | solution.py:22
  23.0 0.7 copy-start.8
  23.7 0.7 copy-start.7
  26.1 2.1 %copy-start.6 = (f32[2,16,256]{2,1,0:T(8,128)S(1)}, f32[2,16,256]{2,1,0:T(8,128)}, u32[]{:S(2)}) copy-start(f32[2,16,256]{2,1,0:T(8,128)} %param.13) | copy-start | bytes 98308
  26.1 114.0 %collective-permute-start.2 = (f32[2,8,2048]{2,1,0:T(8,128)S(1)}, f32[2,8,2048]{2,1,0:T(8,128)S(1)}, u32[]{:S(2)}, u32[]{:S(2)}) collective-permute-start(f32[2,8,2048]{2,1,0:T(8,128)S(1)} %pad_maximum_fusion.1), channel_id=1, source_target_pairs={{0,32},{32,0},{64,96},{96,64},{128,160},{160,128},{192,224},{224,1... | collective-permute-start | bytes 393224 | tf_op jit(solution)/shard_map/ppermute | solution.py:22
  144.2 7.1 %collective-permute-start.3 = (f32[2,8,16,128]{3,2,1,0:T(8,128)S(1)}, f32[2,8,16,128]{3,2,1,0:T(8,128)S(1)}, u32[]{:S(2)}, u32[]{:S(2)}) collective-permute-start(f32[2,8,16,128]{3,2,1,0:T(8,128)S(1)} %pad_maximum_fusion.2), channel_id=1, source_target_pairs={{31,0},{0,1},{1,2},{2,3},{3,4},{4,5},{5,6},{6,7},{7,8},{8,9},{9,10... | collective-permute-start | bytes 393224 | tf_op jit(solution)/shard_map/ppermute | solution.py:238
  145.6 5.7 %copy-start.2 = (f32[8,16,128]{2,1,0:T(8,128)S(1)}, f32[8,16,128]{2,1,0:T(8,128)}, u32[]{:S(2)}) copy-start(f32[8,16,128]{2,1,0:T(8,128)} %get-tuple-element.9) | copy-start | bytes 196612
  145.6 5.7 %copy-start.3 = (f32[8,16,128]{2,1,0:T(8,128)S(1)}, f32[8,16,128]{2,1,0:T(8,128)}, u32[]{:S(2)}) copy-start(f32[8,16,128]{2,1,0:T(8,128)} %get-tuple-element.10) | copy-start | bytes 196612
  145.6 5.7 %collective-permute-start.4 = (f32[2,8,16,128]{3,2,1,0:T(8,128)S(1)}, f32[2,8,16,128]{3,2,1,0:T(8,128)S(1)}, u32[]{:S(2)}, u32[]{:S(2)}) collective-permute-start(f32[2,8,16,128]{3,2,1,0:T(8,128)S(1)} %pad_maximum_fusion.2), channel_id=1, source_target_pairs={{1,0},{2,1},{3,2},{4,3},{5,4},{6,5},{7,6},{8,7},{9,8},{10,9},{11,1... | collective-permute-start | bytes 393224 | tf_op jit(solution)/shard_map/ppermute | solution.py:238
  147.4 8.7 %collective-permute-start.5 = (f32[2,8,16,128]{3,2,1,0:T(8,128)S(1)}, f32[2,8,16,128]{3,2,1,0:T(8,128)S(1)}, u32[]{:S(2)}, u32[]{:S(2)}) collective-permute-start(f32[2,8,16,128]{3,2,1,0:T(8,128)S(1)} %pad_maximum_fusion.2), channel_id=1, source_target_pairs={{2,0},{3,1},{4,2},{5,3},{6,4},{7,5},{8,6},{9,7},{10,8},{11,9},{12,... | collective-permute-start | bytes 393224 | tf_op jit(solution)/shard_map/ppermute | solution.py:238
  151.3 4.7 %collective-permute-start.6 = (f32[2,8,16,128]{3,2,1,0:T(8,128)S(1)}, f32[2,8,16,128]{3,2,1,0:T(8,128)S(1)}, u32[]{:S(2)}, u32[]{:S(2)}) collective-permute-start(f32[2,8,16,128]{3,2,1,0:T(8,128)S(1)} %pad_maximum_fusion.2), channel_id=1, source_target_pairs={{3,0},{4,1},{5,2},{6,3},{7,4},{8,5},{9,6},{10,7},{11,8},{12,9},{13... | collective-permute-start | bytes 393224 | tf_op jit(solution)/shard_map/ppermute | solution.py:238
  156.1 0.8 copy-start
  160.4 0.9 copy-start.5
  161.3 6.4 %collective-permute-start.7 = (f32[2,8,2048]{2,1,0:T(8,128)S(1)}, f32[2,8,2048]{2,1,0:T(8,128)S(1)}, u32[]{:S(2)}, u32[]{:S(2)}) collective-permute-start(f32[2,8,2048]{2,1,0:T(8,128)S(1)} %pad_maximum_fusion.3), channel_id=1, source_target_pairs={{0,32},{32,0},{64,96},{96,64},{128,160},{160,128},{192,224},{224,1... | collective-permute-start | bytes 393224 | tf_op jit(solution)/shard_map/ppermute | solution.py:22
  167.8 9.2 %collective-permute-start.8 = (f32[2,8,2048]{2,1,0:T(8,128)S(1)}, f32[2,8,2048]{2,1,0:T(8,128)S(1)}, u32[]{:S(2)}, u32[]{:S(2)}) collective-permute-start(f32[2,8,2048]{2,1,0:T(8,128)S(1)} %pad_maximum_fusion.4), channel_id=1, source_target_pairs={{0,64},{64,0},{32,96},{96,32},{128,192},{192,128},{160,224},{224,1... | collective-permute-start | bytes 393224 | tf_op jit(solution)/shard_map/ppermute | solution.py:22
  177.1 12.3 %copy-start.4 = (f32[8,16,128]{2,1,0:T(8,128)S(1)}, f32[8,16,128]{2,1,0:T(8,128)}, u32[]{:S(2)}) copy-start(f32[8,16,128]{2,1,0:T(8,128)} %get-tuple-element.11) | copy-start | bytes 196612
  177.1 12.2 %collective-permute-start.9 = (f32[2,8,2048]{2,1,0:T(8,128)S(1)}, f32[2,8,2048]{2,1,0:T(8,128)S(1)}, u32[]{:S(2)}, u32[]{:S(2)}) collective-permute-start(f32[2,8,2048]{2,1,0:T(8,128)S(1)} %pad_maximum_fusion.5), channel_id=1, source_target_pairs={{0,128},{128,0},{32,160},{160,32},{64,192},{192,64},{96,224},{224,... | collective-permute-start | bytes 393224 | tf_op jit(solution)/shard_map/ppermute | solution.py:22
Sparse Core Ops, SparseCore 0:
  26.0 112.4 all-reduce.2

commit v7 on v6

--- a/solution.py
+++ b/solution.py
@@ -238,6 +238,38 @@
     return lax.ppermute(block, axis, [((i + delta) % count, i) for i in range(count)])
 
 
+def digit_radices(count):
+    radices = []
+    for radix in (2, 4, 4):
+        if count % radix == 0 and count > 1:
+            radices.append(radix)
+            count //= radix
+    while count > 1:
+        radices.append(2)
+        count //= 2
+    return radices
+
+
+def gather_radix(block, axis):
+    count = lax.axis_size(axis)
+    me = lax.axis_index(axis)
+    stride = 1
+    for radix in digit_radices(count):
+        digit = me // stride % radix
+        pieces = [block]
+        for delta in range(1, radix):
+            route = []
+            for index in range(count):
+                own_digit = index // stride % radix
+                source = index + ((own_digit + delta) % radix - own_digit) * stride
+                route.append((source, index))
+            pieces.append(lax.ppermute(block, axis, route))
+        stacked = jnp.roll(jnp.stack(pieces), digit, axis=0)
+        block = stacked.reshape((radix * block.shape[0],) + block.shape[1:])
+        stride *= radix
+    return block
+
+
 def gather_doubling(block, axis):
     count = lax.axis_size(axis)
     me = lax.axis_index(axis)
@@ -262,9 +294,15 @@
     imag_part = jnp.zeros_like(signal)
     for bit_index in range(levels - 1, -1, -1):
         half_span = 1 << bit_index
-        partner = from_partner(jnp.stack([real_part, imag_part]), "tm", bit_index)
         upper_half = device_pos // half_span % 2 == 1
         cosine, sine_part = twiddle(device_pos % half_span, 2 * half_span)
+        if bit_index == levels - 1:
+            partner_real = from_partner(real_part, "tm", bit_index)
+            diff_real = partner_real - real_part
+            imag_part = jnp.where(upper_half, diff_real * sine_part, 0.0)
+            real_part = jnp.where(upper_half, diff_real * cosine, real_part + partner_real)
+            continue
+        partner = from_partner(jnp.stack([real_part, imag_part]), "tm", bit_index)
         diff_real = partner[0] - real_part
         diff_imag = partner[1] - imag_part
         new_real = jnp.where(
@@ -287,8 +325,7 @@
     packed = jnp.concatenate(
         [response.reshape(2 * band_width, -1), offsets.reshape(1, -1).astype(jnp.float32)], axis=0
     )
-    slots = jnp.zeros((lax.axis_size("chan"),) + packed.shape, packed.dtype)
-    table = lax.psum(lax.dynamic_update_index_in_dim(slots, packed, lax.axis_index("chan"), 0), "chan")
+    table = gather_radix(packed[None], "chan")
     entries = table.shape[1]
     table = table.transpose(1, 0, 2).reshape(entries, inner, outer).transpose(0, 2, 1)
     responses = table[: 2 * band_width].reshape(2, band_width, outer, inner)
@@ -301,10 +338,15 @@
     imag_part = imag_part.reshape(own, length)
     for bit_index in range(levels):
         half_span = 1 << bit_index
-        partner = from_partner(jnp.stack([real_part, imag_part]), "tm", bit_index)
         upper_half = device_pos // half_span % 2 == 1
         cosine, sine_part = twiddle(device_pos % half_span, 2 * half_span)
         sine_part = -sine_part
+        if bit_index == levels - 1:
+            own_prod = real_part * cosine - imag_part * sine_part
+            partner_real = from_partner(jnp.where(upper_half, own_prod, real_part), "tm", bit_index)
+            real_part = jnp.where(upper_half, partner_real - own_prod, real_part + partner_real)
+            break
+        partner = from_partner(jnp.stack([real_part, imag_part]), "tm", bit_index)
         base_real = jnp.where(upper_half, partner[0], real_part)
         base_imag = jnp.where(upper_half, partner[1], imag_part)
         scaled_real = jnp.where(upper_half, real_part, partner[0])

time: 197 us -> 89.5 us (0.45)
  the two profiles are of different devices: /device:TPU:8 before, /device:TPU:30 now
where the time goes in v7:
time: 89.5 us; the launch traced here: 88.9 us
  waiting for transfers between devices  45.6 us (51%)
  starting transfers between devices  24.9 us (28%)
  local copies, waits for them, and re-layouts  6.27 us (7%)
  Pallas kernels  5.95 us (7%)
  other arithmetic  5.6 us (6%)
    ppermute x6, waiting for transfers between devices, from_partner(): return lax.ppermute(block, axis, route)  20.2 us
    ppermute x4, waiting for transfers between devices, from_offset(): lax.ppermute(block, axis, [((i + delta) % count, i) for i in range(count)])  13.2 us
    ppermute x6, starting transfers between devices, from_partner(): return lax.ppermute(block, axis, route)  12.8 us
    ppermute x7, waiting for transfers between devices, gather_radix(): pieces.append(lax.ppermute(block, axis, route))  12.2 us
    ppermute x7, starting transfers between devices, gather_radix(): pieces.append(lax.ppermute(block, axis, route))  8.06 us
    ppermute x4, starting transfers between devices, from_offset(): lax.ppermute(block, axis, [((i + delta) % count, i) for i in range(count)])  4.05 us
    pallas_call x1, Pallas kernels, inverse_call(): pl.pallas_call(inverse_kernel, out_shape=(shape, shape), in_specs=specs,...  3.47 us
    pallas_call x1, Pallas kernels, forward_call(): pl.pallas_call(forward_kernel, out_shape=(shape, shape), in_specs=vmem_sp...  2.48 us
  transfers between devices with their start and end apart: 17, of which 11 were waited for; matrix products, arithmetic and copies ran while one was open for 6% of the time, Pallas kernels for 0%

profile of v7, /device:TPU:30, one launch (start us, length us, event | category | flops | bytes accessed | tf_op | source)
XLA Modules:
  0.0 88.9 jit_solution(13844747155254941701)
XLA Ops:
  0.7 0.7 fusion.12
  1.4 1.2 %collective-permute-done.7 = f32[1,33,64]{2,1,0:T(8,128)S(1)} collective-permute-done((f32[1,33,64]{2,1,0:T(8,128)S(1)}, f32[1,33,64]{2,1,0:T(8,128)S(1)}, u32[]{:S(2)}, u32[]{:S(2)}) %collective-permute-start.7) | collective-permute-done | bytes 8480 | tf_op jit(solution)/shard_map/ppermute | solution.py:266
  2.6 0.8 collective-permute-start.8
  3.5 7.2 %collective-permute-start = (f32[8,2048]{1,0:T(8,128)}, f32[8,2048]{1,0:T(8,128)S(1)}, u32[]{:S(2)}, u32[]{:S(2)}) collective-permute-start(f32[8,2048]{1,0:T(8,128)} %param.12), channel_id=1, source_target_pairs={{0,128},{128,0},{32,160},{160,32},{64,192},{192,64},{96,224},{224,... | collective-permute-start | bytes 196616 | tf_op jit(solution)/shard_map/ppermute | solution.py:22
  11.0 1.4 %copy.18 = f32[4,2,8,128]{3,1,2,0:T(2,128)} copy(f32[4,2,8,128]{3,2,1,0:T(8,128)} %bitcast.188) | data formatting | bytes 65536
  12.4 0.9 %collective-permute-start.9 = (f32[2,33,64]{2,1,0:T(8,128)S(1)}, f32[2,33,64]{2,1,0:T(8,128)S(1)}, u32[]{:S(2)}, u32[]{:S(2)}) collective-permute-start(f32[2,33,64]{2,1,0:T(8,128)S(1)} %bitcast.185), channel_id=1, source_target_pairs={{4,0},{5,1},{6,2},{7,3},{0,4},{1,5},{2,6},{3,7},{12,8},{13,9},{14,... | collective-permute-start | bytes 50696 | tf_op jit(solution)/shard_map/ppermute | solution.py:266
  13.3 2.2 %collective-permute-start.10 = (f32[2,33,64]{2,1,0:T(8,128)S(1)}, f32[2,33,64]{2,1,0:T(8,128)S(1)}, u32[]{:S(2)}, u32[]{:S(2)}) collective-permute-start(f32[2,33,64]{2,1,0:T(8,128)S(1)} %bitcast.186), channel_id=1, source_target_pairs={{6,0},{7,1},{0,2},{1,3},{2,4},{3,5},{4,6},{5,7},{14,8},{15,9},{8,1... | collective-permute-start | bytes 50696 | tf_op jit(solution)/shard_map/ppermute | solution.py:266
  15.5 2.4 %collective-permute-done.9 = f32[2,33,64]{2,1,0:T(8,128)S(1)} collective-permute-done((f32[2,33,64]{2,1,0:T(8,128)S(1)}, f32[2,33,64]{2,1,0:T(8,128)S(1)}, u32[]{:S(2)}, u32[]{:S(2)}) %collective-permute-start.9) | collective-permute-done | bytes 16928 | tf_op jit(solution)/shard_map/ppermute | solution.py:266
  18.4 0.9 %collective-permute-start.11 = (f32[8,33,64]{1,2,0:T(8,128)S(1)}, f32[8,33,64]{1,2,0:T(8,128)S(1)}, u32[]{:S(2)}, u32[]{:S(2)}) collective-permute-start(f32[8,33,64]{1,2,0:T(8,128)S(1)} %bitcast.168), channel_id=1, source_target_pairs={{8,0},{9,1},{10,2},{11,3},{12,4},{13,5},{14,6},{15,7},{16,8},{17,9... | collective-permute-start | bytes 202760 | tf_op jit(solution)/shard_map/ppermute | solution.py:266
  19.3 1.1 %collective-permute-start.12 = (f32[8,33,64]{1,2,0:T(8,128)S(1)}, f32[8,33,64]{1,2,0:T(8,128)S(1)}, u32[]{:S(2)}, u32[]{:S(2)}) collective-permute-start(f32[8,33,64]{1,2,0:T(8,128)S(1)} %bitcast.169), channel_id=1, source_target_pairs={{16,0},{17,1},{18,2},{19,3},{20,4},{21,5},{22,6},{23,7},{24,8},{25... | collective-permute-start | bytes 202760 | tf_op jit(solution)/shard_map/ppermute | solution.py:266
  20.4 2.1 %collective-permute-start.13 = (f32[8,33,64]{1,2,0:T(8,128)S(1)}, f32[8,33,64]{1,2,0:T(8,128)S(1)}, u32[]{:S(2)}, u32[]{:S(2)}) collective-permute-start(f32[8,33,64]{1,2,0:T(8,128)S(1)} %bitcast.170), channel_id=1, source_target_pairs={{24,0},{25,1},{26,2},{27,3},{28,4},{29,5},{30,6},{31,7},{0,8},{1,9... | collective-permute-start | bytes 202760 | tf_op jit(solution)/shard_map/ppermute | solution.py:266
  22.6 1.6 %collective-permute-start.1 = (f32[2,8,2048]{2,1,0:T(8,128)S(1)}, f32[2,8,2048]{2,1,0:T(8,128)S(1)}, u32[]{:S(2)}, u32[]{:S(2)}) collective-permute-start(f32[2,8,2048]{2,1,0:T(8,128)S(1)} %pad_maximum_fusion), channel_id=1, source_target_pairs={{0,64},{64,0},{32,96},{96,32},{128,192},{192,128},{160,224},{224,1... | collective-permute-start | bytes 393224 | tf_op jit(solution)/shard_map/ppermute | solution.py:22
  24.1 7.8 %collective-permute-done.11 = f32[8,33,64]{1,2,0:T(8,128)S(1)} collective-permute-done((f32[8,33,64]{1,2,0:T(8,128)S(1)}, f32[8,33,64]{1,2,0:T(8,128)S(1)}, u32[]{:S(2)}, u32[]{:S(2)}) %collective-permute-start.11) | collective-permute-done | bytes 67616 | tf_op jit(solution)/shard_map/ppermute | solution.py:266
  32.8 1.1 %collective-permute-start.2 = (f32[2,8,2048]{2,1,0:T(8,128)S(1)}, f32[2,8,2048]{2,1,0:T(8,128)S(1)}, u32[]{:S(2)}, u32[]{:S(2)}) collective-permute-start(f32[2,8,2048]{2,1,0:T(8,128)S(1)} %pad_maximum_fusion.1), channel_id=1, source_target_pairs={{0,32},{32,0},{64,96},{96,64},{128,160},{160,128},{192,224},{224,1... | collective-permute-start | bytes 393224 | tf_op jit(solution)/shard_map/ppermute | solution.py:22
  35.2 2.7 %collective-permute-done.2 = f32[2,8,2048]{2,1,0:T(8,128)S(1)} collective-permute-done((f32[2,8,2048]{2,1,0:T(8,128)S(1)}, f32[2,8,2048]{2,1,0:T(8,128)S(1)}, u32[]{:S(2)}, u32[]{:S(2)}) %collective-permute-start.2) | collective-permute-done | bytes 131104 | tf_op jit(solution)/shard_map/ppermute | solution.py:22
  38.5 2.5 %shard_map.118 = (f32[8,16,128]{2,1,0:T(8,128)}, f32[8,16,128]{2,1,0:T(8,128)}) custom-call(f32[8,16,128]{2,1,0:T(8,128)} %get-tuple-element.31.xr_ref, f32[8,16,128]{2,1,0:T(8,128)} %get-tuple-element.30.xi_ref, f32[8,16,128]{2,1,0:T(8,128)} %constant.226.clone.twr_ref, f32[8,16,128]{2,1,0:T(8,128)} %constant.227.clone.twi_ref, ...), custom_call_target="tpu_custom_call" | custom-call | tf_op jit(solution)/shard_map/pallas_call | solution.py:217
  41.0 0.9 pad_maximum_fusion.2
  42.6 1.7 %collective-permute-start.4 = (f32[2,8,16,128]{3,2,1,0:T(8,128)S(1)}, f32[2,8,16,128]{3,2,1,0:T(8,128)S(1)}, u32[]{:S(2)}, u32[]{:S(2)}) collective-permute-start(f32[2,8,16,128]{3,2,1,0:T(8,128)S(1)} %pad_maximum_fusion.2), channel_id=1, source_target_pairs={{1,0},{2,1},{3,2},{4,3},{5,4},{6,5},{7,6},{8,7},{9,8},{10,9},{11,1... | collective-permute-start | bytes 393224 | tf_op jit(solution)/shard_map/ppermute | solution.py:238
  44.3 1.9 %collective-permute-start.5 = (f32[2,8,16,128]{3,2,1,0:T(8,128)S(1)}, f32[2,8,16,128]{3,2,1,0:T(8,128)S(1)}, u32[]{:S(2)}, u32[]{:S(2)}) collective-permute-start(f32[2,8,16,128]{3,2,1,0:T(8,128)S(1)} %pad_maximum_fusion.2), channel_id=1, source_target_pairs={{2,0},{3,1},{4,2},{5,3},{6,4},{7,5},{8,6},{9,7},{10,8},{11,9},{12,... | collective-permute-start | bytes 393224 | tf_op jit(solution)/shard_map/ppermute | solution.py:238
  46.6 0.9 constant_dynamic-update-slice_fusion.3
  47.5 1.1 %collective-permute-done.4 = f32[2,8,16,128]{3,2,1,0:T(8,128)S(1)} collective-permute-done((f32[2,8,16,128]{3,2,1,0:T(8,128)S(1)}, f32[2,8,16,128]{3,2,1,0:T(8,128)S(1)}, u32[]{:S(2)}, u32[]{:S(2)}) %collective-permute-start.4) | collective-permute-done | bytes 131104 | tf_op jit(solution)/shard_map/ppermute | solution.py:238
  48.6 12.1 %collective-permute-done.5 = f32[2,8,16,128]{3,2,1,0:T(8,128)S(1)} collective-permute-done((f32[2,8,16,128]{3,2,1,0:T(8,128)S(1)}, f32[2,8,16,128]{3,2,1,0:T(8,128)S(1)}, u32[]{:S(2)}, u32[]{:S(2)}) %collective-permute-start.5) | collective-permute-done | bytes 131104 | tf_op jit(solution)/shard_map/ppermute | solution.py:238
  60.7 0.8 copy-done
  61.6 3.5 %shard_map.119 = (f32[8,16,128]{2,1,0:T(8,128)}, f32[8,16,128]{2,1,0:T(8,128)}) custom-call(f32[2,40,16,128]{3,2,1,0:T(8,128)} %copy-done, s32[16,128]{1,0:T(8,128)} %fusion.14.shift_ref, f32[2,16,16,128]{3,2,1,0:T(8,128)} %bitcast.175, f32[8192]{0:T(1024)} %bitcast.187, f32[8,16,128]{2,1,0:T(8,128)} %constant.226.clone.twr_ref, ...), custom_call_target="tpu_custom_call" | custom-call | tf_op jit(solution)/shard_map/pallas_call | solution.py:228
  65.0 0.9 stack_reshape.14
  65.9 0.9 stack_reshape.15
  66.8 1.1 %collective-permute-start.14 = (f32[2,8,2048]{2,1,0:T(8,128)S(1)}, f32[2,8,2048]{2,1,0:T(8,128)S(1)}, u32[]{:S(2)}, u32[]{:S(2)}) collective-permute-start(f32[2,8,2048]{2,1,0:T(8,128)S(1)} %pad_maximum_fusion.3), channel_id=1, source_target_pairs={{0,32},{32,0},{64,96},{96,64},{128,160},{160,128},{192,224},{224,1... | collective-permute-start | bytes 393224 | tf_op jit(solution)/shard_map/ppermute | solution.py:22
  67.9 3.9 %collective-permute-done.14 = f32[2,8,2048]{2,1,0:T(8,128)S(1)} collective-permute-done((f32[2,8,2048]{2,1,0:T(8,128)S(1)}, f32[2,8,2048]{2,1,0:T(8,128)S(1)}, u32[]{:S(2)}, u32[]{:S(2)}) %collective-permute-start.14) | collective-permute-done | bytes 131104 | tf_op jit(solution)/shard_map/ppermute | solution.py:22
  71.9 1.7 %collective-permute-start.15 = (f32[2,8,2048]{2,1,0:T(8,128)S(1)}, f32[2,8,2048]{2,1,0:T(8,128)S(1)}, u32[]{:S(2)}, u32[]{:S(2)}) collective-permute-start(f32[2,8,2048]{2,1,0:T(8,128)S(1)} %pad_maximum_fusion.4), channel_id=1, source_target_pairs={{0,64},{64,0},{32,96},{96,32},{128,192},{192,128},{160,224},{224,1... | collective-permute-start | bytes 393224 | tf_op jit(solution)/shard_map/ppermute | solution.py:22
  73.6 0.9 %add_select_fusion.2 = (f32[8,2048]{1,0:T(8,128)S(1)}, f32[8,2048]{1,0:T(8,128)S(1)}) fusion(f32[1,8,16,128]{3,2,1,0:T(8,128)} %bitcast.179, f32[1,8,16,128]{3,2,1,0:T(8,128)} %bitcast.178, f32[2,8,2048]{2,1,0:T(8,128)S(1)} %collective-permute-done.14, pred[]{:T(512)S(6)} %eq.39), kind=kLoop, calls=%fused_computation.33 | loop fusion | flops 229376 | bytes 393217 | tf_op jit(solution)/shard_map/jit(_where)/select_n | solution.py:356
  74.5 5.4 %collective-permute-done.15 = f32[2,8,2048]{2,1,0:T(8,128)S(1)} collective-permute-done((f32[2,8,2048]{2,1,0:T(8,128)S(1)}, f32[2,8,2048]{2,1,0:T(8,128)S(1)}, u32[]{:S(2)}, u32[]{:S(2)}) %collective-permute-start.15) | collective-permute-done | bytes 131104 | tf_op jit(solution)/shard_map/ppermute | solution.py:22
  80.1 8.2 %collective-permute-done.16 = f32[8,2048]{1,0:T(8,128)S(1)} collective-permute-done((f32[8,2048]{1,0:T(8,128)S(1)}, f32[8,2048]{1,0:T(8,128)S(1)}, u32[]{:S(2)}, u32[]{:S(2)}) %collective-permute-start.16) | collective-permute-done | bytes 65568 | tf_op jit(solution)/shard_map/ppermute | solution.py:22
  (53 shorter events, 5.9 us)
Async XLA Ops:
  0.0 22.5 %copy-start.1 = (f32[8,2048]{1,0:T(8,128)S(1)}, f32[8,2048]{1,0:T(8,128)}, u32[]{:S(2)}) copy-start(f32[8,2048]{1,0:T(8,128)} %param.12) | copy-start | bytes 196612
  1.4 1.2 %collective-permute-start.7 = (f32[1,33,64]{2,1,0:T(8,128)S(1)}, f32[1,33,64]{2,1,0:T(8,128)S(1)}, u32[]{:S(2)}, u32[]{:S(2)}) collective-permute-start(f32[1,33,64]{2,1,0:T(8,128)S(1)} %get-tuple-element.29), channel_id=1, source_target_pairs={{1,0},{0,1},{3,2},{2,3},{5,4},{4,5},{7,6},{6,7},{9,8},{8,9},{11,10... | collective-permute-start | bytes 25352 | tf_op jit(solution)/shard_map/ppermute | solution.py:266
  2.6 12.9 %collective-permute-start.8 = (f32[2,33,64]{2,1,0:T(8,128)S(1)}, f32[2,33,64]{2,1,0:T(8,128)S(1)}, u32[]{:S(2)}, u32[]{:S(2)}) collective-permute-start(f32[2,33,64]{2,1,0:T(8,128)S(1)} %bitcast.184), channel_id=1, source_target_pairs={{2,0},{3,1},{4,2},{5,3},{6,4},{7,5},{0,6},{1,7},{10,8},{11,9},{12,... | collective-permute-start | bytes 50696 | tf_op jit(solution)/shard_map/ppermute | solution.py:266
  3.5 19.1 %collective-permute-start = (f32[8,2048]{1,0:T(8,128)}, f32[8,2048]{1,0:T(8,128)S(1)}, u32[]{:S(2)}, u32[]{:S(2)}) collective-permute-start(f32[8,2048]{1,0:T(8,128)} %param.12), channel_id=1, source_target_pairs={{0,128},{128,0},{32,160},{160,32},{64,192},{192,64},{96,224},{224,... | collective-permute-start | bytes 196616 | tf_op jit(solution)/shard_map/ppermute | solution.py:22
  12.4 5.5 %collective-permute-start.9 = (f32[2,33,64]{2,1,0:T(8,128)S(1)}, f32[2,33,64]{2,1,0:T(8,128)S(1)}, u32[]{:S(2)}, u32[]{:S(2)}) collective-permute-start(f32[2,33,64]{2,1,0:T(8,128)S(1)} %bitcast.185), channel_id=1, source_target_pairs={{4,0},{5,1},{6,2},{7,3},{0,4},{1,5},{2,6},{3,7},{12,8},{13,9},{14,... | collective-permute-start | bytes 50696 | tf_op jit(solution)/shard_map/ppermute | solution.py:266
  13.3 4.8 %collective-permute-start.10 = (f32[2,33,64]{2,1,0:T(8,128)S(1)}, f32[2,33,64]{2,1,0:T(8,128)S(1)}, u32[]{:S(2)}, u32[]{:S(2)}) collective-permute-start(f32[2,33,64]{2,1,0:T(8,128)S(1)} %bitcast.186), channel_id=1, source_target_pairs={{6,0},{7,1},{0,2},{1,3},{2,4},{3,5},{4,6},{5,7},{14,8},{15,9},{8,1... | collective-permute-start | bytes 50696 | tf_op jit(solution)/shard_map/ppermute | solution.py:266
  18.4 13.6 %collective-permute-start.11 = (f32[8,33,64]{1,2,0:T(8,128)S(1)}, f32[8,33,64]{1,2,0:T(8,128)S(1)}, u32[]{:S(2)}, u32[]{:S(2)}) collective-permute-start(f32[8,33,64]{1,2,0:T(8,128)S(1)} %bitcast.168), channel_id=1, source_target_pairs={{8,0},{9,1},{10,2},{11,3},{12,4},{13,5},{14,6},{15,7},{16,8},{17,9... | collective-permute-start | bytes 202760 | tf_op jit(solution)/shard_map/ppermute | solution.py:266
  19.3 12.7 %collective-permute-start.12 = (f32[8,33,64]{1,2,0:T(8,128)S(1)}, f32[8,33,64]{1,2,0:T(8,128)S(1)}, u32[]{:S(2)}, u32[]{:S(2)}) collective-permute-start(f32[8,33,64]{1,2,0:T(8,128)S(1)} %bitcast.169), channel_id=1, source_target_pairs={{16,0},{17,1},{18,2},{19,3},{20,4},{21,5},{22,6},{23,7},{24,8},{25... | collective-permute-start | bytes 202760 | tf_op jit(solution)/shard_map/ppermute | solution.py:266
  20.4 12.2 %collective-permute-start.13 = (f32[8,33,64]{1,2,0:T(8,128)S(1)}, f32[8,33,64]{1,2,0:T(8,128)S(1)}, u32[]{:S(2)}, u32[]{:S(2)}) collective-permute-start(f32[8,33,64]{1,2,0:T(8,128)S(1)} %bitcast.170), channel_id=1, source_target_pairs={{24,0},{25,1},{26,2},{27,3},{28,4},{29,5},{30,6},{31,7},{0,8},{1,9... | collective-permute-start | bytes 202760 | tf_op jit(solution)/shard_map/ppermute | solution.py:266
  22.6 10.1 %collective-permute-start.1 = (f32[2,8,2048]{2,1,0:T(8,128)S(1)}, f32[2,8,2048]{2,1,0:T(8,128)S(1)}, u32[]{:S(2)}, u32[]{:S(2)}) collective-permute-start(f32[2,8,2048]{2,1,0:T(8,128)S(1)} %pad_maximum_fusion), channel_id=1, source_target_pairs={{0,64},{64,0},{32,96},{96,32},{128,192},{192,128},{160,224},{224,1... | collective-permute-start | bytes 393224 | tf_op jit(solution)/shard_map/ppermute | solution.py:22
  32.8 5.1 %collective-permute-start.2 = (f32[2,8,2048]{2,1,0:T(8,128)S(1)}, f32[2,8,2048]{2,1,0:T(8,128)S(1)}, u32[]{:S(2)}, u32[]{:S(2)}) collective-permute-start(f32[2,8,2048]{2,1,0:T(8,128)S(1)} %pad_maximum_fusion.1), channel_id=1, source_target_pairs={{0,32},{32,0},{64,96},{96,64},{128,160},{160,128},{192,224},{224,1... | collective-permute-start | bytes 393224 | tf_op jit(solution)/shard_map/ppermute | solution.py:22
  41.9 4.7 %collective-permute-start.3 = (f32[2,8,16,128]{3,2,1,0:T(8,128)S(1)}, f32[2,8,16,128]{3,2,1,0:T(8,128)S(1)}, u32[]{:S(2)}, u32[]{:S(2)}) collective-permute-start(f32[2,8,16,128]{3,2,1,0:T(8,128)S(1)} %pad_maximum_fusion.2), channel_id=1, source_target_pairs={{31,0},{0,1},{1,2},{2,3},{3,4},{4,5},{5,6},{6,7},{7,8},{8,9},{9,10... | collective-permute-start | bytes 393224 | tf_op jit(solution)/shard_map/ppermute | solution.py:238
  42.6 6.0 %collective-permute-start.4 = (f32[2,8,16,128]{3,2,1,0:T(8,128)S(1)}, f32[2,8,16,128]{3,2,1,0:T(8,128)S(1)}, u32[]{:S(2)}, u32[]{:S(2)}) collective-permute-start(f32[2,8,16,128]{3,2,1,0:T(8,128)S(1)} %pad_maximum_fusion.2), channel_id=1, source_target_pairs={{1,0},{2,1},{3,2},{4,3},{5,4},{6,5},{7,6},{8,7},{9,8},{10,9},{11,1... | collective-permute-start | bytes 393224 | tf_op jit(solution)/shard_map/ppermute | solution.py:238
  44.3 16.4 %collective-permute-start.5 = (f32[2,8,16,128]{3,2,1,0:T(8,128)S(1)}, f32[2,8,16,128]{3,2,1,0:T(8,128)S(1)}, u32[]{:S(2)}, u32[]{:S(2)}) collective-permute-start(f32[2,8,16,128]{3,2,1,0:T(8,128)S(1)} %pad_maximum_fusion.2), channel_id=1, source_target_pairs={{2,0},{3,1},{4,2},{5,3},{6,4},{7,5},{8,6},{9,7},{10,8},{11,9},{12,... | collective-permute-start | bytes 393224 | tf_op jit(solution)/shard_map/ppermute | solution.py:238
  46.2 14.5 %collective-permute-start.6 = (f32[2,8,16,128]{3,2,1,0:T(8,128)S(1)}, f32[2,8,16,128]{3,2,1,0:T(8,128)S(1)}, u32[]{:S(2)}, u32[]{:S(2)}) collective-permute-start(f32[2,8,16,128]{3,2,1,0:T(8,128)S(1)} %pad_maximum_fusion.2), channel_id=1, source_target_pairs={{3,0},{4,1},{5,2},{6,3},{7,4},{8,5},{9,6},{10,7},{11,8},{12,9},{13... | collective-permute-start | bytes 393224 | tf_op jit(solution)/shard_map/ppermute | solution.py:238
  60.7 0.8 copy-start
  66.8 5.1 %collective-permute-start.14 = (f32[2,8,2048]{2,1,0:T(8,128)S(1)}, f32[2,8,2048]{2,1,0:T(8,128)S(1)}, u32[]{:S(2)}, u32[]{:S(2)}) collective-permute-start(f32[2,8,2048]{2,1,0:T(8,128)S(1)} %pad_maximum_fusion.3), channel_id=1, source_target_pairs={{0,32},{32,0},{64,96},{96,64},{128,160},{160,128},{192,224},{224,1... | collective-permute-start | bytes 393224 | tf_op jit(solution)/shard_map/ppermute | solution.py:22
  71.9 8.1 %collective-permute-start.15 = (f32[2,8,2048]{2,1,0:T(8,128)S(1)}, f32[2,8,2048]{2,1,0:T(8,128)S(1)}, u32[]{:S(2)}, u32[]{:S(2)}) collective-permute-start(f32[2,8,2048]{2,1,0:T(8,128)S(1)} %pad_maximum_fusion.4), channel_id=1, source_target_pairs={{0,64},{64,0},{32,96},{96,32},{128,192},{192,128},{160,224},{224,1... | collective-permute-start | bytes 393224 | tf_op jit(solution)/shard_map/ppermute | solution.py:22
  80.0 8.3 %collective-permute-start.16 = (f32[8,2048]{1,0:T(8,128)S(1)}, f32[8,2048]{1,0:T(8,128)S(1)}, u32[]{:S(2)}, u32[]{:S(2)}) collective-permute-start(f32[8,2048]{1,0:T(8,128)S(1)} %get-tuple-element.13), channel_id=1, source_target_pairs={{0,128},{128,0},{32,160},{160,32},{64,192},{192,64},{96,224},{224,... | collective-permute-start | bytes 196616 | tf_op jit(solution)/shard_map/ppermute | solution.py:22

commit v8 on v6

--- a/solution.py
+++ b/solution.py
@@ -8,8 +8,6 @@
 from jax.experimental import pallas as pl
 from jax.experimental.pallas import tpu as pltpu
 from jax.sharding import PartitionSpec as P
-
-PRECISE = lax.Precision.HIGHEST
 
 
 def from_partner(block, axis, stride):
@@ -27,11 +25,6 @@
     return (jnp.cos(angle), jnp.sin(angle))
 
 
-def dft_table(length):
-    steps = lax.iota(jnp.int32, length)
-    return twiddle(steps[:, None] * steps[None, :] % length, length)
-
-
 def reverse_bits(value, bit_count):
     result = value * 0
     for bit_index in range(bit_count):
@@ -39,75 +32,21 @@
     return result
 
 
-def complex_einsum(form, left_real, left_imag, right_real, right_imag):
-    out_real = jnp.einsum(form, left_real, right_real, precision=PRECISE) - jnp.einsum(
-        form, left_imag, right_imag, precision=PRECISE
-    )
-    out_imag = jnp.einsum(form, left_real, right_imag, precision=PRECISE) + jnp.einsum(
-        form, left_imag, right_real, precision=PRECISE
-    )
-    return (out_real, out_imag)
-
-
-def forward_local(real_part, imag_part, phase_bin, total_len, inner_len):
-    channel_count, length = real_part.shape
-    outer_len = length // inner_len
-    sample_pos = lax.iota(jnp.int32, length)
-    cosine, sine_part = twiddle(sample_pos * phase_bin % total_len, total_len)
-    real_part, imag_part = (
-        real_part * cosine - imag_part * sine_part,
-        real_part * sine_part + imag_part * cosine,
-    )
-    real_part = real_part.reshape(channel_count, inner_len, outer_len)
-    imag_part = imag_part.reshape(channel_count, inner_len, outer_len)
-    table_real, table_imag = dft_table(inner_len)
-    real_part, imag_part = complex_einsum(
-        "cab,ak->cbk", real_part, imag_part, table_real, table_imag
-    )
-    outer_ids = lax.iota(jnp.int32, outer_len)[:, None]
-    inner_ids = lax.iota(jnp.int32, inner_len)[None, :]
-    cosine, sine_part = twiddle(outer_ids * inner_ids, length)
-    real_part, imag_part = (
-        real_part * cosine - imag_part * sine_part,
-        real_part * sine_part + imag_part * cosine,
-    )
-    table_real, table_imag = dft_table(outer_len)
-    return complex_einsum("cbk,bm->mck", real_part, imag_part, table_real, table_imag)
-
-
-def inverse_local(spec_real, spec_imag, phase_bin, total_len):
-    outer_len, channel_count, inner_len = spec_real.shape
-    length = outer_len * inner_len
-    table_real, table_imag = dft_table(outer_len)
-    real_part, imag_part = complex_einsum(
-        "mck,mb->cbk", spec_real, spec_imag, table_real, -table_imag
-    )
-    outer_ids = lax.iota(jnp.int32, outer_len)[:, None]
-    inner_ids = lax.iota(jnp.int32, inner_len)[None, :]
-    cosine, sine_part = twiddle(outer_ids * inner_ids, length)
-    sine_part = -sine_part
-    real_part, imag_part = (
-        real_part * cosine - imag_part * sine_part,
-        real_part * sine_part + imag_part * cosine,
-    )
-    table_real, table_imag = dft_table(inner_len)
-    real_part, imag_part = complex_einsum(
-        "cbk,ka->cab", real_part, imag_part, table_real, -table_imag
-    )
-    real_part = real_part.reshape(channel_count, length)
-    imag_part = imag_part.reshape(channel_count, length)
-    sample_pos = lax.iota(jnp.int32, length)
-    cosine, sine_part = twiddle(sample_pos * phase_bin % total_len, total_len)
-    sine_part = -sine_part
-    return (real_part * cosine - imag_part * sine_part, real_part * sine_part + imag_part * cosine)
-
-
 LANES = 128
+
+
+def split_bf16(value):
+    high = value.astype(jnp.bfloat16)
+    return (high, (value - high.astype(jnp.float32)).astype(jnp.bfloat16))
 
 
 def cdot(left_real, left_imag, right_real, right_imag):
     def dot(a, b):
-        return jnp.dot(a, b, precision=PRECISE, preferred_element_type=jnp.float32)
+        a_high, a_low = split_bf16(a)
+        b_high, b_low = split_bf16(b)
+        total = jnp.dot(a_high, b_low, preferred_element_type=jnp.float32)
+        total = total + jnp.dot(a_low, b_high, preferred_element_type=jnp.float32)
+        return total + jnp.dot(a_high, b_high, preferred_element_type=jnp.float32)
 
     return (
         dot(left_real, right_real) - dot(left_imag, right_imag),
@@ -238,33 +177,25 @@
     return lax.ppermute(block, axis, [((i + delta) % count, i) for i in range(count)])
 
 
-def gather_doubling(block, axis):
-    count = lax.axis_size(axis)
-    me = lax.axis_index(axis)
-    stride = 1
-    while stride < count:
-        partner = from_partner(block, axis, stride.bit_length() - 1)
-        upper = me // stride % 2 == 1
-        block = jnp.where(upper, jnp.concatenate([partner, block]), jnp.concatenate([block, partner]))
-        stride *= 2
-    return block
-
-
-def per_device(signal, band, response, offsets):
+def per_device_body(signal, band, response, offsets):
     blocks = lax.axis_size("tm")
     levels = blocks.bit_length() - 1
     device_pos = lax.axis_index("tm")
-    phase_bin = reverse_bits(device_pos, levels)
     channel_count, length = signal.shape
     total_len = length * blocks
-    inner_len = math.gcd(128, length // lax.axis_size("chan"))
     real_part = signal
     imag_part = jnp.zeros_like(signal)
     for bit_index in range(levels - 1, -1, -1):
         half_span = 1 << bit_index
-        partner = from_partner(jnp.stack([real_part, imag_part]), "tm", bit_index)
         upper_half = device_pos // half_span % 2 == 1
         cosine, sine_part = twiddle(device_pos % half_span, 2 * half_span)
+        if bit_index == levels - 1:
+            partner_real = from_partner(real_part, "tm", bit_index)
+            diff_real = partner_real - real_part
+            imag_part = jnp.where(upper_half, diff_real * sine_part, 0.0)
+            real_part = jnp.where(upper_half, diff_real * cosine, real_part + partner_real)
+            continue
+        partner = from_partner(jnp.stack([real_part, imag_part]), "tm", bit_index)
         diff_real = partner[0] - real_part
         diff_imag = partner[1] - imag_part
         new_real = jnp.where(
@@ -287,9 +218,12 @@
     packed = jnp.concatenate(
         [response.reshape(2 * band_width, -1), offsets.reshape(1, -1).astype(jnp.float32)], axis=0
     )
-    slots = jnp.zeros((lax.axis_size("chan"),) + packed.shape, packed.dtype)
-    table = lax.psum(lax.dynamic_update_index_in_dim(slots, packed, lax.axis_index("chan"), 0), "chan")
+    peers = lax.axis_size("chan")
+    table = lax.all_to_all(
+        jnp.broadcast_to(packed[None], (peers,) + packed.shape), "chan", 0, 0, tiled=True
+    )
     entries = table.shape[1]
+    table, _ = lax.optimization_barrier((table, spec_real))
     table = table.transpose(1, 0, 2).reshape(entries, inner, outer).transpose(0, 2, 1)
     responses = table[: 2 * band_width].reshape(2, band_width, outer, inner)
     shift = (table[2 * band_width].astype(jnp.int32) + half_width) % channel_all - half_width
@@ -301,10 +235,15 @@
     imag_part = imag_part.reshape(own, length)
     for bit_index in range(levels):
         half_span = 1 << bit_index
-        partner = from_partner(jnp.stack([real_part, imag_part]), "tm", bit_index)
         upper_half = device_pos // half_span % 2 == 1
         cosine, sine_part = twiddle(device_pos % half_span, 2 * half_span)
         sine_part = -sine_part
+        if bit_index == levels - 1:
+            own_prod = real_part * cosine - imag_part * sine_part
+            partner_real = from_partner(jnp.where(upper_half, own_prod, real_part), "tm", bit_index)
+            real_part = jnp.where(upper_half, partner_real - own_prod, real_part + partner_real)
+            break
+        partner = from_partner(jnp.stack([real_part, imag_part]), "tm", bit_index)
         base_real = jnp.where(upper_half, partner[0], real_part)
         base_imag = jnp.where(upper_half, partner[1], imag_part)
         scaled_real = jnp.where(upper_half, real_part, partner[0])
@@ -321,5 +260,5 @@
     in_specs = (P("chan", "tm"), P(), P(None, "tm", None, "chan"), P("tm", "chan"))
     out_specs = P("chan", "tm")
     return jax.shard_map(
-        per_device, mesh=mesh, in_specs=in_specs, out_specs=out_specs, check_vma=False
-    )
+        per_device_body, mesh=mesh, in_specs=in_specs, out_specs=out_specs, check_vma=False
+    )

time: 197 us -> 76.7 us (0.39)
  the two profiles are of different devices: /device:TPU:8 before, /device:TPU:30 now
where the time goes in v8:
time: 76.7 us; the launch traced here: 76.1 us
  starting transfers between devices  29.6 us (39%)
  waiting for transfers between devices  29.2 us (38%)
  local copies, waits for them, and re-layouts  7.46 us (10%)
  Pallas kernels  5.63 us (7%)
  other arithmetic  3.73 us (5%)
    ppermute x6, starting transfers between devices, from_partner(): return lax.ppermute(block, axis, route)  18.6 us
    ppermute x6, waiting for transfers between devices, from_partner(): return lax.ppermute(block, axis, route)  15.5 us
    ppermute x4, waiting for transfers between devices, from_offset(): lax.ppermute(block, axis, [((i + delta) % count, i) for i in range(count)])  9.9 us
    all_to_all x1, starting transfers between devices, per_device_body(): lax.all_to_all(jnp.broadcast_to(packed[None], (peers,) + packed.shape), '...  7.31 us
    all_to_all x1, waiting for transfers between devices, per_device_body(): lax.all_to_all(jnp.broadcast_to(packed[None], (peers,) + packed.shape), '...  3.75 us
    ppermute x4, starting transfers between devices, from_offset(): lax.ppermute(block, axis, [((i + delta) % count, i) for i in range(count)])  3.72 us
    unnamed x23, local copies, waits for them, and re-layouts  3.57 us
    pallas_call x1, Pallas kernels, inverse_call(): pl.pallas_call(inverse_kernel, out_shape=(shape, shape), in_specs=specs,...  3.35 us
  transfers between devices with their start and end apart: 11, of which 6 were waited for; matrix products, arithmetic and copies ran while one was open for 8% of the time, Pallas kernels for 0%

profile of v8, /device:TPU:30, one launch (start us, length us, event | category | flops | bytes accessed | tf_op | source)
XLA Modules:
  0.0 76.1 jit_solution(3287789903965094165)
XLA Ops:
  0.0 7.2 %collective-permute-start = (f32[8,2048]{1,0:T(8,128)}, f32[8,2048]{1,0:T(8,128)S(1)}, u32[]{:S(2)}, u32[]{:S(2)}) collective-permute-start(f32[8,2048]{1,0:T(8,128)} %param.12), channel_id=1, source_target_pairs={{0,128},{128,0},{32,160},{160,32},{64,192},{192,64},{96,224},{224,... | collective-permute-start | bytes 196616 | tf_op jit(solution)/shard_map/ppermute | solution.py:20
  7.4 2.5 %collective-permute-done = f32[8,2048]{1,0:T(8,128)S(1)} collective-permute-done((f32[8,2048]{1,0:T(8,128)}, f32[8,2048]{1,0:T(8,128)S(1)}, u32[]{:S(2)}, u32[]{:S(2)}) %collective-permute-start) | collective-permute-done | bytes 65568 | tf_op jit(solution)/shard_map/ppermute | solution.py:20
  9.9 2.9 %collective-permute-start.1 = (f32[2,8,2048]{2,1,0:T(8,128)S(1)}, f32[2,8,2048]{2,1,0:T(8,128)S(1)}, u32[]{:S(2)}, u32[]{:S(2)}) collective-permute-start(f32[2,8,2048]{2,1,0:T(8,128)S(1)} %pad_maximum_fusion), channel_id=1, source_target_pairs={{0,64},{64,0},{32,96},{96,32},{128,192},{192,128},{160,224},{224,1... | collective-permute-start | bytes 393224 | tf_op jit(solution)/shard_map/ppermute | solution.py:20
  13.0 1.1 %reshape.40 = f32[32,1,2112]{2,1,0:T(1,128)} reshape(f32[32,33,64]{2,1,0:T(8,128)S(1)} %broadcast_in_dim.11) | data formatting | bytes 540672
  14.0 7.3 %all-to-all-start = ((f32[32,1,2112]{2,1,0:T(1,128)}), f32[32,1,2112]{2,1,0:T(1,128)S(1)}, u32[]{:S(2)}, u32[]{:S(2)}) async-start(f32[32,1,2112]{2,1,0:T(1,128)} %reshape.40), calls=%async_computation | async-start | bytes 557056 | tf_op jit(solution)/shard_map/all_to_all | solution.py:222
  21.6 0.9 %collective-permute-start.2 = (f32[2,8,2048]{2,1,0:T(8,128)S(1)}, f32[2,8,2048]{2,1,0:T(8,128)S(1)}, u32[]{:S(2)}, u32[]{:S(2)}) collective-permute-start(f32[2,8,2048]{2,1,0:T(8,128)S(1)} %pad_maximum_fusion.1), channel_id=1, source_target_pairs={{0,32},{32,0},{64,96},{96,64},{128,160},{160,128},{192,224},{224,1... | collective-permute-start | bytes 393224 | tf_op jit(solution)/shard_map/ppermute | solution.py:20
  22.6 0.6 copy.19
  23.2 3.8 %all-to-all-done = f32[32,1,2112]{2,1,0:T(1,128)S(1)} async-done(((f32[32,1,2112]{2,1,0:T(1,128)}), f32[32,1,2112]{2,1,0:T(1,128)S(1)}, u32[]{:S(2)}, u32[]{:S(2)}) %all-to-all-start) | async-done | bytes 270368 | tf_op jit(solution)/shard_map/all_to_all | solution.py:222
  26.9 0.5 broadcast.43
  27.4 1.3 %reduce = f32[32,2112]{1,0:T(8,128)S(1)} reduce(f32[32,1,2112]{2,1,0:T(1,128)S(1)} %all-to-all-done, f32[]{:T(128)} %broadcast.43), dimensions={1}, to_apply=%all_to_all.3.reduce_sub_computation | reduce | bytes 540676 | tf_op jit(solution)/shard_map/all_to_all | solution.py:222
  28.9 0.7 copy_bitcast_fusion
  29.6 2.3 %shard_map.118 = (f32[8,16,128]{2,1,0:T(8,128)}, f32[8,16,128]{2,1,0:T(8,128)}) custom-call(f32[8,16,128]{2,1,0:T(8,128)} %get-tuple-element.29.xr_ref, f32[8,16,128]{2,1,0:T(8,128)} %get-tuple-element.28.xi_ref, f32[8,16,128]{2,1,0:T(8,128)} %constant.144.clone.twr_ref, f32[8,16,128]{2,1,0:T(8,128)} %constant.145.clone.twi_ref, ...), custom_call_target="tpu_custom_call" | custom-call | tf_op jit(solution)/shard_map/pallas_call | solution.py:156
  31.9 0.9 %pad_maximum_fusion.2 = f32[2,8,16,128]{3,2,1,0:T(8,128)S(1)} fusion(f32[1,8,16,128]{3,2,1,0:T(8,128)} %bitcast.142, f32[1,8,16,128]{3,2,1,0:T(8,128)} %bitcast.140), kind=kLoop, calls=%fused_computation.2 | loop fusion | flops 32768 | bytes 262144 | tf_op jit(solution)/shard_map/stack | solution.py:230
  32.8 0.5 collective-permute-start.3
  33.3 1.3 %collective-permute-start.4 = (f32[2,8,16,128]{3,2,1,0:T(8,128)S(1)}, f32[2,8,16,128]{3,2,1,0:T(8,128)S(1)}, u32[]{:S(2)}, u32[]{:S(2)}) collective-permute-start(f32[2,8,16,128]{3,2,1,0:T(8,128)S(1)} %pad_maximum_fusion.2), channel_id=1, source_target_pairs={{1,0},{2,1},{3,2},{4,3},{5,4},{6,5},{7,6},{8,7},{9,8},{10,9},{11,1... | collective-permute-start | bytes 393224 | tf_op jit(solution)/shard_map/ppermute | solution.py:177
  34.6 0.7 collective-permute-start.5
  35.3 1.2 %collective-permute-start.6 = (f32[2,8,16,128]{3,2,1,0:T(8,128)S(1)}, f32[2,8,16,128]{3,2,1,0:T(8,128)S(1)}, u32[]{:S(2)}, u32[]{:S(2)}) collective-permute-start(f32[2,8,16,128]{3,2,1,0:T(8,128)S(1)} %pad_maximum_fusion.2), channel_id=1, source_target_pairs={{3,0},{4,1},{5,2},{6,3},{7,4},{8,5},{9,6},{10,7},{11,8},{12,9},{13... | collective-permute-start | bytes 393224 | tf_op jit(solution)/shard_map/ppermute | solution.py:177
  36.9 0.5 copy.16
  37.4 0.7 slice.53
  38.1 0.6 fusion.9.shift_ref
  38.7 0.8 %copy-done.4 = f32[8,16,128]{2,1,0:T(8,128)S(1)} copy-done((f32[8,16,128]{2,1,0:T(8,128)S(1)}, f32[8,16,128]{2,1,0:T(8,128)}, u32[]{:S(2)}) %copy-start.4) | copy-done | bytes 65560
  39.6 9.9 %collective-permute-done.5 = f32[2,8,16,128]{3,2,1,0:T(8,128)S(1)} collective-permute-done((f32[2,8,16,128]{3,2,1,0:T(8,128)S(1)}, f32[2,8,16,128]{3,2,1,0:T(8,128)S(1)}, u32[]{:S(2)}, u32[]{:S(2)}) %collective-permute-start.5) | collective-permute-done | bytes 131104 | tf_op jit(solution)/shard_map/ppermute | solution.py:177
  49.6 0.8 %copy-done = f32[2,40,16,128]{3,2,1,0:T(8,128)} copy-done((f32[2,40,16,128]{3,2,1,0:T(8,128)}, f32[2,40,16,128]{3,2,1,0:T(8,128)S(1)}, u32[]{:S(2)}) %copy-start) | copy-done | bytes 655384
  50.4 3.3 %shard_map.119 = (f32[8,16,128]{2,1,0:T(8,128)}, f32[8,16,128]{2,1,0:T(8,128)}) custom-call(f32[2,40,16,128]{3,2,1,0:T(8,128)} %copy-done, s32[16,128]{1,0:T(8,128)} %fusion.9.shift_ref, f32[2,16,16,128]{3,2,1,0:T(8,128)} %bitcast.135, f32[8192]{0:T(1024)} %bitcast.144, f32[8,16,128]{2,1,0:T(8,128)} %constant.144.clone.twr_ref, ...), custom_call_target="tpu_custom_call" | custom-call | tf_op jit(solution)/shard_map/pallas_call | solution.py:167
  53.8 0.9 %stack_reshape.6 = f32[1,8,2048]{2,1,0:T(8,128)S(1)} reshape(f32[8,16,128]{2,1,0:T(8,128)} %get-tuple-element.13) | data formatting | bytes 131072 | tf_op jit(solution)/shard_map/stack;reshape | solution.py:246
  54.7 0.9 %collective-permute-start.7 = (f32[2,8,2048]{2,1,0:T(8,128)S(1)}, f32[2,8,2048]{2,1,0:T(8,128)S(1)}, u32[]{:S(2)}, u32[]{:S(2)}) collective-permute-start(f32[2,8,2048]{2,1,0:T(8,128)S(1)} %pad_maximum_fusion.3), channel_id=1, source_target_pairs={{0,32},{32,0},{64,96},{96,64},{128,160},{160,128},{192,224},{224,1... | collective-permute-start | bytes 393224 | tf_op jit(solution)/shard_map/ppermute | solution.py:20
  55.6 4.1 %collective-permute-done.7 = f32[2,8,2048]{2,1,0:T(8,128)S(1)} collective-permute-done((f32[2,8,2048]{2,1,0:T(8,128)S(1)}, f32[2,8,2048]{2,1,0:T(8,128)S(1)}, u32[]{:S(2)}, u32[]{:S(2)}) %collective-permute-start.7) | collective-permute-done | bytes 131104 | tf_op jit(solution)/shard_map/ppermute | solution.py:20
  59.8 0.7 collective-permute-start.8
  60.7 6.5 %collective-permute-done.8 = f32[2,8,2048]{2,1,0:T(8,128)S(1)} collective-permute-done((f32[2,8,2048]{2,1,0:T(8,128)S(1)}, f32[2,8,2048]{2,1,0:T(8,128)S(1)}, u32[]{:S(2)}, u32[]{:S(2)}) %collective-permute-start.8) | collective-permute-done | bytes 131104 | tf_op jit(solution)/shard_map/ppermute | solution.py:20
  67.2 5.9 %collective-permute-start.9 = (f32[8,2048]{1,0:T(8,128)S(1)}, f32[8,2048]{1,0:T(8,128)S(1)}, u32[]{:S(2)}, u32[]{:S(2)}) collective-permute-start(f32[8,2048]{1,0:T(8,128)S(1)} %get-tuple-element.15), channel_id=1, source_target_pairs={{0,128},{128,0},{32,160},{160,32},{64,192},{192,64},{96,224},{224,... | collective-permute-start | bytes 196616 | tf_op jit(solution)/shard_map/ppermute | solution.py:20
  73.1 2.4 %collective-permute-done.9 = f32[8,2048]{1,0:T(8,128)S(1)} collective-permute-done((f32[8,2048]{1,0:T(8,128)S(1)}, f32[8,2048]{1,0:T(8,128)S(1)}, u32[]{:S(2)}, u32[]{:S(2)}) %collective-permute-start.9) | collective-permute-done | bytes 65568 | tf_op jit(solution)/shard_map/ppermute | solution.py:20
  75.5 0.6 select_multiply_fusion
  (42 shorter events, 1.1 us)
Async XLA Ops:
  0.0 9.9 %copy-start.3 = (f32[8,2048]{1,0:T(8,128)S(1)}, f32[8,2048]{1,0:T(8,128)}, u32[]{:S(2)}) copy-start(f32[8,2048]{1,0:T(8,128)} %param.12) | copy-start | bytes 196612
  0.0 9.9 %collective-permute-start = (f32[8,2048]{1,0:T(8,128)}, f32[8,2048]{1,0:T(8,128)S(1)}, u32[]{:S(2)}, u32[]{:S(2)}) collective-permute-start(f32[8,2048]{1,0:T(8,128)} %param.12), channel_id=1, source_target_pairs={{0,128},{128,0},{32,160},{160,32},{64,192},{192,64},{96,224},{224,... | collective-permute-start | bytes 196616 | tf_op jit(solution)/shard_map/ppermute | solution.py:20
  9.9 3.0 %copy-start.8 = (s32[1,64]{1,0:T(1,128)S(1)}, s32[1,64]{1,0:T(1,128)}, u32[]{:S(2)}) copy-start(s32[1,64]{1,0:T(1,128)} %param.15) | copy-start | bytes 772
  9.9 3.0 %copy-start.7 = (f32[2,1,16,64]{3,2,1,0:T(8,128)S(1)}, f32[2,1,16,64]{3,2,1,0:T(8,128)}, u32[]{:S(2)}) copy-start(f32[2,1,16,64]{3,2,1,0:T(8,128)} %param.14) | copy-start | bytes 24580
  9.9 11.6 %collective-permute-start.1 = (f32[2,8,2048]{2,1,0:T(8,128)S(1)}, f32[2,8,2048]{2,1,0:T(8,128)S(1)}, u32[]{:S(2)}, u32[]{:S(2)}) collective-permute-start(f32[2,8,2048]{2,1,0:T(8,128)S(1)} %pad_maximum_fusion), channel_id=1, source_target_pairs={{0,64},{64,0},{32,96},{96,32},{128,192},{192,128},{160,224},{224,1... | collective-permute-start | bytes 393224 | tf_op jit(solution)/shard_map/ppermute | solution.py:20
  14.0 12.9 %all-to-all-start = ((f32[32,1,2112]{2,1,0:T(1,128)}), f32[32,1,2112]{2,1,0:T(1,128)S(1)}, u32[]{:S(2)}, u32[]{:S(2)}) async-start(f32[32,1,2112]{2,1,0:T(1,128)} %reshape.40), calls=%async_computation | async-start | bytes 557056 | tf_op jit(solution)/shard_map/all_to_all | solution.py:222
  21.6 1.0 %copy-start.6 = (f32[2,16,256]{2,1,0:T(8,128)S(1)}, f32[2,16,256]{2,1,0:T(8,128)}, u32[]{:S(2)}) copy-start(f32[2,16,256]{2,1,0:T(8,128)} %param.13) | copy-start | bytes 98308
  21.6 7.3 %collective-permute-start.2 = (f32[2,8,2048]{2,1,0:T(8,128)S(1)}, f32[2,8,2048]{2,1,0:T(8,128)S(1)}, u32[]{:S(2)}, u32[]{:S(2)}) collective-permute-start(f32[2,8,2048]{2,1,0:T(8,128)S(1)} %pad_maximum_fusion.1), channel_id=1, source_target_pairs={{0,32},{32,0},{64,96},{96,64},{128,160},{160,128},{192,224},{224,1... | collective-permute-start | bytes 393224 | tf_op jit(solution)/shard_map/ppermute | solution.py:20
  32.8 6.0 %collective-permute-start.3 = (f32[2,8,16,128]{3,2,1,0:T(8,128)S(1)}, f32[2,8,16,128]{3,2,1,0:T(8,128)S(1)}, u32[]{:S(2)}, u32[]{:S(2)}) collective-permute-start(f32[2,8,16,128]{3,2,1,0:T(8,128)S(1)} %pad_maximum_fusion.2), channel_id=1, source_target_pairs={{31,0},{0,1},{1,2},{2,3},{3,4},{4,5},{5,6},{6,7},{7,8},{8,9},{9,10... | collective-permute-start | bytes 393224 | tf_op jit(solution)/shard_map/ppermute | solution.py:177
  33.3 6.3 %collective-permute-start.4 = (f32[2,8,16,128]{3,2,1,0:T(8,128)S(1)}, f32[2,8,16,128]{3,2,1,0:T(8,128)S(1)}, u32[]{:S(2)}, u32[]{:S(2)}) collective-permute-start(f32[2,8,16,128]{3,2,1,0:T(8,128)S(1)} %pad_maximum_fusion.2), channel_id=1, source_target_pairs={{1,0},{2,1},{3,2},{4,3},{5,4},{6,5},{7,6},{8,7},{9,8},{10,9},{11,1... | collective-permute-start | bytes 393224 | tf_op jit(solution)/shard_map/ppermute | solution.py:177
  34.6 14.9 %collective-permute-start.5 = (f32[2,8,16,128]{3,2,1,0:T(8,128)S(1)}, f32[2,8,16,128]{3,2,1,0:T(8,128)S(1)}, u32[]{:S(2)}, u32[]{:S(2)}) collective-permute-start(f32[2,8,16,128]{3,2,1,0:T(8,128)S(1)} %pad_maximum_fusion.2), channel_id=1, source_target_pairs={{2,0},{3,1},{4,2},{5,3},{6,4},{7,5},{8,6},{9,7},{10,8},{11,9},{12,... | collective-permute-start | bytes 393224 | tf_op jit(solution)/shard_map/ppermute | solution.py:177
  35.3 14.3 %collective-permute-start.6 = (f32[2,8,16,128]{3,2,1,0:T(8,128)S(1)}, f32[2,8,16,128]{3,2,1,0:T(8,128)S(1)}, u32[]{:S(2)}, u32[]{:S(2)}) collective-permute-start(f32[2,8,16,128]{3,2,1,0:T(8,128)S(1)} %pad_maximum_fusion.2), channel_id=1, source_target_pairs={{3,0},{4,1},{5,2},{6,3},{7,4},{8,5},{9,6},{10,7},{11,8},{12,9},{13... | collective-permute-start | bytes 393224 | tf_op jit(solution)/shard_map/ppermute | solution.py:177
  38.7 0.8 %copy-start.4 = (f32[8,16,128]{2,1,0:T(8,128)S(1)}, f32[8,16,128]{2,1,0:T(8,128)}, u32[]{:S(2)}) copy-start(f32[8,16,128]{2,1,0:T(8,128)} %get-tuple-element.10) | copy-start | bytes 196612
  38.7 0.9 %copy-start.5 = (f32[8,16,128]{2,1,0:T(8,128)S(1)}, f32[8,16,128]{2,1,0:T(8,128)}, u32[]{:S(2)}) copy-start(f32[8,16,128]{2,1,0:T(8,128)} %get-tuple-element.11) | copy-start | bytes 196612
  49.6 0.8 %copy-start = (f32[2,40,16,128]{3,2,1,0:T(8,128)}, f32[2,40,16,128]{3,2,1,0:T(8,128)S(1)}, u32[]{:S(2)}) copy-start(f32[2,40,16,128]{3,2,1,0:T(8,128)S(1)} %constant_dynamic-update-slice_fusion.win_ref) | copy-start | bytes 1966084
  53.8 0.9 %copy-start.2 = (f32[8,16,128]{2,1,0:T(8,128)S(1)}, f32[8,16,128]{2,1,0:T(8,128)}, u32[]{:S(2)}) copy-start(f32[8,16,128]{2,1,0:T(8,128)} %get-tuple-element.14) | copy-start | bytes 196612
  54.7 5.1 %collective-permute-start.7 = (f32[2,8,2048]{2,1,0:T(8,128)S(1)}, f32[2,8,2048]{2,1,0:T(8,128)S(1)}, u32[]{:S(2)}, u32[]{:S(2)}) collective-permute-start(f32[2,8,2048]{2,1,0:T(8,128)S(1)} %pad_maximum_fusion.3), channel_id=1, source_target_pairs={{0,32},{32,0},{64,96},{96,64},{128,160},{160,128},{192,224},{224,1... | collective-permute-start | bytes 393224 | tf_op jit(solution)/shard_map/ppermute | solution.py:20
  59.8 0.8 %copy-start.1 = (f32[8,16,128]{2,1,0:T(8,128)S(1)}, f32[8,16,128]{2,1,0:T(8,128)}, u32[]{:S(2)}) copy-start(f32[8,16,128]{2,1,0:T(8,128)} %get-tuple-element.13) | copy-start | bytes 196612
  59.8 7.4 %collective-permute-start.8 = (f32[2,8,2048]{2,1,0:T(8,128)S(1)}, f32[2,8,2048]{2,1,0:T(8,128)S(1)}, u32[]{:S(2)}, u32[]{:S(2)}) collective-permute-start(f32[2,8,2048]{2,1,0:T(8,128)S(1)} %pad_maximum_fusion.4), channel_id=1, source_target_pairs={{0,64},{64,0},{32,96},{96,32},{128,192},{192,128},{160,224},{224,1... | collective-permute-start | bytes 393224 | tf_op jit(solution)/shard_map/ppermute | solution.py:20
  67.2 8.3 %collective-permute-start.9 = (f32[8,2048]{1,0:T(8,128)S(1)}, f32[8,2048]{1,0:T(8,128)S(1)}, u32[]{:S(2)}, u32[]{:S(2)}) collective-permute-start(f32[8,2048]{1,0:T(8,128)S(1)} %get-tuple-element.15), channel_id=1, source_target_pairs={{0,128},{128,0},{32,160},{160,32},{64,192},{192,64},{96,224},{224,... | collective-permute-start | bytes 196616 | tf_op jit(solution)/shard_map/ppermute | solution.py:20

commit v9 on v8

--- a/solution.py
+++ b/solution.py
@@ -8,6 +8,9 @@
 from jax.experimental import pallas as pl
 from jax.experimental.pallas import tpu as pltpu
 from jax.sharding import PartitionSpec as P
+
+
+PRECISE = lax.Precision.HIGHEST
 
 
 def from_partner(block, axis, stride):
@@ -35,18 +38,9 @@
 LANES = 128
 
 
-def split_bf16(value):
-    high = value.astype(jnp.bfloat16)
-    return (high, (value - high.astype(jnp.float32)).astype(jnp.bfloat16))
-
-
 def cdot(left_real, left_imag, right_real, right_imag):
     def dot(a, b):
-        a_high, a_low = split_bf16(a)
-        b_high, b_low = split_bf16(b)
-        total = jnp.dot(a_high, b_low, preferred_element_type=jnp.float32)
-        total = total + jnp.dot(a_low, b_high, preferred_element_type=jnp.float32)
-        return total + jnp.dot(a_high, b_high, preferred_element_type=jnp.float32)
+        return jnp.dot(a, b, precision=PRECISE, preferred_element_type=jnp.float32)
 
     return (
         dot(left_real, right_real) - dot(left_imag, right_imag),

time: 76.7 us -> 77 us (level)
  no operation moved by 1% of the time
where the time goes in v9:
time: 77 us; the launch traced here: 76.5 us
  starting transfers between devices  29.6 us (38%)
  waiting for transfers between devices  29.2 us (38%)
  local copies, waits for them, and re-layouts  7.46 us (10%)
  Pallas kernels  5.96 us (8%)
  other arithmetic  3.73 us (5%)
    ppermute x6, starting transfers between devices, from_partner(): return lax.ppermute(block, axis, route)  18.6 us
    ppermute x6, waiting for transfers between devices, from_partner(): return lax.ppermute(block, axis, route)  15.5 us
    ppermute x4, waiting for transfers between devices, from_offset(): lax.ppermute(block, axis, [((i + delta) % count, i) for i in range(count)])  9.9 us
    all_to_all x1, starting transfers between devices, per_device_body(): lax.all_to_all(jnp.broadcast_to(packed[None], (peers,) + packed.shape), '...  7.31 us
    all_to_all x1, waiting for transfers between devices, per_device_body(): lax.all_to_all(jnp.broadcast_to(packed[None], (peers,) + packed.shape), '...  3.75 us
    ppermute x4, starting transfers between devices, from_offset(): lax.ppermute(block, axis, [((i + delta) % count, i) for i in range(count)])  3.72 us
    unnamed x23, local copies, waits for them, and re-layouts  3.57 us
    pallas_call x1, Pallas kernels, inverse_call(): pl.pallas_call(inverse_kernel, out_shape=(shape, shape), in_specs=specs,...  3.47 us
  transfers between devices with their start and end apart: 11, of which 6 were waited for; matrix products, arithmetic and copies ran while one was open for 8% of the time, Pallas kernels for 0%

profile of v9, /device:TPU:30, one launch (start us, length us, event | category | flops | bytes accessed | tf_op | source)
XLA Modules:
  0.0 76.5 jit_solution(8593662043404505314)
XLA Ops:
  0.0 7.2 %collective-permute-start = (f32[8,2048]{1,0:T(8,128)}, f32[8,2048]{1,0:T(8,128)S(1)}, u32[]{:S(2)}, u32[]{:S(2)}) collective-permute-start(f32[8,2048]{1,0:T(8,128)} %param.12), channel_id=1, source_target_pairs={{0,128},{128,0},{32,160},{160,32},{64,192},{192,64},{96,224},{224,... | collective-permute-start | bytes 196616 | tf_op jit(solution)/shard_map/ppermute | solution.py:23
  7.4 2.5 %collective-permute-done = f32[8,2048]{1,0:T(8,128)S(1)} collective-permute-done((f32[8,2048]{1,0:T(8,128)}, f32[8,2048]{1,0:T(8,128)S(1)}, u32[]{:S(2)}, u32[]{:S(2)}) %collective-permute-start) | collective-permute-done | bytes 65568 | tf_op jit(solution)/shard_map/ppermute | solution.py:23
  9.9 2.9 %collective-permute-start.1 = (f32[2,8,2048]{2,1,0:T(8,128)S(1)}, f32[2,8,2048]{2,1,0:T(8,128)S(1)}, u32[]{:S(2)}, u32[]{:S(2)}) collective-permute-start(f32[2,8,2048]{2,1,0:T(8,128)S(1)} %pad_maximum_fusion), channel_id=1, source_target_pairs={{0,64},{64,0},{32,96},{96,32},{128,192},{192,128},{160,224},{224,1... | collective-permute-start | bytes 393224 | tf_op jit(solution)/shard_map/ppermute | solution.py:23
  13.0 1.1 %reshape.40 = f32[32,1,2112]{2,1,0:T(1,128)} reshape(f32[32,33,64]{2,1,0:T(8,128)S(1)} %broadcast_in_dim.11) | data formatting | bytes 540672
  14.0 7.3 %all-to-all-start = ((f32[32,1,2112]{2,1,0:T(1,128)}), f32[32,1,2112]{2,1,0:T(1,128)S(1)}, u32[]{:S(2)}, u32[]{:S(2)}) async-start(f32[32,1,2112]{2,1,0:T(1,128)} %reshape.40), calls=%async_computation | async-start | bytes 557056 | tf_op jit(solution)/shard_map/all_to_all | solution.py:216
  21.6 0.9 %collective-permute-start.2 = (f32[2,8,2048]{2,1,0:T(8,128)S(1)}, f32[2,8,2048]{2,1,0:T(8,128)S(1)}, u32[]{:S(2)}, u32[]{:S(2)}) collective-permute-start(f32[2,8,2048]{2,1,0:T(8,128)S(1)} %pad_maximum_fusion.1), channel_id=1, source_target_pairs={{0,32},{32,0},{64,96},{96,64},{128,160},{160,128},{192,224},{224,1... | collective-permute-start | bytes 393224 | tf_op jit(solution)/shard_map/ppermute | solution.py:23
  22.6 0.6 copy.19
  23.2 3.8 %all-to-all-done = f32[32,1,2112]{2,1,0:T(1,128)S(1)} async-done(((f32[32,1,2112]{2,1,0:T(1,128)}), f32[32,1,2112]{2,1,0:T(1,128)S(1)}, u32[]{:S(2)}, u32[]{:S(2)}) %all-to-all-start) | async-done | bytes 270368 | tf_op jit(solution)/shard_map/all_to_all | solution.py:216
  26.9 0.5 broadcast.43
  27.4 1.3 %reduce = f32[32,2112]{1,0:T(8,128)S(1)} reduce(f32[32,1,2112]{2,1,0:T(1,128)S(1)} %all-to-all-done, f32[]{:T(128)} %broadcast.43), dimensions={1}, to_apply=%all_to_all.3.reduce_sub_computation | reduce | bytes 540676 | tf_op jit(solution)/shard_map/all_to_all | solution.py:216
  28.9 0.7 copy_bitcast_fusion
  29.6 2.5 %shard_map.118 = (f32[8,16,128]{2,1,0:T(8,128)}, f32[8,16,128]{2,1,0:T(8,128)}) custom-call(f32[8,16,128]{2,1,0:T(8,128)} %get-tuple-element.29.xr_ref, f32[8,16,128]{2,1,0:T(8,128)} %get-tuple-element.28.xi_ref, f32[8,16,128]{2,1,0:T(8,128)} %constant.144.clone.twr_ref, f32[8,16,128]{2,1,0:T(8,128)} %constant.145.clone.twi_ref, ...), custom_call_target="tpu_custom_call" | custom-call | tf_op jit(solution)/shard_map/pallas_call | solution.py:150
  32.1 0.9 %pad_maximum_fusion.2 = f32[2,8,16,128]{3,2,1,0:T(8,128)S(1)} fusion(f32[1,8,16,128]{3,2,1,0:T(8,128)} %bitcast.142, f32[1,8,16,128]{3,2,1,0:T(8,128)} %bitcast.140), kind=kLoop, calls=%fused_computation.2 | loop fusion | flops 32768 | bytes 262144 | tf_op jit(solution)/shard_map/stack | solution.py:224
  33.0 0.5 collective-permute-start.3
  33.5 1.3 %collective-permute-start.4 = (f32[2,8,16,128]{3,2,1,0:T(8,128)S(1)}, f32[2,8,16,128]{3,2,1,0:T(8,128)S(1)}, u32[]{:S(2)}, u32[]{:S(2)}) collective-permute-start(f32[2,8,16,128]{3,2,1,0:T(8,128)S(1)} %pad_maximum_fusion.2), channel_id=1, source_target_pairs={{1,0},{2,1},{3,2},{4,3},{5,4},{6,5},{7,6},{8,7},{9,8},{10,9},{11,1... | collective-permute-start | bytes 393224 | tf_op jit(solution)/shard_map/ppermute | solution.py:171
  34.8 0.7 collective-permute-start.5
  35.5 1.2 %collective-permute-start.6 = (f32[2,8,16,128]{3,2,1,0:T(8,128)S(1)}, f32[2,8,16,128]{3,2,1,0:T(8,128)S(1)}, u32[]{:S(2)}, u32[]{:S(2)}) collective-permute-start(f32[2,8,16,128]{3,2,1,0:T(8,128)S(1)} %pad_maximum_fusion.2), channel_id=1, source_target_pairs={{3,0},{4,1},{5,2},{6,3},{7,4},{8,5},{9,6},{10,7},{11,8},{12,9},{13... | collective-permute-start | bytes 393224 | tf_op jit(solution)/shard_map/ppermute | solution.py:171
  37.1 0.5 copy.16
  37.6 0.7 slice.53
  38.3 0.6 fusion.9.shift_ref
  38.9 0.8 %copy-done.4 = f32[8,16,128]{2,1,0:T(8,128)S(1)} copy-done((f32[8,16,128]{2,1,0:T(8,128)S(1)}, f32[8,16,128]{2,1,0:T(8,128)}, u32[]{:S(2)}) %copy-start.4) | copy-done | bytes 65560
  39.8 9.9 %collective-permute-done.5 = f32[2,8,16,128]{3,2,1,0:T(8,128)S(1)} collective-permute-done((f32[2,8,16,128]{3,2,1,0:T(8,128)S(1)}, f32[2,8,16,128]{3,2,1,0:T(8,128)S(1)}, u32[]{:S(2)}, u32[]{:S(2)}) %collective-permute-start.5) | collective-permute-done | bytes 131104 | tf_op jit(solution)/shard_map/ppermute | solution.py:171
  49.8 0.8 %copy-done = f32[2,40,16,128]{3,2,1,0:T(8,128)} copy-done((f32[2,40,16,128]{3,2,1,0:T(8,128)}, f32[2,40,16,128]{3,2,1,0:T(8,128)S(1)}, u32[]{:S(2)}) %copy-start) | copy-done | bytes 655384
  50.6 3.5 %shard_map.119 = (f32[8,16,128]{2,1,0:T(8,128)}, f32[8,16,128]{2,1,0:T(8,128)}) custom-call(f32[2,40,16,128]{3,2,1,0:T(8,128)} %copy-done, s32[16,128]{1,0:T(8,128)} %fusion.9.shift_ref, f32[2,16,16,128]{3,2,1,0:T(8,128)} %bitcast.135, f32[8192]{0:T(1024)} %bitcast.144, f32[8,16,128]{2,1,0:T(8,128)} %constant.144.clone.twr_ref, ...), custom_call_target="tpu_custom_call" | custom-call | tf_op jit(solution)/shard_map/pallas_call | solution.py:161
  54.1 0.9 %stack_reshape.6 = f32[1,8,2048]{2,1,0:T(8,128)S(1)} reshape(f32[8,16,128]{2,1,0:T(8,128)} %get-tuple-element.13) | data formatting | bytes 131072 | tf_op jit(solution)/shard_map/stack;reshape | solution.py:240
  55.0 0.9 %collective-permute-start.7 = (f32[2,8,2048]{2,1,0:T(8,128)S(1)}, f32[2,8,2048]{2,1,0:T(8,128)S(1)}, u32[]{:S(2)}, u32[]{:S(2)}) collective-permute-start(f32[2,8,2048]{2,1,0:T(8,128)S(1)} %pad_maximum_fusion.3), channel_id=1, source_target_pairs={{0,32},{32,0},{64,96},{96,64},{128,160},{160,128},{192,224},{224,1... | collective-permute-start | bytes 393224 | tf_op jit(solution)/shard_map/ppermute | solution.py:23
  56.0 4.1 %collective-permute-done.7 = f32[2,8,2048]{2,1,0:T(8,128)S(1)} collective-permute-done((f32[2,8,2048]{2,1,0:T(8,128)S(1)}, f32[2,8,2048]{2,1,0:T(8,128)S(1)}, u32[]{:S(2)}, u32[]{:S(2)}) %collective-permute-start.7) | collective-permute-done | bytes 131104 | tf_op jit(solution)/shard_map/ppermute | solution.py:23
  60.2 0.7 collective-permute-start.8
  61.0 6.5 %collective-permute-done.8 = f32[2,8,2048]{2,1,0:T(8,128)S(1)} collective-permute-done((f32[2,8,2048]{2,1,0:T(8,128)S(1)}, f32[2,8,2048]{2,1,0:T(8,128)S(1)}, u32[]{:S(2)}, u32[]{:S(2)}) %collective-permute-start.8) | collective-permute-done | bytes 131104 | tf_op jit(solution)/shard_map/ppermute | solution.py:23
  67.6 5.9 %collective-permute-start.9 = (f32[8,2048]{1,0:T(8,128)S(1)}, f32[8,2048]{1,0:T(8,128)S(1)}, u32[]{:S(2)}, u32[]{:S(2)}) collective-permute-start(f32[8,2048]{1,0:T(8,128)S(1)} %get-tuple-element.15), channel_id=1, source_target_pairs={{0,128},{128,0},{32,160},{160,32},{64,192},{192,64},{96,224},{224,... | collective-permute-start | bytes 196616 | tf_op jit(solution)/shard_map/ppermute | solution.py:23
  73.5 2.4 %collective-permute-done.9 = f32[8,2048]{1,0:T(8,128)S(1)} collective-permute-done((f32[8,2048]{1,0:T(8,128)S(1)}, f32[8,2048]{1,0:T(8,128)S(1)}, u32[]{:S(2)}, u32[]{:S(2)}) %collective-permute-start.9) | collective-permute-done | bytes 65568 | tf_op jit(solution)/shard_map/ppermute | solution.py:23
  75.8 0.6 select_multiply_fusion
  (42 shorter events, 1.1 us)
Async XLA Ops:
  0.0 9.9 %copy-start.3 = (f32[8,2048]{1,0:T(8,128)S(1)}, f32[8,2048]{1,0:T(8,128)}, u32[]{:S(2)}) copy-start(f32[8,2048]{1,0:T(8,128)} %param.12) | copy-start | bytes 196612
  0.0 9.9 %collective-permute-start = (f32[8,2048]{1,0:T(8,128)}, f32[8,2048]{1,0:T(8,128)S(1)}, u32[]{:S(2)}, u32[]{:S(2)}) collective-permute-start(f32[8,2048]{1,0:T(8,128)} %param.12), channel_id=1, source_target_pairs={{0,128},{128,0},{32,160},{160,32},{64,192},{192,64},{96,224},{224,... | collective-permute-start | bytes 196616 | tf_op jit(solution)/shard_map/ppermute | solution.py:23
  9.9 3.0 %copy-start.8 = (s32[1,64]{1,0:T(1,128)S(1)}, s32[1,64]{1,0:T(1,128)}, u32[]{:S(2)}) copy-start(s32[1,64]{1,0:T(1,128)} %param.15) | copy-start | bytes 772
  9.9 3.0 %copy-start.7 = (f32[2,1,16,64]{3,2,1,0:T(8,128)S(1)}, f32[2,1,16,64]{3,2,1,0:T(8,128)}, u32[]{:S(2)}) copy-start(f32[2,1,16,64]{3,2,1,0:T(8,128)} %param.14) | copy-start | bytes 24580
  9.9 11.6 %collective-permute-start.1 = (f32[2,8,2048]{2,1,0:T(8,128)S(1)}, f32[2,8,2048]{2,1,0:T(8,128)S(1)}, u32[]{:S(2)}, u32[]{:S(2)}) collective-permute-start(f32[2,8,2048]{2,1,0:T(8,128)S(1)} %pad_maximum_fusion), channel_id=1, source_target_pairs={{0,64},{64,0},{32,96},{96,32},{128,192},{192,128},{160,224},{224,1... | collective-permute-start | bytes 393224 | tf_op jit(solution)/shard_map/ppermute | solution.py:23
  14.0 12.9 %all-to-all-start = ((f32[32,1,2112]{2,1,0:T(1,128)}), f32[32,1,2112]{2,1,0:T(1,128)S(1)}, u32[]{:S(2)}, u32[]{:S(2)}) async-start(f32[32,1,2112]{2,1,0:T(1,128)} %reshape.40), calls=%async_computation | async-start | bytes 557056 | tf_op jit(solution)/shard_map/all_to_all | solution.py:216
  21.6 1.0 %copy-start.6 = (f32[2,16,256]{2,1,0:T(8,128)S(1)}, f32[2,16,256]{2,1,0:T(8,128)}, u32[]{:S(2)}) copy-start(f32[2,16,256]{2,1,0:T(8,128)} %param.13) | copy-start | bytes 98308
  21.6 7.3 %collective-permute-start.2 = (f32[2,8,2048]{2,1,0:T(8,128)S(1)}, f32[2,8,2048]{2,1,0:T(8,128)S(1)}, u32[]{:S(2)}, u32[]{:S(2)}) collective-permute-start(f32[2,8,2048]{2,1,0:T(8,128)S(1)} %pad_maximum_fusion.1), channel_id=1, source_target_pairs={{0,32},{32,0},{64,96},{96,64},{128,160},{160,128},{192,224},{224,1... | collective-permute-start | bytes 393224 | tf_op jit(solution)/shard_map/ppermute | solution.py:23
  33.0 6.0 %collective-permute-start.3 = (f32[2,8,16,128]{3,2,1,0:T(8,128)S(1)}, f32[2,8,16,128]{3,2,1,0:T(8,128)S(1)}, u32[]{:S(2)}, u32[]{:S(2)}) collective-permute-start(f32[2,8,16,128]{3,2,1,0:T(8,128)S(1)} %pad_maximum_fusion.2), channel_id=1, source_target_pairs={{31,0},{0,1},{1,2},{2,3},{3,4},{4,5},{5,6},{6,7},{7,8},{8,9},{9,10... | collective-permute-start | bytes 393224 | tf_op jit(solution)/shard_map/ppermute | solution.py:171
  33.5 6.3 %collective-permute-start.4 = (f32[2,8,16,128]{3,2,1,0:T(8,128)S(1)}, f32[2,8,16,128]{3,2,1,0:T(8,128)S(1)}, u32[]{:S(2)}, u32[]{:S(2)}) collective-permute-start(f32[2,8,16,128]{3,2,1,0:T(8,128)S(1)} %pad_maximum_fusion.2), channel_id=1, source_target_pairs={{1,0},{2,1},{3,2},{4,3},{5,4},{6,5},{7,6},{8,7},{9,8},{10,9},{11,1... | collective-permute-start | bytes 393224 | tf_op jit(solution)/shard_map/ppermute | solution.py:171
  34.8 14.9 %collective-permute-start.5 = (f32[2,8,16,128]{3,2,1,0:T(8,128)S(1)}, f32[2,8,16,128]{3,2,1,0:T(8,128)S(1)}, u32[]{:S(2)}, u32[]{:S(2)}) collective-permute-start(f32[2,8,16,128]{3,2,1,0:T(8,128)S(1)} %pad_maximum_fusion.2), channel_id=1, source_target_pairs={{2,0},{3,1},{4,2},{5,3},{6,4},{7,5},{8,6},{9,7},{10,8},{11,9},{12,... | collective-permute-start | bytes 393224 | tf_op jit(solution)/shard_map/ppermute | solution.py:171
  35.5 14.3 %collective-permute-start.6 = (f32[2,8,16,128]{3,2,1,0:T(8,128)S(1)}, f32[2,8,16,128]{3,2,1,0:T(8,128)S(1)}, u32[]{:S(2)}, u32[]{:S(2)}) collective-permute-start(f32[2,8,16,128]{3,2,1,0:T(8,128)S(1)} %pad_maximum_fusion.2), channel_id=1, source_target_pairs={{3,0},{4,1},{5,2},{6,3},{7,4},{8,5},{9,6},{10,7},{11,8},{12,9},{13... | collective-permute-start | bytes 393224 | tf_op jit(solution)/shard_map/ppermute | solution.py:171
  38.9 0.8 %copy-start.4 = (f32[8,16,128]{2,1,0:T(8,128)S(1)}, f32[8,16,128]{2,1,0:T(8,128)}, u32[]{:S(2)}) copy-start(f32[8,16,128]{2,1,0:T(8,128)} %get-tuple-element.10) | copy-start | bytes 196612
  38.9 0.9 %copy-start.5 = (f32[8,16,128]{2,1,0:T(8,128)S(1)}, f32[8,16,128]{2,1,0:T(8,128)}, u32[]{:S(2)}) copy-start(f32[8,16,128]{2,1,0:T(8,128)} %get-tuple-element.11) | copy-start | bytes 196612
  49.8 0.8 %copy-start = (f32[2,40,16,128]{3,2,1,0:T(8,128)}, f32[2,40,16,128]{3,2,1,0:T(8,128)S(1)}, u32[]{:S(2)}) copy-start(f32[2,40,16,128]{3,2,1,0:T(8,128)S(1)} %constant_dynamic-update-slice_fusion.win_ref) | copy-start | bytes 1966084
  54.1 0.9 %copy-start.2 = (f32[8,16,128]{2,1,0:T(8,128)S(1)}, f32[8,16,128]{2,1,0:T(8,128)}, u32[]{:S(2)}) copy-start(f32[8,16,128]{2,1,0:T(8,128)} %get-tuple-element.14) | copy-start | bytes 196612
  55.0 5.1 %collective-permute-start.7 = (f32[2,8,2048]{2,1,0:T(8,128)S(1)}, f32[2,8,2048]{2,1,0:T(8,128)S(1)}, u32[]{:S(2)}, u32[]{:S(2)}) collective-permute-start(f32[2,8,2048]{2,1,0:T(8,128)S(1)} %pad_maximum_fusion.3), channel_id=1, source_target_pairs={{0,32},{32,0},{64,96},{96,64},{128,160},{160,128},{192,224},{224,1... | collective-permute-start | bytes 393224 | tf_op jit(solution)/shard_map/ppermute | solution.py:23
  60.1 0.8 %copy-start.1 = (f32[8,16,128]{2,1,0:T(8,128)S(1)}, f32[8,16,128]{2,1,0:T(8,128)}, u32[]{:S(2)}) copy-start(f32[8,16,128]{2,1,0:T(8,128)} %get-tuple-element.13) | copy-start | bytes 196612
  60.2 7.4 %collective-permute-start.8 = (f32[2,8,2048]{2,1,0:T(8,128)S(1)}, f32[2,8,2048]{2,1,0:T(8,128)S(1)}, u32[]{:S(2)}, u32[]{:S(2)}) collective-permute-start(f32[2,8,2048]{2,1,0:T(8,128)S(1)} %pad_maximum_fusion.4), channel_id=1, source_target_pairs={{0,64},{64,0},{32,96},{96,32},{128,192},{192,128},{160,224},{224,1... | collective-permute-start | bytes 393224 | tf_op jit(solution)/shard_map/ppermute | solution.py:23
  67.6 8.3 %collective-permute-start.9 = (f32[8,2048]{1,0:T(8,128)S(1)}, f32[8,2048]{1,0:T(8,128)S(1)}, u32[]{:S(2)}, u32[]{:S(2)}) collective-permute-start(f32[8,2048]{1,0:T(8,128)S(1)} %get-tuple-element.15), channel_id=1, source_target_pairs={{0,128},{128,0},{32,160},{160,32},{64,192},{192,64},{96,224},{224,... | collective-permute-start | bytes 196616 | tf_op jit(solution)/shard_map/ppermute | solution.py:23

commit v10 on v9

--- a/solution.py
+++ b/solution.py
@@ -48,7 +48,7 @@
     )
 
 
-def forward_kernel(xr_ref, xi_ref, twr_ref, twi_ref, kr_ref, ki_ref, t2r_ref, t2i_ref, wr_ref, wi_ref, yr_ref, yi_ref):
+def forward_kernel(xr_ref, xi_ref, twr_ref, twi_ref, kr_ref, ki_ref, t2r_ref, t2i_ref, wr_ref, wi_ref, y_ref):
     own, outer, inner = xr_ref.shape
     xr = xr_ref[...]
     xi = xi_ref[...]
@@ -62,8 +62,8 @@
     t2i = t2i_ref[...]
     zr, zi = (zr * t2r - zi * t2i, zr * t2i + zi * t2r)
     yr, yi = cdot(zr, zi, wr_ref[...], wi_ref[...])
-    yr_ref[...] = yr.reshape(own, outer, inner)
-    yi_ref[...] = yi.reshape(own, outer, inner)
+    y_ref[0] = yr.reshape(own, outer, inner)
+    y_ref[1] = yi.reshape(own, outer, inner)
 
 
 def inverse_kernel(win_ref, shift_ref, resp_ref, band_ref, twr_ref, twi_ref, kr_ref, ki_ref, t2r_ref, t2i_ref, wr_ref, wi_ref, xr_ref, xi_ref):
@@ -146,12 +146,13 @@
 
 
 def forward_call(xr, xi, tables):
-    shape = jax.ShapeDtypeStruct(xr.shape, jnp.float32)
+    shape = jax.ShapeDtypeStruct((2,) + xr.shape, jnp.float32)
     return pl.pallas_call(
         forward_kernel,
-        out_shape=(shape, shape),
+        out_shape=shape,
         in_specs=vmem_specs(2 + len(tables)),
-        out_specs=tuple(vmem_specs(2)),
+        out_specs=pl.BlockSpec(memory_space=pltpu.VMEM),
+        compiler_params=pltpu.CompilerParams(allow_input_fusion=[True, True] + [False] * len(tables)),
     )(xr, xi, *tables)
 
 
@@ -206,7 +207,7 @@
     half_width = band_width // 2
     channel_all = band.shape[2]
     tables = local_tables(own, outer, inner, blocks, levels)
-    spec_real, spec_imag = forward_call(
+    spectra = forward_call(
         real_part.reshape(own, outer, inner), imag_part.reshape(own, outer, inner), tables
     )
     packed = jnp.concatenate(
@@ -217,11 +218,10 @@
         jnp.broadcast_to(packed[None], (peers,) + packed.shape), "chan", 0, 0, tiled=True
     )
     entries = table.shape[1]
-    table, _ = lax.optimization_barrier((table, spec_real))
+    table, _ = lax.optimization_barrier((table, spectra))
     table = table.transpose(1, 0, 2).reshape(entries, inner, outer).transpose(0, 2, 1)
     responses = table[: 2 * band_width].reshape(2, band_width, outer, inner)
     shift = (table[2 * band_width].astype(jnp.int32) + half_width) % channel_all - half_width
-    spectra = jnp.stack([spec_real, spec_imag])
     neighbours = [from_offset(spectra, "chan", delta) for delta in (-1, 1, 2, 3)]
     window = jnp.concatenate([neighbours[0], spectra] + neighbours[1:], axis=1)
     real_part, imag_part = inverse_call(window, shift, responses, band.reshape(-1), tables, own)

time: 77 us -> 76.2 us (0.990)
  other arithmetic: 3.73 us -> 2.83 us
    another operation x1 -> x0, other arithmetic: 0.88 us -> none  [per_device_body(): spectra = jnp.stack([spec_real, spec_imag])]
    unnamed x23 -> x22, local copies, waits for them, and re-layouts: 3.57 us -> 3.63 us
where the time goes in v10:
time: 76.2 us; the launch traced here: 75.7 us
  starting transfers between devices  29.5 us (39%)
  waiting for transfers between devices  29.3 us (38%)
  local copies, waits for them, and re-layouts  7.54 us (10%)
  Pallas kernels  5.95 us (8%)
  other arithmetic  2.83 us (4%)
    ppermute x6, starting transfers between devices, from_partner(): return lax.ppermute(block, axis, route)  18.6 us
    ppermute x6, waiting for transfers between devices, from_partner(): return lax.ppermute(block, axis, route)  15.5 us
    ppermute x4, waiting for transfers between devices, from_offset(): lax.ppermute(block, axis, [((i + delta) % count, i) for i in range(count)])  10.1 us
    all_to_all x1, starting transfers between devices, per_device_body(): lax.all_to_all(jnp.broadcast_to(packed[None], (peers,) + packed.shape), '...  7.31 us
    all_to_all x1, waiting for transfers between devices, per_device_body(): lax.all_to_all(jnp.broadcast_to(packed[None], (peers,) + packed.shape), '...  3.75 us
    ppermute x4, starting transfers between devices, from_offset(): lax.ppermute(block, axis, [((i + delta) % count, i) for i in range(count)])  3.64 us
    unnamed x22, local copies, waits for them, and re-layouts  3.63 us
    pallas_call x1, Pallas kernels, inverse_call(): pl.pallas_call(inverse_kernel, out_shape=(shape, shape), in_specs=specs,...  3.47 us
  transfers between devices with their start and end apart: 11, of which 6 were waited for; matrix products, arithmetic and copies ran while one was open for 8% of the time, Pallas kernels for 0%

profile of v10, /device:TPU:30, one launch (start us, length us, event | category | flops | bytes accessed | tf_op | source)
XLA Modules:
  0.0 75.7 jit_solution(18065773688300231884)
XLA Ops:
  0.0 7.2 %collective-permute-start = (f32[8,2048]{1,0:T(8,128)}, f32[8,2048]{1,0:T(8,128)S(1)}, u32[]{:S(2)}, u32[]{:S(2)}) collective-permute-start(f32[8,2048]{1,0:T(8,128)} %param.12), channel_id=1, source_target_pairs={{0,128},{128,0},{32,160},{160,32},{64,192},{192,64},{96,224},{224,... | collective-permute-start | bytes 196616 | tf_op jit(solution)/shard_map/ppermute | solution.py:23
  7.4 2.5 %collective-permute-done = f32[8,2048]{1,0:T(8,128)S(1)} collective-permute-done((f32[8,2048]{1,0:T(8,128)}, f32[8,2048]{1,0:T(8,128)S(1)}, u32[]{:S(2)}, u32[]{:S(2)}) %collective-permute-start) | collective-permute-done | bytes 65568 | tf_op jit(solution)/shard_map/ppermute | solution.py:23
  9.9 2.9 %collective-permute-start.1 = (f32[2,8,2048]{2,1,0:T(8,128)S(1)}, f32[2,8,2048]{2,1,0:T(8,128)S(1)}, u32[]{:S(2)}, u32[]{:S(2)}) collective-permute-start(f32[2,8,2048]{2,1,0:T(8,128)S(1)} %pad_maximum_fusion), channel_id=1, source_target_pairs={{0,64},{64,0},{32,96},{96,32},{128,192},{192,128},{160,224},{224,1... | collective-permute-start | bytes 393224 | tf_op jit(solution)/shard_map/ppermute | solution.py:23
  13.0 1.1 %reshape.40 = f32[32,1,2112]{2,1,0:T(1,128)} reshape(f32[32,33,64]{2,1,0:T(8,128)S(1)} %broadcast_in_dim.11) | data formatting | bytes 540672
  14.0 7.3 %all-to-all-start = ((f32[32,1,2112]{2,1,0:T(1,128)}), f32[32,1,2112]{2,1,0:T(1,128)S(1)}, u32[]{:S(2)}, u32[]{:S(2)}) async-start(f32[32,1,2112]{2,1,0:T(1,128)} %reshape.40), calls=%async_computation | async-start | bytes 557056 | tf_op jit(solution)/shard_map/all_to_all | solution.py:217
  21.6 0.9 %collective-permute-start.2 = (f32[2,8,2048]{2,1,0:T(8,128)S(1)}, f32[2,8,2048]{2,1,0:T(8,128)S(1)}, u32[]{:S(2)}, u32[]{:S(2)}) collective-permute-start(f32[2,8,2048]{2,1,0:T(8,128)S(1)} %pad_maximum_fusion.1), channel_id=1, source_target_pairs={{0,32},{32,0},{64,96},{96,64},{128,160},{160,128},{192,224},{224,1... | collective-permute-start | bytes 393224 | tf_op jit(solution)/shard_map/ppermute | solution.py:23
  22.6 0.6 copy.19
  23.2 3.7 %all-to-all-done = f32[32,1,2112]{2,1,0:T(1,128)S(1)} async-done(((f32[32,1,2112]{2,1,0:T(1,128)}), f32[32,1,2112]{2,1,0:T(1,128)S(1)}, u32[]{:S(2)}, u32[]{:S(2)}) %all-to-all-start) | async-done | bytes 270368 | tf_op jit(solution)/shard_map/all_to_all | solution.py:217
  26.9 0.5 broadcast.43
  27.4 1.3 %reduce = f32[32,2112]{1,0:T(8,128)S(1)} reduce(f32[32,1,2112]{2,1,0:T(1,128)S(1)} %all-to-all-done, f32[]{:T(128)} %broadcast.43), dimensions={1}, to_apply=%all_to_all.3.reduce_sub_computation | reduce | bytes 540676 | tf_op jit(solution)/shard_map/all_to_all | solution.py:217
  28.9 0.7 copy_bitcast_fusion
  29.6 2.5 %shard_map.118 = f32[2,8,16,128]{3,2,1,0:T(8,128)} custom-call(f32[8,16,128]{2,1,0:T(8,128)} %get-tuple-element.25.xr_ref, f32[8,16,128]{2,1,0:T(8,128)} %get-tuple-element.24.xi_ref, f32[8,16,128]{2,1,0:T(8,128)} %constant.144.clone.twr_ref, f32[8,16,128]{2,1,0:T(8,128)} %constant.145.clone.twi_ref, f32[128,128]{1,0:T(8,128)} %constant.146.clone.kr_ref, ...), custom_call_target="tpu_custom_call" | custom-call | tf_op jit(solution)/shard_map/pallas_call | solution.py:150
  32.1 0.5 collective-permute-start.3
  32.5 1.3 %collective-permute-start.4 = (f32[2,8,16,128]{3,2,1,0:T(8,128)}, f32[2,8,16,128]{3,2,1,0:T(8,128)S(1)}, u32[]{:S(2)}, u32[]{:S(2)}) collective-permute-start(f32[2,8,16,128]{3,2,1,0:T(8,128)} %shard_map.118), channel_id=1, source_target_pairs={{1,0},{2,1},{3,2},{4,3},{5,4},{6,5},{7,6},{8,7},{9,8},{10,9},{11,1... | collective-permute-start | bytes 393224 | tf_op jit(solution)/shard_map/ppermute | solution.py:172
  33.8 0.7 collective-permute-start.5
  34.5 1.2 %collective-permute-start.6 = (f32[2,8,16,128]{3,2,1,0:T(8,128)}, f32[2,8,16,128]{3,2,1,0:T(8,128)S(1)}, u32[]{:S(2)}, u32[]{:S(2)}) collective-permute-start(f32[2,8,16,128]{3,2,1,0:T(8,128)} %shard_map.118), channel_id=1, source_target_pairs={{3,0},{4,1},{5,2},{6,3},{7,4},{8,5},{9,6},{10,7},{11,8},{12,9},{13... | collective-permute-start | bytes 393224 | tf_op jit(solution)/shard_map/ppermute | solution.py:172
  35.7 0.4 copy.15
  36.1 0.5 copy.16
  36.6 0.7 slice.53
  37.4 0.6 fusion.9.shift_ref
  38.0 0.9 %copy-done.1 = f32[2,8,16,128]{3,2,1,0:T(8,128)S(1)} copy-done((f32[2,8,16,128]{3,2,1,0:T(8,128)S(1)}, f32[2,8,16,128]{3,2,1,0:T(8,128)}, u32[]{:S(2)}) %copy-start.1) | copy-done | bytes 131096
  38.9 10.1 %collective-permute-done.5 = f32[2,8,16,128]{3,2,1,0:T(8,128)S(1)} collective-permute-done((f32[2,8,16,128]{3,2,1,0:T(8,128)}, f32[2,8,16,128]{3,2,1,0:T(8,128)S(1)}, u32[]{:S(2)}, u32[]{:S(2)}) %collective-permute-start.5) | collective-permute-done | bytes 131104 | tf_op jit(solution)/shard_map/ppermute | solution.py:172
  49.0 0.8 %copy-done = f32[2,40,16,128]{3,2,1,0:T(8,128)} copy-done((f32[2,40,16,128]{3,2,1,0:T(8,128)}, f32[2,40,16,128]{3,2,1,0:T(8,128)S(1)}, u32[]{:S(2)}) %copy-start) | copy-done | bytes 655384
  49.9 3.5 %shard_map.119 = (f32[8,16,128]{2,1,0:T(8,128)}, f32[8,16,128]{2,1,0:T(8,128)}) custom-call(f32[2,40,16,128]{3,2,1,0:T(8,128)} %copy-done, s32[16,128]{1,0:T(8,128)} %fusion.9.shift_ref, f32[2,16,16,128]{3,2,1,0:T(8,128)} %bitcast.133, f32[8192]{0:T(1024)} %bitcast.138, f32[8,16,128]{2,1,0:T(8,128)} %constant.144.clone.twr_ref, ...), custom_call_target="tpu_custom_call" | custom-call | tf_op jit(solution)/shard_map/pallas_call | solution.py:162
  53.3 0.9 %stack_reshape.6 = f32[1,8,2048]{2,1,0:T(8,128)S(1)} reshape(f32[8,16,128]{2,1,0:T(8,128)} %get-tuple-element.9) | data formatting | bytes 131072 | tf_op jit(solution)/shard_map/stack;reshape | solution.py:240
  54.3 0.9 %collective-permute-start.7 = (f32[2,8,2048]{2,1,0:T(8,128)S(1)}, f32[2,8,2048]{2,1,0:T(8,128)S(1)}, u32[]{:S(2)}, u32[]{:S(2)}) collective-permute-start(f32[2,8,2048]{2,1,0:T(8,128)S(1)} %pad_maximum_fusion.2), channel_id=1, source_target_pairs={{0,32},{32,0},{64,96},{96,64},{128,160},{160,128},{192,224},{224,1... | collective-permute-start | bytes 393224 | tf_op jit(solution)/shard_map/ppermute | solution.py:23
  55.2 4.1 %collective-permute-done.7 = f32[2,8,2048]{2,1,0:T(8,128)S(1)} collective-permute-done((f32[2,8,2048]{2,1,0:T(8,128)S(1)}, f32[2,8,2048]{2,1,0:T(8,128)S(1)}, u32[]{:S(2)}, u32[]{:S(2)}) %collective-permute-start.7) | collective-permute-done | bytes 131104 | tf_op jit(solution)/shard_map/ppermute | solution.py:23
  59.4 0.7 collective-permute-start.8
  60.3 6.5 %collective-permute-done.8 = f32[2,8,2048]{2,1,0:T(8,128)S(1)} collective-permute-done((f32[2,8,2048]{2,1,0:T(8,128)S(1)}, f32[2,8,2048]{2,1,0:T(8,128)S(1)}, u32[]{:S(2)}, u32[]{:S(2)}) %collective-permute-start.8) | collective-permute-done | bytes 131104 | tf_op jit(solution)/shard_map/ppermute | solution.py:23
  66.8 5.9 %collective-permute-start.9 = (f32[8,2048]{1,0:T(8,128)S(1)}, f32[8,2048]{1,0:T(8,128)S(1)}, u32[]{:S(2)}, u32[]{:S(2)}) collective-permute-start(f32[8,2048]{1,0:T(8,128)S(1)} %get-tuple-element.11), channel_id=1, source_target_pairs={{0,128},{128,0},{32,160},{160,32},{64,192},{192,64},{96,224},{224,... | collective-permute-start | bytes 196616 | tf_op jit(solution)/shard_map/ppermute | solution.py:23
  72.7 2.4 %collective-permute-done.9 = f32[8,2048]{1,0:T(8,128)S(1)} collective-permute-done((f32[8,2048]{1,0:T(8,128)S(1)}, f32[8,2048]{1,0:T(8,128)S(1)}, u32[]{:S(2)}, u32[]{:S(2)}) %collective-permute-start.9) | collective-permute-done | bytes 65568 | tf_op jit(solution)/shard_map/ppermute | solution.py:23
  75.1 0.6 select_multiply_fusion
  (39 shorter events, 0.7 us)
Async XLA Ops:
  0.0 9.9 %copy-start.4 = (f32[8,2048]{1,0:T(8,128)S(1)}, f32[8,2048]{1,0:T(8,128)}, u32[]{:S(2)}) copy-start(f32[8,2048]{1,0:T(8,128)} %param.12) | copy-start | bytes 196612
  0.0 9.9 %collective-permute-start = (f32[8,2048]{1,0:T(8,128)}, f32[8,2048]{1,0:T(8,128)S(1)}, u32[]{:S(2)}, u32[]{:S(2)}) collective-permute-start(f32[8,2048]{1,0:T(8,128)} %param.12), channel_id=1, source_target_pairs={{0,128},{128,0},{32,160},{160,32},{64,192},{192,64},{96,224},{224,... | collective-permute-start | bytes 196616 | tf_op jit(solution)/shard_map/ppermute | solution.py:23
  9.9 3.0 %copy-start.7 = (s32[1,64]{1,0:T(1,128)S(1)}, s32[1,64]{1,0:T(1,128)}, u32[]{:S(2)}) copy-start(s32[1,64]{1,0:T(1,128)} %param.15) | copy-start | bytes 772
  9.9 3.0 %copy-start.6 = (f32[2,1,16,64]{3,2,1,0:T(8,128)S(1)}, f32[2,1,16,64]{3,2,1,0:T(8,128)}, u32[]{:S(2)}) copy-start(f32[2,1,16,64]{3,2,1,0:T(8,128)} %param.14) | copy-start | bytes 24580
  9.9 11.6 %collective-permute-start.1 = (f32[2,8,2048]{2,1,0:T(8,128)S(1)}, f32[2,8,2048]{2,1,0:T(8,128)S(1)}, u32[]{:S(2)}, u32[]{:S(2)}) collective-permute-start(f32[2,8,2048]{2,1,0:T(8,128)S(1)} %pad_maximum_fusion), channel_id=1, source_target_pairs={{0,64},{64,0},{32,96},{96,32},{128,192},{192,128},{160,224},{224,1... | collective-permute-start | bytes 393224 | tf_op jit(solution)/shard_map/ppermute | solution.py:23
  14.0 12.9 %all-to-all-start = ((f32[32,1,2112]{2,1,0:T(1,128)}), f32[32,1,2112]{2,1,0:T(1,128)S(1)}, u32[]{:S(2)}, u32[]{:S(2)}) async-start(f32[32,1,2112]{2,1,0:T(1,128)} %reshape.40), calls=%async_computation | async-start | bytes 557056 | tf_op jit(solution)/shard_map/all_to_all | solution.py:217
  21.6 1.0 %copy-start.5 = (f32[2,16,256]{2,1,0:T(8,128)S(1)}, f32[2,16,256]{2,1,0:T(8,128)}, u32[]{:S(2)}) copy-start(f32[2,16,256]{2,1,0:T(8,128)} %param.13) | copy-start | bytes 98308
  21.6 7.3 %collective-permute-start.2 = (f32[2,8,2048]{2,1,0:T(8,128)S(1)}, f32[2,8,2048]{2,1,0:T(8,128)S(1)}, u32[]{:S(2)}, u32[]{:S(2)}) collective-permute-start(f32[2,8,2048]{2,1,0:T(8,128)S(1)} %pad_maximum_fusion.1), channel_id=1, source_target_pairs={{0,32},{32,0},{64,96},{96,64},{128,160},{160,128},{192,224},{224,1... | collective-permute-start | bytes 393224 | tf_op jit(solution)/shard_map/ppermute | solution.py:23
  32.1 5.9 %collective-permute-start.3 = (f32[2,8,16,128]{3,2,1,0:T(8,128)}, f32[2,8,16,128]{3,2,1,0:T(8,128)S(1)}, u32[]{:S(2)}, u32[]{:S(2)}) collective-permute-start(f32[2,8,16,128]{3,2,1,0:T(8,128)} %shard_map.118), channel_id=1, source_target_pairs={{31,0},{0,1},{1,2},{2,3},{3,4},{4,5},{5,6},{6,7},{7,8},{8,9},{9,10... | collective-permute-start | bytes 393224 | tf_op jit(solution)/shard_map/ppermute | solution.py:172
  32.5 6.3 %collective-permute-start.4 = (f32[2,8,16,128]{3,2,1,0:T(8,128)}, f32[2,8,16,128]{3,2,1,0:T(8,128)S(1)}, u32[]{:S(2)}, u32[]{:S(2)}) collective-permute-start(f32[2,8,16,128]{3,2,1,0:T(8,128)} %shard_map.118), channel_id=1, source_target_pairs={{1,0},{2,1},{3,2},{4,3},{5,4},{6,5},{7,6},{8,7},{9,8},{10,9},{11,1... | collective-permute-start | bytes 393224 | tf_op jit(solution)/shard_map/ppermute | solution.py:172
  33.8 15.1 %collective-permute-start.5 = (f32[2,8,16,128]{3,2,1,0:T(8,128)}, f32[2,8,16,128]{3,2,1,0:T(8,128)S(1)}, u32[]{:S(2)}, u32[]{:S(2)}) collective-permute-start(f32[2,8,16,128]{3,2,1,0:T(8,128)} %shard_map.118), channel_id=1, source_target_pairs={{2,0},{3,1},{4,2},{5,3},{6,4},{7,5},{8,6},{9,7},{10,8},{11,9},{12,... | collective-permute-start | bytes 393224 | tf_op jit(solution)/shard_map/ppermute | solution.py:172
  34.5 14.5 %collective-permute-start.6 = (f32[2,8,16,128]{3,2,1,0:T(8,128)}, f32[2,8,16,128]{3,2,1,0:T(8,128)S(1)}, u32[]{:S(2)}, u32[]{:S(2)}) collective-permute-start(f32[2,8,16,128]{3,2,1,0:T(8,128)} %shard_map.118), channel_id=1, source_target_pairs={{3,0},{4,1},{5,2},{6,3},{7,4},{8,5},{9,6},{10,7},{11,8},{12,9},{13... | collective-permute-start | bytes 393224 | tf_op jit(solution)/shard_map/ppermute | solution.py:172
  38.0 0.9 %copy-start.1 = (f32[2,8,16,128]{3,2,1,0:T(8,128)S(1)}, f32[2,8,16,128]{3,2,1,0:T(8,128)}, u32[]{:S(2)}) copy-start(f32[2,8,16,128]{3,2,1,0:T(8,128)} %shard_map.118) | copy-start | bytes 393220
  49.0 0.9 %copy-start = (f32[2,40,16,128]{3,2,1,0:T(8,128)}, f32[2,40,16,128]{3,2,1,0:T(8,128)S(1)}, u32[]{:S(2)}) copy-start(f32[2,40,16,128]{3,2,1,0:T(8,128)S(1)} %constant_dynamic-update-slice_fusion.win_ref) | copy-start | bytes 1966084
  53.3 0.9 %copy-start.3 = (f32[8,16,128]{2,1,0:T(8,128)S(1)}, f32[8,16,128]{2,1,0:T(8,128)}, u32[]{:S(2)}) copy-start(f32[8,16,128]{2,1,0:T(8,128)} %get-tuple-element.10) | copy-start | bytes 196612
  54.3 5.1 %collective-permute-start.7 = (f32[2,8,2048]{2,1,0:T(8,128)S(1)}, f32[2,8,2048]{2,1,0:T(8,128)S(1)}, u32[]{:S(2)}, u32[]{:S(2)}) collective-permute-start(f32[2,8,2048]{2,1,0:T(8,128)S(1)} %pad_maximum_fusion.2), channel_id=1, source_target_pairs={{0,32},{32,0},{64,96},{96,64},{128,160},{160,128},{192,224},{224,1... | collective-permute-start | bytes 393224 | tf_op jit(solution)/shard_map/ppermute | solution.py:23
  59.4 0.8 %copy-start.2 = (f32[8,16,128]{2,1,0:T(8,128)S(1)}, f32[8,16,128]{2,1,0:T(8,128)}, u32[]{:S(2)}) copy-start(f32[8,16,128]{2,1,0:T(8,128)} %get-tuple-element.9) | copy-start | bytes 196612
  59.4 7.4 %collective-permute-start.8 = (f32[2,8,2048]{2,1,0:T(8,128)S(1)}, f32[2,8,2048]{2,1,0:T(8,128)S(1)}, u32[]{:S(2)}, u32[]{:S(2)}) collective-permute-start(f32[2,8,2048]{2,1,0:T(8,128)S(1)} %pad_maximum_fusion.3), channel_id=1, source_target_pairs={{0,64},{64,0},{32,96},{96,32},{128,192},{192,128},{160,224},{224,1... | collective-permute-start | bytes 393224 | tf_op jit(solution)/shard_map/ppermute | solution.py:23
  66.8 8.3 %collective-permute-start.9 = (f32[8,2048]{1,0:T(8,128)S(1)}, f32[8,2048]{1,0:T(8,128)S(1)}, u32[]{:S(2)}, u32[]{:S(2)}) collective-permute-start(f32[8,2048]{1,0:T(8,128)S(1)} %get-tuple-element.11), channel_id=1, source_target_pairs={{0,128},{128,0},{32,160},{160,32},{64,192},{192,64},{96,224},{224,... | collective-permute-start | bytes 196616 | tf_op jit(solution)/shard_map/ppermute | solution.py:23
